TPU v7x, 512 devices: a whole 4x8x8 slice. The times are simulated.
512 devices in a mesh: row: 32 (over x, z), col: 16 (over y, core).
Axes of the slice: x: 4, y: 8, z: 8, core: 2. Of those that a mesh axis runs over, the one named last changes fastest.
Arguments:
- charges: float32 [524288], P(('row', 'col')), may hold values from -0.5 to 1.5
- structure_id: int32 [524288], P(('row', 'col')), may hold values from 0 to 4095, as said below
- live_count: int32 [512], P(('row', 'col')), may hold values from 512 to 1024, as said below
- cell_index: int32 [3, 524288], P(None, ('row', 'col')), may hold values from 0 to 255, as said below
- fraction: float32 [3, 524288], P(None, ('row', 'col')), may hold values from 0 to 1
- influence: float32 [256, 256, 256], P('col', 'row'), may hold values from 0.1 to 10
Outputs:
- forces: float32 [3, 524288], P(None, ('row', 'col'))
- atom_energy: float32 [524288], P(('row', 'col'))
Inputs may be any that keep to these rules, and one draw needn't show every extreme that they name: `structure_id`: devices are numbered row-major over (row, col). Slots 0 to 7 of device d are live and belong to fragments d * 8 to d * 8 + 7, so every fragment has a live atom; every other slot names a fragment of its own device, of one of the four devices beside it along row or col (wrapping around), or of the device whose number is d plus half the number of devices (wrapping around). Device d's live atoms are its first live_count[d] slots; the count reaches 1024 on some device in every draw. `cell_index`: the atom slots of the device at (row r, col c) lie in its mesh block: first index from r * 8 to r * 8 + 7, second from c * 16 to c * 16 + 15; the third is anywhere.
All inputs are finite; a program needn't handle non-finite values.
Results may differ from a plain program's by a relative error of at most 0.000065.
Values sent between devices are 32-bit elements; how exact they have to be, the bound alone decides.
No kernel may reach another device: no remote copies, remote signals or barrier semaphores. Data moves between devices by JAX's collectives and lax.ppermute only.
A program may use at most 64 MiB of HBM per device.

v0:
```python
import functools

import jax
import jax.numpy as jnp
import numpy as np
from jax import lax
from jax.experimental import pallas as pl
from jax.experimental.pallas import tpu as pltpu
from jax.sharding import Mesh
from jax.sharding import PartitionSpec as P

N_ROW = 32
N_COL = 16
DEV = N_ROW * N_COL
CX = 8
CY = 16
N = 256
ATOMS = 1024
FRAG = 8
NK = 9
XI = CX + 3
PACK = 14
LANES = 128
ROW = ("row_0", "row_1")
COL = ("col_0", "col_1")
ALL = ROW + COL
MAIN = XI * CY
PLANE = MAIN + XI * 8
f32 = jnp.float32
bf16 = jnp.bfloat16


def kz_of(c, slot):
    if slot == 8 and c >= 8:
        return None
    return 16 * c + slot


def halves(table):
    high = table.astype(np.float32).astype(bf16)
    low = (table - high.astype(np.float64)).astype(np.float32).astype(bf16)
    return high, low


def z_lane(c, part):
    if c < PACK:
        return part * LANES + NK * c
    return 2 * LANES + NK * (2 * part + c - PACK)


@functools.cache
def z_table():
    table = np.zeros((N, 3 * LANES))
    z = np.arange(N)
    for c in range(N_COL):
        for slot in range(NK):
            kz = kz_of(c, slot)
            if kz is None:
                continue
            angle = 2.0 * np.pi * (kz * z % N) / N
            table[:, z_lane(c, 0) + slot] = np.cos(angle)
            table[:, z_lane(c, 1) + slot] = -np.sin(angle)
    return np.stack(halves(table))


@functools.cache
def y_table():
    table = np.zeros((2, N, N_COL, 40))
    ky = np.arange(N)
    for c in range(N_COL):
        for row in range(40):
            if row < 16:
                part, j = 0, row
            elif row < 24:
                part, j = (row - 16) // 4, 16 + row % 4
                if j == 19:
                    continue
            else:
                part, j = 1, row - 24
            angle = 2.0 * np.pi * (ky * (CY * c + j) % N) / N
            if part == 0:
                table[0, :, c, row] = np.cos(angle)
                table[1, :, c, row] = -np.sin(angle)
            else:
                table[0, :, c, row] = np.sin(angle)
                table[1, :, c, row] = np.cos(angle)
    return table.reshape(2 * N, N_COL * 40)


@functools.cache
def y_forward():
    return np.concatenate(halves(y_table()), axis=0)


@functools.cache
def y_back():
    return np.concatenate(halves(y_table().T.copy()), axis=0)


@functools.cache
def x_tables():
    twiddle = np.zeros((N_ROW, 2, LANES))
    k1 = np.arange(N_ROW)
    mix = np.zeros((2, LANES, 2, LANES))
    for i in range(XI):
        angle = 2.0 * np.pi * (i * k1 % N) / N
        for slot in range(NK):
            twiddle[:, 0, i * NK + slot] = np.cos(angle)
            twiddle[:, 1, i * NK + slot] = -np.sin(angle)
            for k2 in range(8):
                a = 2.0 * np.pi * (i * k2 % 8) / 8
                src, dst = i * NK + slot, slot * 8 + k2
                mix[0, src, 0, dst] = np.cos(a)
                mix[0, src, 1, dst] = -np.sin(a)
                mix[1, src, 0, dst] = np.sin(a)
                mix[1, src, 1, dst] = np.cos(a)
    return twiddle.astype(np.float32), np.stack(halves(mix.reshape(2 * LANES, 2 * LANES)))


def split(x):
    high = x.astype(bf16)
    low = (x - high.astype(f32)).astype(bf16)
    return high, low


def dot(a, b, dims=(((1,), (0,)), ((), ()))):
    return lax.dot_general(a, b, dims, preferred_element_type=f32)


NT = (((1,), (1,)), ((), ()))


def spline_values(fraction):
    remain = 1.0 - fraction
    square = fraction * fraction
    cubic = square * fraction
    return (
        remain * remain * remain * (1.0 / 6.0),
        (3.0 * cubic - 6.0 * square + 4.0) * (1.0 / 6.0),
        (-3.0 * cubic + 3.0 * square + 3.0 * fraction + 1.0) * (1.0 / 6.0),
        cubic * (1.0 / 6.0),
    )


def spline_slopes(fraction):
    remain = 1.0 - fraction
    square = fraction * fraction
    return (
        -0.5 * remain * remain,
        0.5 * (3.0 * square - 4.0 * fraction),
        0.5 * (-3.0 * square + 2.0 * fraction + 1.0),
        0.5 * square,
    )


def place(cell, weights, number):
    out = jnp.zeros(number.shape, f32)
    for offset in range(4):
        out = jnp.where(number == cell + offset, weights[offset], out)
    return out


def place_periodic(cell, weights):
    number = lax.broadcasted_iota(jnp.int32, (N, ATOMS), 0)
    out = jnp.zeros((N, ATOMS), f32)
    for offset in range(4):
        out = jnp.where(number == (cell + offset) % N, weights[offset], out)
    return out


def y_halo_rows(cell, weights):
    row = lax.broadcasted_iota(jnp.int32, (8, ATOMS), 0)
    return place(cell, weights, CY + row % 4)


def owners(device):
    row = device // N_COL
    col = device % N_COL
    return (
        device,
        (row + 1) % N_ROW * N_COL + col,
        (row + N_ROW - 1) % N_ROW * N_COL + col,
        row * N_COL + (col + 1) % N_COL,
        row * N_COL + (col + N_COL - 1) % N_COL,
        (device + DEV // 2) % DEV,
    )


def member_masks(device, live, sid):
    row = lax.broadcasted_iota(jnp.int32, (8, ATOMS), 0)
    lane = lax.broadcasted_iota(jnp.int32, (8, ATOMS), 1)
    alive = lane < live
    return [(sid == row + owner * FRAG) & alive for owner in owners(device)]


def partial_sums(device, live, sid, charges):
    out = []
    for mask in member_masks(device, live, sid):
        total = jnp.sum(jnp.where(mask, charges, 0.0), axis=1, keepdims=True)
        count = jnp.sum(jnp.where(mask, 1.0, 0.0), axis=1, keepdims=True)
        total = jnp.broadcast_to(total, (8, LANES))
        count = jnp.broadcast_to(count, (8, LANES))
        out.append(jnp.concatenate([total, count], axis=0))
    return out


def neutral_charges(device, live, sid, charges, means):
    acc = jnp.zeros((8, ATOMS), f32)
    for mask, mean in zip(member_masks(device, live, sid), means):
        acc = acc + jnp.where(mask, mean[:, 0:1], 0.0)
    mean = jnp.sum(acc, axis=0, keepdims=True)
    lane = lax.broadcasted_iota(jnp.int32, (1, ATOMS), 1)
    return jnp.where(lane < live, charges - mean, 0.0)


def lane_iota(rows):
    return lax.broadcasted_iota(jnp.int32, (rows, LANES), 1)


def group_tile(c, part):
    lane = z_lane(c, part)
    return lane // LANES, lane % LANES


def to_messages(wave, roll):
    lanes = lane_iota(16)
    sub = lax.broadcasted_iota(jnp.int32, (8, LANES), 0)
    out = []
    for c in range(N_COL):
        main = [jnp.zeros((16, LANES), f32), jnp.zeros((16, LANES), f32)]
        halo = [jnp.zeros((8, LANES), f32), jnp.zeros((8, LANES), f32)]
        for part in range(2):
            tile, lane = group_tile(c, part)
            cols = slice(tile * LANES, (tile + 1) * LANES)
            for x in range(XI):
                shift = (NK * x - lane) % LANES
                here = (lanes >= NK * x) & (lanes < NK * x + NK)
                piece = wave[x * CY : (x + 1) * CY, cols]
                edge = wave[MAIN + x * 8 : MAIN + (x + 1) * 8, cols]
                if shift:
                    piece = roll(piece, shift, 1)
                    edge = roll(edge, shift, 1)
                main[part] = jnp.where(here, piece, main[part])
                halo[part] = jnp.where(here[:8], edge, halo[part])
        both = jnp.where(sub < 4, halo[0], halo[1])
        out.append(jnp.concatenate([main[0], both, main[1]], axis=0))
    return out


def from_messages(message, roll):
    lanes = lane_iota(16)
    sub = lax.broadcasted_iota(jnp.int32, (8, LANES), 0)
    main = []
    halo = []
    for x in range(XI):
        wide = [jnp.zeros((16, LANES), f32) for _ in range(3)]
        edges = [jnp.zeros((8, LANES), f32) for _ in range(3)]
        for c in range(N_COL):
            block = message(c)
            for part in range(2):
                tile, lane = group_tile(c, part)
                shift = (lane - NK * x) % LANES
                here = (lanes >= lane) & (lanes < lane + NK)
                piece = block[0:16] if part == 0 else block[24:40]
                edge = block[16:24]
                if shift:
                    piece = roll(piece, shift, 1)
                    edge = roll(edge, shift, 1)
                wide[tile] = jnp.where(here, piece, wide[tile])
                own = sub < 4 if part == 0 else sub >= 4
                edges[tile] = jnp.where(here[:8] & own, edge, edges[tile])
        main.append(jnp.concatenate(wide, axis=1))
        halo.append(jnp.concatenate(edges, axis=1))
    return jnp.concatenate(main + halo, axis=0)


def spread_to_z(neutral, cell_x, cell_y, cell_z, fraction, table, roll):
    weights = spline_values(fraction)
    wx = [w[0:1] for w in weights]
    wy = [w[1:2] for w in weights]
    wz = [w[2:3] * neutral for w in weights]
    z_rows = place_periodic(cell_z, wz)
    x_rows = place(cell_x, wx, lax.broadcasted_iota(jnp.int32, (16, ATOMS), 0))
    y_rows = place(cell_y, wy, lax.broadcasted_iota(jnp.int32, (16, ATOMS), 0))
    y_edge = y_halo_rows(cell_y, wy)
    plane = jnp.concatenate(
        [y_rows * x_rows[x : x + 1] for x in range(XI)]
        + [y_edge * x_rows[x : x + 1] for x in range(XI)],
        axis=0,
    )
    plane_high, plane_low = split(plane)
    z_high, z_low = split(z_rows)
    grid = dot(plane_high, z_high, NT) + (dot(plane_low, z_high, NT) + dot(plane_high, z_low, NT))
    grid_high, grid_low = split(grid)
    wave = dot(grid_high, table[0]) + (dot(grid_low, table[0]) + dot(grid_high, table[1]))
    return to_messages(wave, roll)


def y_stage(x, table):
    high, low = split(x)
    half = table.shape[0] // 2
    both = dot(table, jnp.concatenate([high, low], axis=1))
    return both[:half, :LANES] + (both[:half, LANES:] + both[half:, :LANES])


def fft(values, sign):
    count = len(values)
    if count == 1:
        return values
    even = fft(values[0::2], sign)
    odd = fft(values[1::2], sign)
    out = [None] * count
    for k in range(count // 2):
        re, im = odd[k]
        if k == 0:
            pass
        elif 4 * k == count:
            re, im = (-sign * im, sign * re)
        else:
            angle = 2.0 * np.pi * k / count
            c, s = float(np.cos(angle)), float(sign * np.sin(angle))
            re, im = (re * c - im * s, re * s + im * c)
        er, ei = even[k]
        out[k] = (er + re, ei + im)
        out[k + count // 2] = (er - re, ei - im)
    return out


def x_forward(values, twiddle):
    out = []
    for k1, (re, im) in enumerate(fft(values, -1.0)):
        cos, sin = twiddle(k1)
        out.append(jnp.concatenate([re * cos - im * sin, re * sin + im * cos], axis=1))
    return jnp.concatenate(out, axis=0)


def x_mix(wave, gain, mix):
    high, low = split(wave)
    spectrum = dot(high, mix[0]) + (dot(low, mix[0]) + dot(high, mix[1]))
    spectrum = spectrum * gain
    high, low = split(spectrum)
    return dot(high, mix[0], NT) + (dot(low, mix[0], NT) + dot(high, mix[1], NT))


def x_back(wave, twiddle):
    values = []
    for k1 in range(N_ROW):
        re = wave[k1 * 8 : (k1 + 1) * 8, :LANES]
        im = wave[k1 * 8 : (k1 + 1) * 8, LANES:]
        cos, sin = twiddle(k1)
        values.append((re * cos + im * sin, im * cos - re * sin))
    return fft(values, 1.0)


def gain_table(device, own, mirror, edge, roll):
    col = device % N_COL
    r = lax.broadcasted_iota(jnp.int32, (72, 128), 0)
    k = lax.broadcasted_iota(jnp.int32, (72, 128), 1)
    take_own = (k == r).astype(bf16)
    r = lax.broadcasted_iota(jnp.int32, (72, 64), 0)
    k = lax.broadcasted_iota(jnp.int32, (72, 64), 1)
    slot, i = r // 8, r % 8
    take_mirror = ((slot > 0) & (i > 0) & (k == (8 - slot) * 8 + 8 - i)).astype(bf16)
    r = lax.broadcasted_iota(jnp.int32, (72, 8), 0)
    k = lax.broadcasted_iota(jnp.int32, (72, 8), 1)
    take_edge = ((r // 8 > 0) & (r % 8 == 0) & (k == 8 - r // 8)).astype(bf16)
    kx = lax.broadcasted_iota(jnp.int32, (N, N), 0)
    lane = lax.broadcasted_iota(jnp.int32, (N, N), 1)
    wave = lane // 8 + 32 * (lane % 8)
    order = (kx == wave).astype(bf16)
    reverse = (kx == (N - wave) % N).astype(bf16)

    def ordered(x, select, permutation):
        high, low = split(x)
        high = dot(select, high).astype(bf16)
        low = dot(select, low).astype(bf16)
        return dot(high, permutation) + dot(low, permutation)

    gain = ordered(own, take_own, order)
    gain = gain + ordered(mirror, take_mirror, reverse) + ordered(edge, take_edge, reverse)
    row = lax.broadcasted_iota(jnp.int32, (72, N), 0)
    gain = jnp.where((row >= 64) & (col >= 8), 0.0, gain) * (1.0 / (N * N * N))
    lanes = lane_iota(8)
    out = []
    for k1 in range(N_ROW):
        tile, lane = (k1 * 8) // LANES, (k1 * 8) % LANES
        acc = jnp.zeros((8, LANES), f32)
        for slot in range(NK):
            piece = gain[slot * 8 : (slot + 1) * 8, tile * LANES : (tile + 1) * LANES]
            shift = (slot * 8 - lane) % LANES
            if shift:
                piece = roll(piece, shift, 1)
            acc = jnp.where((lanes >= slot * 8) & (lanes < slot * 8 + 8), piece, acc)
        out.append(acc)
    return out


def interpolate(wave, neutral, cell_x, cell_y, cell_z, fraction, table):
    weights = spline_values(fraction)
    slopes = spline_slopes(fraction)
    number = lax.broadcasted_iota(jnp.int32, (16, ATOMS), 0)
    x_rows = place(cell_x, [w[0:1] for w in weights], number)
    x_slopes = place(cell_x, [w[0:1] for w in slopes], number)
    wy = [w[1:2] for w in weights]
    vy = [w[1:2] for w in slopes]
    y_rows, y_slopes = place(cell_y, wy, number), place(cell_y, vy, number)
    y_edge, y_edge_slopes = y_halo_rows(cell_y, wy), y_halo_rows(cell_y, vy)
    z_rows = place_periodic(cell_z, [w[2:3] for w in weights])
    z_slopes = place_periodic(cell_z, [w[2:3] for w in slopes])
    high, low = split(wave)
    grid = dot(high, table[0], NT) + (dot(low, table[0], NT) + dot(high, table[1], NT))
    grid_high, grid_low = split(grid)

    def sample(rows):
        high, low = split(rows)
        return dot(grid_high, high) + (dot(grid_low, high) + dot(grid_high, low))

    at = sample(z_rows)
    at_slope = sample(z_slopes)
    value = jnp.zeros((8, ATOMS), f32)
    grad_x, grad_y, grad_z = value, value, value

    def eight(x):
        return x[:8] + x[8:]

    for x in range(XI):
        main = at[x * CY : (x + 1) * CY]
        edge = at[MAIN + x * 8 : MAIN + (x + 1) * 8]
        main_slope = at_slope[x * CY : (x + 1) * CY]
        edge_slope = at_slope[MAIN + x * 8 : MAIN + (x + 1) * 8]
        plain = eight(main * y_rows) + edge * y_edge
        turned = eight(main * y_slopes) + edge * y_edge_slopes
        risen = eight(main_slope * y_rows) + edge_slope * y_edge
        value = value + plain * x_rows[x : x + 1]
        grad_x = grad_x + plain * x_slopes[x : x + 1]
        grad_y = grad_y + turned * x_rows[x : x + 1]
        grad_z = grad_z + risen * x_rows[x : x + 1]

    def total(x):
        return jnp.sum(x, axis=0, keepdims=True)

    energy = 0.5 * neutral * total(value)
    force = [-neutral * total(g) for g in (grad_x, grad_y, grad_z)]
    return energy, force


def partial_kernel(dev, live, sid, charges, *out):
    for ref, x in zip(out, partial_sums(dev[0], live[0], sid[...], charges[...])):
        ref[...] = x


def mean_kernel(own, a, b, c, d, e, mirror, mean, packed):
    total = own[...] + a[...] + b[...] + c[...] + d[...] + e[...]
    result = total[:8] / total[8:]
    mean[...] = result
    packed[0:8, :] = result
    for p in range(8):
        packed[8 + p : 9 + p, :] = mirror[p, 0:1, :LANES]
        packed[16 + p : 17 + p, :] = mirror[p, 0:1, LANES:]


def local_cells(dev, cells):
    return (
        cells[0:1] - dev // N_COL * CX,
        cells[1:2] - dev % N_COL * CY,
        cells[2:3],
    )


def spread_kernel(dev, live, sid, charges, cells, fraction, m0, m1, m2, m3, m4, m5, table, out, neutral_out):
    d = dev[0]
    means = [m0[...], m1[...], m2[0:8, :], m3[...], m4[...], m5[...]]
    neutral = neutral_charges(d, live[0], sid[...], charges[...], means)
    neutral_out[...] = neutral
    x, y, z = local_cells(d, cells[...])
    for c, message in enumerate(spread_to_z(neutral, x, y, z, fraction[...], table, pltpu.roll)):
        out[c] = message


def y_forward_kernel(x, table, out):
    y = y_stage(x[...].reshape(N_COL * 40, LANES), table[...])
    out[:, :, :LANES] = y[:N].reshape(N_ROW, 8, LANES)
    out[:, :, LANES:] = y[N:].reshape(N_ROW, 8, LANES)


def y_back_kernel(x, table, out):
    re = x[:, :, :LANES].reshape(N, LANES)
    im = x[:, :, LANES:].reshape(N, LANES)
    y = y_stage(jnp.concatenate([re, im], axis=0), table[...])
    out[...] = y.reshape(N_COL, 40, LANES)


def gain_kernel(dev, own, mirror, packed, out):
    edge = jnp.concatenate([packed[8:16, :], packed[16:24, :]], axis=1)
    flat = own[...].reshape(128, N)
    pieces = gain_table(dev[0], flat, mirror[...].reshape(64, N), edge, pltpu.roll)
    for k1, piece in enumerate(pieces):
        out[k1 * 8 : (k1 + 1) * 8, :LANES] = piece
        out[k1 * 8 : (k1 + 1) * 8, LANES:] = piece


def x_kernel(x, gain, twiddle, mix, out):
    def factor(k1):
        return twiddle[k1, 0:1, :], twiddle[k1, 1:2, :]

    values = [(x[r, :, :LANES], x[r, :, LANES:]) for r in range(N_ROW)]
    wave = x_mix(x_forward(values, factor), gain[...], mix)
    for r, (re, im) in enumerate(x_back(wave, factor)):
        out[r, :, :LANES] = re
        out[r, :, LANES:] = im


def atom_kernel(dev, message, neutral, cells, fraction, table, force, energy):
    wave = from_messages(lambda c: message[c], pltpu.roll)
    x, y, z = local_cells(dev[0], cells[...])
    e, g = interpolate(wave, neutral[...], x, y, z, fraction[...], table)
    energy[...] = e
    for d in range(3):
        force[d : d + 1, :] = g[d]


def call(kernel, shapes, scalars, *args):
    smem = pl.BlockSpec(memory_space=pltpu.SMEM)
    vmem = pl.BlockSpec(memory_space=pltpu.VMEM)
    many = len(shapes) > 1
    out_shape = [jax.ShapeDtypeStruct(s, f32) for s in shapes]
    return pl.pallas_call(
        kernel,
        out_shape=out_shape if many else out_shape[0],
        in_specs=[smem] * scalars + [vmem] * (len(args) - scalars),
        out_specs=[vmem] * len(shapes) if many else vmem,
        compiler_params=pltpu.CompilerParams(vmem_limit_bytes=48 << 20),
    )(*args)


def shifted(x, axis, distance):
    count = lax.axis_size(axis)
    return lax.ppermute(x, axis, [(i, (i + distance) % count) for i in range(count)])


def swap(x, axis):
    return lax.all_to_all(x, axis, split_axis=0, concat_axis=0, tiled=True)


def body(charges, structure_id, live_count, cells, fraction, influence):
    dev = lax.axis_index(ALL).astype(jnp.int32).reshape(1)
    charges = charges.reshape(1, ATOMS)
    sid = structure_id.reshape(1, ATOMS)
    mirror = lax.ppermute(influence[8:], ALL, [(i, DEV - 1 - i) for i in range(DEV)])
    parts = call(partial_kernel, [(16, LANES)] * 6, 2, dev, live_count, sid, charges)
    mean, packed = call(
        mean_kernel,
        [(8, LANES), (24, LANES)],
        0,
        parts[0],
        shifted(parts[1], ROW, 1),
        shifted(parts[2], ROW, -1),
        shifted(parts[3], COL, 1),
        shifted(parts[4], COL, -1),
        shifted(parts[5], ALL, DEV // 2),
        mirror,
    )
    packed = shifted(packed, ROW, 1)
    after_row = shifted(mean, ROW, -1)
    after_col = shifted(mean, COL, -1)
    before_col = shifted(mean, COL, 1)
    far = shifted(mean, ALL, DEV // 2)
    messages, neutral = call(
        spread_kernel,
        [(N_COL, 40, LANES), (1, ATOMS)],
        2,
        dev, live_count, sid, charges, cells, fraction,
        mean, after_row, packed, after_col, before_col, far,
        z_table(),
    )
    gain = call(gain_kernel, [(N, 2 * LANES)], 1, dev, influence, mirror, packed)
    twiddle, mix = x_tables()
    columns = swap(messages, COL)
    rows = call(y_forward_kernel, [(N_ROW, 8, 2 * LANES)], 0, columns, y_forward())
    rows = swap(rows, ROW)
    rows = call(x_kernel, [(N_ROW, 8, 2 * LANES)], 0, rows, gain, twiddle, mix)
    rows = swap(rows, ROW)
    columns = call(y_back_kernel, [(N_COL, 40, LANES)], 0, rows, y_back())
    columns = swap(columns, COL)
    forces, energy = call(
        atom_kernel,
        [(3, ATOMS), (1, ATOMS)],
        1,
        dev, columns, neutral, cells, fraction, z_table(),
    )
    return forces, energy.reshape(ATOMS)


def solution(mesh):
    torus = Mesh(mesh.devices.reshape(4, 8, 8, 2), ALL)
    placed = (P(ALL), P(ALL), P(ALL), P(None, ALL), P(None, ALL), P(COL, ROW, None))
    return jax.shard_map(
        body, mesh=torus, in_specs=placed, out_specs=(P(None, ALL), P(ALL)), check_vma=False
    )
```

profile of v0, /device:TPU:1, one launch (start us, length us, event | category | flops | bytes accessed | tf_op | source)
XLA Modules:
  0.0 136.5 jit_solution(10478181801752959066)
XLA Ops:
  0.6 0.8 slice.3
  1.5 17.1 %collective-permute-start.5 = (f32[8,8,256]{2,1,0:T(8,128)S(1)}, f32[8,8,256]{2,1,0:T(8,128)S(1)}, u32[]{:S(2)}, u32[]{:S(2)}) collective-permute-start(f32[8,8,256]{2,1,0:T(8,128)S(1)} %slice.3), channel_id=1, source_target_pairs={{0,511},{1,510},{2,509},{3,508},{4,507},{5,506},{6,505},{7,504},{8... | collective-permute-start | bytes 196616 | tf_op jit(solution)/shard_map/ppermute | solution.py:549
  19.3 0.0 copy-start.11
  19.3 0.7 copy-done.11
  20.0 0.0 copy-start.13
  20.0 0.7 copy-done.13
  20.7 0.1 shard_map.122
  20.8 3.1 %collective-permute-start = (f32[16,128]{1,0:T(8,128)S(1)}, f32[16,128]{1,0:T(8,128)S(1)}, u32[]{:S(2)}, u32[]{:S(2)}) collective-permute-start(f32[16,128]{1,0:T(8,128)S(1)} %get-tuple-element.15), channel_id=1, source_target_pairs={{0,16},{16,32},{32,48},{48,64},{64,80},{80,96},{96,112},{112,128},... | collective-permute-start | bytes 24584 | tf_op jit(solution)/shard_map/ppermute | solution.py:538
  23.9 5.6 %collective-permute-start.1 = (f32[16,128]{1,0:T(8,128)S(1)}, f32[16,128]{1,0:T(8,128)S(1)}, u32[]{:S(2)}, u32[]{:S(2)}) collective-permute-start(f32[16,128]{1,0:T(8,128)S(1)} %get-tuple-element.16), channel_id=1, source_target_pairs={{0,496},{16,0},{32,16},{48,32},{64,48},{80,64},{96,80},{112,96},{1... | collective-permute-start | bytes 24584 | tf_op jit(solution)/shard_map/ppermute | solution.py:538
  29.4 2.2 %collective-permute-start.2 = (f32[16,128]{1,0:T(8,128)S(1)}, f32[16,128]{1,0:T(8,128)S(1)}, u32[]{:S(2)}, u32[]{:S(2)}) collective-permute-start(f32[16,128]{1,0:T(8,128)S(1)} %get-tuple-element.17), channel_id=1, source_target_pairs={{0,1},{1,2},{2,3},{3,4},{4,5},{5,6},{6,7},{7,8},{8,9},{9,10},{10,1... | collective-permute-start | bytes 24584 | tf_op jit(solution)/shard_map/ppermute | solution.py:538
  31.7 0.0 collective-permute-start.3
  31.7 0.0 collective-permute-done.a
  31.7 1.9 %collective-permute-start.4 = (f32[16,128]{1,0:T(8,128)S(1)}, f32[16,128]{1,0:T(8,128)S(1)}, u32[]{:S(2)}, u32[]{:S(2)}) collective-permute-start(f32[16,128]{1,0:T(8,128)S(1)} %get-tuple-element.19), channel_id=1, source_target_pairs={{0,256},{1,257},{2,258},{3,259},{4,260},{5,261},{6,262},{7,263},{8... | collective-permute-start | bytes 24584 | tf_op jit(solution)/shard_map/ppermute | solution.py:538
  33.6 0.0 collective-permute-done.1.b
  33.6 0.0 collective-permute-done.2.c
  33.6 1.1 collective-permute-done.3.d
  34.7 2.8 %collective-permute-done.4.e = f32[16,128]{1,0:T(8,128)S(1)} collective-permute-done((f32[16,128]{1,0:T(8,128)S(1)}, f32[16,128]{1,0:T(8,128)S(1)}, u32[]{:S(2)}, u32[]{:S(2)}) %collective-permute-start.4) | collective-permute-done | bytes 8224 | tf_op jit(solution)/shard_map/ppermute | solution.py:538
  37.6 0.0 collective-permute-done.5.mirror
  37.6 1.9 %collective-permute-start.7 = (f32[24,128]{1,0:T(8,128)S(1)}, f32[24,128]{1,0:T(8,128)S(1)}, u32[]{:S(2)}, u32[]{:S(2)}) collective-permute-start(f32[24,128]{1,0:T(8,128)S(1)} %get-tuple-element.21), channel_id=1, source_target_pairs={{0,16},{16,32},{32,48},{48,64},{64,80},{80,96},{96,112},{112,128},... | collective-permute-start | bytes 36872 | tf_op jit(solution)/shard_map/ppermute | solution.py:538
  39.5 1.9 %collective-permute-start.10 = (f32[8,128]{1,0:T(8,128)S(1)}, f32[8,128]{1,0:T(8,128)S(1)}, u32[]{:S(2)}, u32[]{:S(2)}) collective-permute-start(f32[8,128]{1,0:T(8,128)S(1)} %get-tuple-element.20.m0), channel_id=1, source_target_pairs={{0,256},{1,257},{2,258},{3,259},{4,260},{5,261},{6,262},{7,263},{8... | collective-permute-start | bytes 12296 | tf_op jit(solution)/shard_map/ppermute | solution.py:538
  41.4 6.7 %collective-permute-start.6 = (f32[8,128]{1,0:T(8,128)S(1)}, f32[8,128]{1,0:T(8,128)S(1)}, u32[]{:S(2)}, u32[]{:S(2)}) collective-permute-start(f32[8,128]{1,0:T(8,128)S(1)} %get-tuple-element.20.m0), channel_id=1, source_target_pairs={{0,496},{16,0},{32,16},{48,32},{64,48},{80,64},{96,80},{112,96},{1... | collective-permute-start | bytes 12296 | tf_op jit(solution)/shard_map/ppermute | solution.py:538
  48.1 2.8 %collective-permute-start.8 = (f32[8,128]{1,0:T(8,128)S(1)}, f32[8,128]{1,0:T(8,128)S(1)}, u32[]{:S(2)}, u32[]{:S(2)}) collective-permute-start(f32[8,128]{1,0:T(8,128)S(1)} %get-tuple-element.20.m0), channel_id=1, source_target_pairs={{0,15},{1,0},{2,1},{3,2},{4,3},{5,4},{6,5},{7,6},{8,7},{9,8},{10,9... | collective-permute-start | bytes 12296 | tf_op jit(solution)/shard_map/ppermute | solution.py:538
  50.9 0.7 collective-permute-start.9
  51.6 0.0 collective-permute-done.10.m5
  51.6 0.0 collective-permute-done.6.m1
  51.6 1.3 collective-permute-done.8.m3
  52.9 0.0 collective-permute-done.9.m4
  52.9 0.0 collective-permute-done.7.m2.packed
  52.9 0.0 copy-start
  52.9 1.0 copy-done
  53.9 0.0 copy-start.6
  53.9 0.7 copy-done.6
  54.6 0.0 copy-start.8
  54.6 0.7 copy-done.8
  55.3 0.0 copy-start.12
  55.3 0.7 copy-done.12
  56.0 0.0 copy-start.14
  56.0 0.7 copy-done.14
  56.7 2.9 %shard_map.124 = (f32[16,40,128]{2,1,0:T(8,128)S(1)}, f32[1,1024]{1,0:T(1,128)S(1)}) custom-call(s32[1]{0:T(128)} %bitcast.dev, s32[1]{0:T(128)S(6)} %copy.13.live, s32[1,1024]{1,0:T(1,128)S(1)} %bitcast.5, f32[1,1024]{1,0:T(1,128)S(1)} %bitcast.7, s32[3,1024]{1,0:T(4,128)S(1)} %copy-done.6, f32[3,1024]{1,0:T(4,128)S(1)} %copy-done.8, ...), custom_call_target="tpu_custom_call" | custom-call | tf_op jit(solution)/shard_map/pallas_call | solution.py:527
  59.6 19.3 %all_to_all.20.x = f32[16,40,128]{2,1,0:T(8,128)S(1)} all-to-all(f32[16,40,128]{2,1,0:T(8,128)S(1)} %get-tuple-element.22), channel_id=1, replica_groups=mesh['row_0'=4,'row_1'=8,'col_0'=8,'col_1'=2] {'col_0','col_1'}, dimensions={0} | all-to-all | bytes 655360 | tf_op jit(solution)/shard_map/all_to_all | solution.py:542
  78.9 0.0 copy-start.3
  78.9 1.3 copy-done.3
  80.2 0.0 copy-start.4
  80.2 0.0 copy-start.5
  80.2 0.0 copy-start.10
  80.2 1.3 shard_map.125
  81.5 0.0 copy-start.2
  81.5 4.4 %all-to-all-start.1 = ((f32[32,8,256]{2,1,0:T(8,128)}), f32[32,8,256]{2,1,0:T(8,128)S(1)}, u32[]{:S(2)}, u32[]{:S(2)}) async-start(f32[32,8,256]{2,1,0:T(8,128)} %shard_map.125), calls=%async_computation.1 | async-start | bytes 524288 | tf_op jit(solution)/shard_map/all_to_all | solution.py:542
  85.9 0.0 copy-done.4
  85.9 0.9 shard_map.126.gain
  86.8 10.5 %all-to-all-done.1.x = f32[32,8,256]{2,1,0:T(8,128)S(1)} async-done(((f32[32,8,256]{2,1,0:T(8,128)}), f32[32,8,256]{2,1,0:T(8,128)S(1)}, u32[]{:S(2)}, u32[]{:S(2)}) %all-to-all-start.1) | async-done | bytes 262176 | tf_op jit(solution)/shard_map/all_to_all | solution.py:542
  97.4 0.0 copy-done.5
  97.4 0.0 copy-done.10
  97.4 0.7 shard_map.127
  98.1 14.9 %all_to_all.21.x = f32[32,8,256]{2,1,0:T(8,128)S(1)} all-to-all(f32[32,8,256]{2,1,0:T(8,128)S(1)} %shard_map.127), channel_id=1, replica_groups=mesh['row_0'=4,'row_1'=8,'col_0'=8,'col_1'=2] {'row_0','row_1'}, dimensions={0} | all-to-all | bytes 524288 | tf_op jit(solution)/shard_map/all_to_all | solution.py:542
  113.0 0.0 copy-done.2
  113.0 0.0 copy-start.7
  113.0 0.0 copy-start.9
  113.1 0.5 shard_map.128
  113.6 19.2 %all_to_all.22.message = f32[16,40,128]{2,1,0:T(8,128)S(1)} all-to-all(f32[16,40,128]{2,1,0:T(8,128)S(1)} %shard_map.128), channel_id=1, replica_groups=mesh['row_0'=4,'row_1'=8,'col_0'=8,'col_1'=2] {'col_0','col_1'}, dimensions={0} | all-to-all | bytes 655360 | tf_op jit(solution)/shard_map/all_to_all | solution.py:542
  132.7 0.0 copy-done.1
  132.7 0.0 copy-done.7
  132.7 0.0 copy-done.9
  132.8 3.8 %shard_map.129 = (f32[3,1024]{1,0:T(4,128)}, f32[1,1024]{1,0:T(1,128)}) custom-call(s32[1]{0:T(128)} %bitcast.dev, f32[16,40,128]{2,1,0:T(8,128)S(1)} %all_to_all.22.message, f32[1,1024]{1,0:T(1,128)S(1)} %get-tuple-element.23.neutral, s32[3,1024]{1,0:T(4,128)S(1)} %copy-done.7, f32[3,1024]{1,0:T(4,128)S(1)} %copy-done.9, bf16[2,256,384]{2,1,0:T(8,128)(2,1)S(1)} %copy-done.1), custom_call_target="tpu_custom_call" | custom-call | tf_op jit(solution)/shard_map/pallas_call | solution.py:527
  (2 shorter events, 0.0 us)
Async XLA Ops:
  1.5 36.1 %collective-permute-start.5 = (f32[8,8,256]{2,1,0:T(8,128)S(1)}, f32[8,8,256]{2,1,0:T(8,128)S(1)}, u32[]{:S(2)}, u32[]{:S(2)}) collective-permute-start(f32[8,8,256]{2,1,0:T(8,128)S(1)} %slice.3), channel_id=1, source_target_pairs={{0,511},{1,510},{2,509},{3,508},{4,507},{5,506},{6,505},{7,504},{8... | collective-permute-start | bytes 196616 | tf_op jit(solution)/shard_map/ppermute | solution.py:549
  19.3 0.7 copy-start.11
  20.0 0.7 copy-start.13
  20.8 10.9 %collective-permute-start = (f32[16,128]{1,0:T(8,128)S(1)}, f32[16,128]{1,0:T(8,128)S(1)}, u32[]{:S(2)}, u32[]{:S(2)}) collective-permute-start(f32[16,128]{1,0:T(8,128)S(1)} %get-tuple-element.15), channel_id=1, source_target_pairs={{0,16},{16,32},{32,48},{48,64},{64,80},{80,96},{96,112},{112,128},... | collective-permute-start | bytes 24584 | tf_op jit(solution)/shard_map/ppermute | solution.py:538
  23.9 9.7 %collective-permute-start.1 = (f32[16,128]{1,0:T(8,128)S(1)}, f32[16,128]{1,0:T(8,128)S(1)}, u32[]{:S(2)}, u32[]{:S(2)}) collective-permute-start(f32[16,128]{1,0:T(8,128)S(1)} %get-tuple-element.16), channel_id=1, source_target_pairs={{0,496},{16,0},{32,16},{48,32},{64,48},{80,64},{96,80},{112,96},{1... | collective-permute-start | bytes 24584 | tf_op jit(solution)/shard_map/ppermute | solution.py:538
  29.4 4.2 %collective-permute-start.2 = (f32[16,128]{1,0:T(8,128)S(1)}, f32[16,128]{1,0:T(8,128)S(1)}, u32[]{:S(2)}, u32[]{:S(2)}) collective-permute-start(f32[16,128]{1,0:T(8,128)S(1)} %get-tuple-element.17), channel_id=1, source_target_pairs={{0,1},{1,2},{2,3},{3,4},{4,5},{5,6},{6,7},{7,8},{8,9},{9,10},{10,1... | collective-permute-start | bytes 24584 | tf_op jit(solution)/shard_map/ppermute | solution.py:538
  31.7 3.1 %collective-permute-start.3 = (f32[16,128]{1,0:T(8,128)S(1)}, f32[16,128]{1,0:T(8,128)S(1)}, u32[]{:S(2)}, u32[]{:S(2)}) collective-permute-start(f32[16,128]{1,0:T(8,128)S(1)} %get-tuple-element.18), channel_id=1, source_target_pairs={{0,15},{1,0},{2,1},{3,2},{4,3},{5,4},{6,5},{7,6},{8,7},{9,8},{10,9... | collective-permute-start | bytes 24584 | tf_op jit(solution)/shard_map/ppermute | solution.py:538
  31.7 5.9 %collective-permute-start.4 = (f32[16,128]{1,0:T(8,128)S(1)}, f32[16,128]{1,0:T(8,128)S(1)}, u32[]{:S(2)}, u32[]{:S(2)}) collective-permute-start(f32[16,128]{1,0:T(8,128)S(1)} %get-tuple-element.19), channel_id=1, source_target_pairs={{0,256},{1,257},{2,258},{3,259},{4,260},{5,261},{6,262},{7,263},{8... | collective-permute-start | bytes 24584 | tf_op jit(solution)/shard_map/ppermute | solution.py:538
  37.6 15.3 %collective-permute-start.7 = (f32[24,128]{1,0:T(8,128)S(1)}, f32[24,128]{1,0:T(8,128)S(1)}, u32[]{:S(2)}, u32[]{:S(2)}) collective-permute-start(f32[24,128]{1,0:T(8,128)S(1)} %get-tuple-element.21), channel_id=1, source_target_pairs={{0,16},{16,32},{32,48},{48,64},{64,80},{80,96},{96,112},{112,128},... | collective-permute-start | bytes 36872 | tf_op jit(solution)/shard_map/ppermute | solution.py:538
  39.5 12.1 %collective-permute-start.10 = (f32[8,128]{1,0:T(8,128)S(1)}, f32[8,128]{1,0:T(8,128)S(1)}, u32[]{:S(2)}, u32[]{:S(2)}) collective-permute-start(f32[8,128]{1,0:T(8,128)S(1)} %get-tuple-element.20.m0), channel_id=1, source_target_pairs={{0,256},{1,257},{2,258},{3,259},{4,260},{5,261},{6,262},{7,263},{8... | collective-permute-start | bytes 12296 | tf_op jit(solution)/shard_map/ppermute | solution.py:538
  41.4 10.2 %collective-permute-start.6 = (f32[8,128]{1,0:T(8,128)S(1)}, f32[8,128]{1,0:T(8,128)S(1)}, u32[]{:S(2)}, u32[]{:S(2)}) collective-permute-start(f32[8,128]{1,0:T(8,128)S(1)} %get-tuple-element.20.m0), channel_id=1, source_target_pairs={{0,496},{16,0},{32,16},{48,32},{64,48},{80,64},{96,80},{112,96},{1... | collective-permute-start | bytes 12296 | tf_op jit(solution)/shard_map/ppermute | solution.py:538
  48.1 4.8 %collective-permute-start.8 = (f32[8,128]{1,0:T(8,128)S(1)}, f32[8,128]{1,0:T(8,128)S(1)}, u32[]{:S(2)}, u32[]{:S(2)}) collective-permute-start(f32[8,128]{1,0:T(8,128)S(1)} %get-tuple-element.20.m0), channel_id=1, source_target_pairs={{0,15},{1,0},{2,1},{3,2},{4,3},{5,4},{6,5},{7,6},{8,7},{9,8},{10,9... | collective-permute-start | bytes 12296 | tf_op jit(solution)/shard_map/ppermute | solution.py:538
  50.9 1.9 %collective-permute-start.9 = (f32[8,128]{1,0:T(8,128)S(1)}, f32[8,128]{1,0:T(8,128)S(1)}, u32[]{:S(2)}, u32[]{:S(2)}) collective-permute-start(f32[8,128]{1,0:T(8,128)S(1)} %get-tuple-element.20.m0), channel_id=1, source_target_pairs={{0,1},{1,2},{2,3},{3,4},{4,5},{5,6},{6,7},{7,8},{8,9},{9,10},{10,1... | collective-permute-start | bytes 12296 | tf_op jit(solution)/shard_map/ppermute | solution.py:538
  52.9 1.0 copy-start
  53.9 0.7 copy-start.6
  54.6 0.7 copy-start.8
  55.3 0.7 copy-start.12
  56.0 0.7 copy-start.14
  78.9 1.3 copy-start.3
  80.2 5.7 %copy-start.4 = (f32[16,8,256]{2,1,0:T(8,128)S(1)}, f32[16,8,256]{2,1,0:T(8,128)}, u32[]{:S(2)}) copy-start(f32[16,8,256]{2,1,0:T(8,128)} %own.1) | copy-start | bytes 393220
  80.2 17.2 %copy-start.5 = (bf16[2,256,256]{2,1,0:T(8,128)(2,1)S(1)}, bf16[2,256,256]{2,1,0:T(8,128)(2,1)}, u32[]{:S(2)}) copy-start(bf16[2,256,256]{2,1,0:T(8,128)(2,1)} %constant.36.clone.mix) | copy-start | bytes 786436
  80.2 17.2 %copy-start.10 = (f32[32,2,128]{2,1,0:T(2,128)S(1)}, f32[32,2,128]{2,1,0:T(2,128)}, u32[]{:S(2)}) copy-start(f32[32,2,128]{2,1,0:T(2,128)} %constant.35.clone.twiddle) | copy-start | bytes 98308
  81.5 31.5 %copy-start.2 = (bf16[1280,512]{1,0:T(8,128)(2,1)S(1)}, bf16[1280,512]{1,0:T(8,128)(2,1)}, u32[]{:S(2)}) copy-start(bf16[1280,512]{1,0:T(8,128)(2,1)} %constant.37.clone.table) | copy-start | bytes 3932164
  81.5 15.9 %all-to-all-start.1 = ((f32[32,8,256]{2,1,0:T(8,128)}), f32[32,8,256]{2,1,0:T(8,128)S(1)}, u32[]{:S(2)}, u32[]{:S(2)}) async-start(f32[32,8,256]{2,1,0:T(8,128)} %shard_map.125), calls=%async_computation.1 | async-start | bytes 524288 | tf_op jit(solution)/shard_map/all_to_all | solution.py:542
  113.0 19.7 %copy-start.1 = (bf16[2,256,384]{2,1,0:T(8,128)(2,1)S(1)}, bf16[2,256,384]{2,1,0:T(8,128)(2,1)}, u32[]{:S(2)}) copy-start(bf16[2,256,384]{2,1,0:T(8,128)(2,1)} %constant.33.clone.table) | copy-start | bytes 1179652
  113.0 19.7 %copy-start.7 = (s32[3,1024]{1,0:T(4,128)S(1)}, s32[3,1024]{1,0:T(4,128)}, u32[]{:S(2)}) copy-start(s32[3,1024]{1,0:T(4,128)} %cells.3) | copy-start | bytes 36868
  113.0 19.7 %copy-start.9 = (f32[3,1024]{1,0:T(4,128)S(1)}, f32[3,1024]{1,0:T(4,128)}, u32[]{:S(2)}) copy-start(f32[3,1024]{1,0:T(4,128)} %fraction.3) | copy-start | bytes 36868
where the time goes:
time: 137 us
  blocking collectives  53.4 us (39%)
  starting transfers between devices  48.4 us (35%)
  waiting for transfers between devices  15.8 us (12%)
  Pallas kernels  10.2 us (7%)
  local copies, waits for them, and re-layouts  7.36 us (5%)
  between operations  1.45 us (1%)
    all_to_all x3, blocking collectives, swap(): return lax.all_to_all(x, axis, split_axis=0, concat_axis=0, tiled=True)  53.4 us
    ppermute x10, starting transfers between devices, shifted(): lax.ppermute(x, axis, [(i, (i + distance) % count) for i in range(count)])  26.8 us
    ppermute x1, starting transfers between devices, body(): lax.ppermute(influence[8:], ALL, [(i, DEV - 1 - i) for i in range(DEV)])  17.1 us
    all_to_all x1, waiting for transfers between devices, swap(): return lax.all_to_all(x, axis, split_axis=0, concat_axis=0, tiled=True)  10.5 us
    pallas_call x8, Pallas kernels, call(): pl.pallas_call(kernel, out_shape=out_shape if many else out_shape[0], in_...  10.2 us
    unnamed x30, local copies, waits for them, and re-layouts  6.51 us
    ppermute x10, waiting for transfers between devices, shifted(): lax.ppermute(x, axis, [(i, (i + distance) % count) for i in range(count)])  5.23 us
    all_to_all x1, starting transfers between devices, swap(): return lax.all_to_all(x, axis, split_axis=0, concat_axis=0, tiled=True)  4.43 us
  transfers between devices with their start and end apart: 12, of which 4 were waited for; matrix products, arithmetic and copies ran while one was open for 0% of the time, Pallas kernels for 1%

commit v1 on v0

--- a/solution.py
+++ b/solution.py
@@ -93,11 +93,6 @@
 
 
 @functools.cache
-def y_back():
-    return np.concatenate(halves(y_table().T.copy()), axis=0)
-
-
-@functools.cache
 def x_tables():
     twiddle = np.zeros((N_ROW, 2, LANES))
     k1 = np.arange(N_ROW)
@@ -194,20 +189,37 @@
 
 
 def partial_sums(device, live, sid, charges):
-    out = []
-    for mask in member_masks(device, live, sid):
+    row = lax.broadcasted_iota(jnp.int32, (8, LANES), 0)
+    lane = lax.broadcasted_iota(jnp.int32, (8, LANES), 1)
+    acc = jnp.zeros((8, LANES), f32)
+    for slot, mask in enumerate(member_masks(device, live, sid)):
         total = jnp.sum(jnp.where(mask, charges, 0.0), axis=1, keepdims=True)
         count = jnp.sum(jnp.where(mask, 1.0, 0.0), axis=1, keepdims=True)
-        total = jnp.broadcast_to(total, (8, LANES))
-        count = jnp.broadcast_to(count, (8, LANES))
-        out.append(jnp.concatenate([total, count], axis=0))
-    return out
+        acc = jnp.where(lane == 16 * slot + row, total, acc)
+        acc = jnp.where(lane == 16 * slot + 8 + row, count, acc)
+    return jnp.sum(acc, axis=0, keepdims=True)
+
+
+def fragment_means(device, sums, roll):
+    row = lax.broadcasted_iota(jnp.int32, (8, LANES), 0)
+    lane = lax.broadcasted_iota(jnp.int32, (8, LANES), 1)
+    means = []
+    for owner in owners(device):
+        around = owners(owner)
+        total = jnp.zeros((1, LANES), f32)
+        for slot, source in enumerate((0, 2, 1, 4, 3, 5)):
+            part = sums(around[source])
+            total = total + (roll(part, LANES - 16 * slot, 1) if slot else part)
+        mean = total / roll(total, LANES - 8, 1)
+        mean = jnp.where(lane == row, jnp.broadcast_to(mean, (8, LANES)), 0.0)
+        means.append(jnp.sum(mean, axis=1, keepdims=True))
+    return means
 
 
 def neutral_charges(device, live, sid, charges, means):
     acc = jnp.zeros((8, ATOMS), f32)
     for mask, mean in zip(member_masks(device, live, sid), means):
-        acc = acc + jnp.where(mask, mean[:, 0:1], 0.0)
+        acc = acc + jnp.where(mask, mean, 0.0)
     mean = jnp.sum(acc, axis=0, keepdims=True)
     lane = lax.broadcasted_iota(jnp.int32, (1, ATOMS), 1)
     return jnp.where(lane < live, charges - mean, 0.0)
@@ -274,12 +286,10 @@
     return jnp.concatenate(main + halo, axis=0)
 
 
-def spread_to_z(neutral, cell_x, cell_y, cell_z, fraction, table, roll):
+def spread_to_z(neutral, cell_x, cell_y, fraction, z_high, z_low, table, roll):
     weights = spline_values(fraction)
-    wx = [w[0:1] for w in weights]
+    wx = [w[0:1] * neutral for w in weights]
     wy = [w[1:2] for w in weights]
-    wz = [w[2:3] * neutral for w in weights]
-    z_rows = place_periodic(cell_z, wz)
     x_rows = place(cell_x, wx, lax.broadcasted_iota(jnp.int32, (16, ATOMS), 0))
     y_rows = place(cell_y, wy, lax.broadcasted_iota(jnp.int32, (16, ATOMS), 0))
     y_edge = y_halo_rows(cell_y, wy)
@@ -289,11 +299,17 @@
         axis=0,
     )
     plane_high, plane_low = split(plane)
-    z_high, z_low = split(z_rows)
     grid = dot(plane_high, z_high, NT) + (dot(plane_low, z_high, NT) + dot(plane_high, z_low, NT))
     grid_high, grid_low = split(grid)
     wave = dot(grid_high, table[0]) + (dot(grid_low, table[0]) + dot(grid_high, table[1]))
     return to_messages(wave, roll)
+
+
+def z_parts(cell_z, fraction):
+    z = fraction[2:3]
+    return split(place_periodic(cell_z, spline_values(z))) + split(
+        place_periodic(cell_z, spline_slopes(z))
+    )
 
 
 def y_stage(x, table):
@@ -301,6 +317,14 @@
     half = table.shape[0] // 2
     both = dot(table, jnp.concatenate([high, low], axis=1))
     return both[:half, :LANES] + (both[:half, LANES:] + both[half:, :LANES])
+
+
+def y_adjoint(re, im, table):
+    x = jnp.concatenate([re.T, im.T], axis=1)
+    high, low = split(x)
+    both = dot(jnp.concatenate([high, low], axis=0), table[: 2 * N])
+    y = both[:LANES] + (both[LANES:] + dot(high, table[2 * N :]))
+    return y.T
 
 
 def fft(values, sign):
@@ -395,7 +419,7 @@
     return out
 
 
-def interpolate(wave, neutral, cell_x, cell_y, cell_z, fraction, table):
+def interpolate(wave, neutral, cell_x, cell_y, fraction, z_rows, z_slopes, table):
     weights = spline_values(fraction)
     slopes = spline_slopes(fraction)
     number = lax.broadcasted_iota(jnp.int32, (16, ATOMS), 0)
@@ -405,18 +429,15 @@
     vy = [w[1:2] for w in slopes]
     y_rows, y_slopes = place(cell_y, wy, number), place(cell_y, vy, number)
     y_edge, y_edge_slopes = y_halo_rows(cell_y, wy), y_halo_rows(cell_y, vy)
-    z_rows = place_periodic(cell_z, [w[2:3] for w in weights])
-    z_slopes = place_periodic(cell_z, [w[2:3] for w in slopes])
     high, low = split(wave)
     grid = dot(high, table[0], NT) + (dot(low, table[0], NT) + dot(high, table[1], NT))
     grid_high, grid_low = split(grid)
 
-    def sample(rows):
-        high, low = split(rows)
+    def sample(high, low):
         return dot(grid_high, high) + (dot(grid_low, high) + dot(grid_high, low))
 
-    at = sample(z_rows)
-    at_slope = sample(z_slopes)
+    at = sample(*z_rows)
+    at_slope = sample(*z_slopes)
     value = jnp.zeros((8, ATOMS), f32)
     grad_x, grad_y, grad_z = value, value, value
 
@@ -444,19 +465,41 @@
     return energy, force
 
 
-def partial_kernel(dev, live, sid, charges, *out):
-    for ref, x in zip(out, partial_sums(dev[0], live[0], sid[...], charges[...])):
+def partial_kernel(dev, live, sid_hbm, charges_hbm, out, sid, charges, sems):
+    copies = [
+        pltpu.make_async_copy(sid_hbm, sid, sems.at[0]),
+        pltpu.make_async_copy(charges_hbm, charges, sems.at[1]),
+    ]
+    for copy in copies:
+        copy.start()
+    for copy in copies:
+        copy.wait()
+    row = partial_sums(dev[0], live[0], sid[...], charges[...])
+    out[...] = jnp.broadcast_to(row, (DEV, LANES))
+
+
+def prefetch_kernel(cells_hbm, fraction_hbm, influence, z_tab, y_tab, mix_tab, turn_tab, *refs):
+    cells, fraction, mirror, edge, z, y, mix, turn = refs[:8]
+    parts, sems = refs[8:12], refs[12]
+    pairs = [
+        (cells_hbm, cells),
+        (fraction_hbm, fraction),
+        (influence.at[8:16], mirror),
+        (influence.at[8:16, 0], edge),
+        (z_tab, z),
+        (y_tab, y),
+        (mix_tab, mix),
+        (turn_tab, turn),
+    ]
+    copies = [pltpu.make_async_copy(a, b, sems.at[i]) for i, (a, b) in enumerate(pairs)]
+    for copy in copies:
+        copy.start()
+    copies[0].wait()
+    copies[1].wait()
+    for ref, x in zip(parts, z_parts(cells[2:3], fraction[...])):
         ref[...] = x
-
-
-def mean_kernel(own, a, b, c, d, e, mirror, mean, packed):
-    total = own[...] + a[...] + b[...] + c[...] + d[...] + e[...]
-    result = total[:8] / total[8:]
-    mean[...] = result
-    packed[0:8, :] = result
-    for p in range(8):
-        packed[8 + p : 9 + p, :] = mirror[p, 0:1, :LANES]
-        packed[16 + p : 17 + p, :] = mirror[p, 0:1, LANES:]
+    for copy in copies[2:]:
+        copy.wait()
 
 
 def local_cells(dev, cells):
@@ -467,13 +510,16 @@
     )
 
 
-def spread_kernel(dev, live, sid, charges, cells, fraction, m0, m1, m2, m3, m4, m5, table, out, neutral_out):
+def spread_kernel(dev, live, sums, sid, charges, cells, fraction, z_high, z_low, table, out, neutral_out):
     d = dev[0]
-    means = [m0[...], m1[...], m2[0:8, :], m3[...], m4[...], m5[...]]
+    means = fragment_means(d, lambda s: sums[pl.ds(s, 1), :], pltpu.roll)
     neutral = neutral_charges(d, live[0], sid[...], charges[...], means)
     neutral_out[...] = neutral
-    x, y, z = local_cells(d, cells[...])
-    for c, message in enumerate(spread_to_z(neutral, x, y, z, fraction[...], table, pltpu.roll)):
+    x, y, _ = local_cells(d, cells[...])
+    messages = spread_to_z(
+        neutral, x, y, fraction[...], z_high[...], z_low[...], table, pltpu.roll
+    )
+    for c, message in enumerate(messages):
         out[c] = message
 
 
@@ -486,14 +532,15 @@
 def y_back_kernel(x, table, out):
     re = x[:, :, :LANES].reshape(N, LANES)
     im = x[:, :, LANES:].reshape(N, LANES)
-    y = y_stage(jnp.concatenate([re, im], axis=0), table[...])
-    out[...] = y.reshape(N_COL, 40, LANES)
-
-
-def gain_kernel(dev, own, mirror, packed, out):
-    edge = jnp.concatenate([packed[8:16, :], packed[16:24, :]], axis=1)
+    out[...] = y_adjoint(re, im, table).reshape(N_COL, 40, LANES)
+
+
+def gain_kernel(dev, influence, mirror, edge, out, own, sem):
+    copy = pltpu.make_async_copy(influence, own, sem)
+    copy.start()
+    copy.wait()
     flat = own[...].reshape(128, N)
-    pieces = gain_table(dev[0], flat, mirror[...].reshape(64, N), edge, pltpu.roll)
+    pieces = gain_table(dev[0], flat, mirror[...].reshape(64, N), edge[...], pltpu.roll)
     for k1, piece in enumerate(pieces):
         out[k1 * 8 : (k1 + 1) * 8, :LANES] = piece
         out[k1 * 8 : (k1 + 1) * 8, LANES:] = piece
@@ -510,32 +557,33 @@
         out[r, :, LANES:] = im
 
 
-def atom_kernel(dev, message, neutral, cells, fraction, table, force, energy):
+def atom_kernel(dev, message, neutral, cells, fraction, zh, zl, vh, vl, table, force, energy):
     wave = from_messages(lambda c: message[c], pltpu.roll)
-    x, y, z = local_cells(dev[0], cells[...])
-    e, g = interpolate(wave, neutral[...], x, y, z, fraction[...], table)
+    x, y, _ = local_cells(dev[0], cells[...])
+    e, g = interpolate(
+        wave, neutral[...], x, y, fraction[...], (zh[...], zl[...]), (vh[...], vl[...]), table
+    )
     energy[...] = e
     for d in range(3):
         force[d : d + 1, :] = g[d]
 
 
-def call(kernel, shapes, scalars, *args):
-    smem = pl.BlockSpec(memory_space=pltpu.SMEM)
-    vmem = pl.BlockSpec(memory_space=pltpu.VMEM)
+def call(kernel, outs, spaces, args, scratch=()):
+    kinds = {
+        "s": pl.BlockSpec(memory_space=pltpu.SMEM),
+        "v": pl.BlockSpec(memory_space=pltpu.VMEM),
+        "h": pl.BlockSpec(memory_space=pl.ANY),
+    }
+    shapes = [jax.ShapeDtypeStruct(o[0], o[1]) if isinstance(o[0], tuple) else jax.ShapeDtypeStruct(o, f32) for o in outs]
     many = len(shapes) > 1
-    out_shape = [jax.ShapeDtypeStruct(s, f32) for s in shapes]
     return pl.pallas_call(
         kernel,
-        out_shape=out_shape if many else out_shape[0],
-        in_specs=[smem] * scalars + [vmem] * (len(args) - scalars),
-        out_specs=[vmem] * len(shapes) if many else vmem,
+        out_shape=shapes if many else shapes[0],
+        in_specs=[kinds[k] for k in spaces],
+        out_specs=[kinds["v"]] * len(shapes) if many else kinds["v"],
+        scratch_shapes=list(scratch),
         compiler_params=pltpu.CompilerParams(vmem_limit_bytes=48 << 20),
     )(*args)
-
-
-def shifted(x, axis, distance):
-    count = lax.axis_size(axis)
-    return lax.ppermute(x, axis, [(i, (i + distance) % count) for i in range(count)])
 
 
 def swap(x, axis):
@@ -546,47 +594,71 @@
     dev = lax.axis_index(ALL).astype(jnp.int32).reshape(1)
     charges = charges.reshape(1, ATOMS)
     sid = structure_id.reshape(1, ATOMS)
-    mirror = lax.ppermute(influence[8:], ALL, [(i, DEV - 1 - i) for i in range(DEV)])
-    parts = call(partial_kernel, [(16, LANES)] * 6, 2, dev, live_count, sid, charges)
-    mean, packed = call(
-        mean_kernel,
-        [(8, LANES), (24, LANES)],
-        0,
-        parts[0],
-        shifted(parts[1], ROW, 1),
-        shifted(parts[2], ROW, -1),
-        shifted(parts[3], COL, 1),
-        shifted(parts[4], COL, -1),
-        shifted(parts[5], ALL, DEV // 2),
-        mirror,
-    )
-    packed = shifted(packed, ROW, 1)
-    after_row = shifted(mean, ROW, -1)
-    after_col = shifted(mean, COL, -1)
-    before_col = shifted(mean, COL, 1)
-    far = shifted(mean, ALL, DEV // 2)
+    sums = call(
+        partial_kernel,
+        [(DEV, LANES)],
+        "sshh",
+        (dev, live_count, sid, charges),
+        [
+            pltpu.VMEM((1, ATOMS), jnp.int32),
+            pltpu.VMEM((1, ATOMS), f32),
+            pltpu.SemaphoreType.DMA((2,)),
+        ],
+    )
+    sums = swap(sums.reshape(DEV, 1, LANES), ALL).reshape(DEV, LANES)
+    twiddle, mix = x_tables()
+    half = ((N, ATOMS), bf16)
+    cells, fraction, mirror, edge, z_tab, y_tab, mix, twiddle, zh, zl, vh, vl = call(
+        prefetch_kernel,
+        [
+            ((3, ATOMS), jnp.int32),
+            (3, ATOMS),
+            (8, 8, N),
+            (8, N),
+            ((2, N, 3 * LANES), bf16),
+            ((4 * N, 40 * N_COL), bf16),
+            ((2, 2 * LANES, 2 * LANES), bf16),
+            (N_ROW, 2, LANES),
+            half,
+            half,
+            half,
+            half,
+        ],
+        "hhhhhhh",
+        (cells, fraction, influence, z_table(), y_forward(), mix, twiddle),
+        [pltpu.SemaphoreType.DMA((8,))],
+    )
+    mirror = lax.ppermute(mirror, ALL, [(i, DEV - 1 - i) for i in range(DEV)])
+    edge = lax.ppermute(
+        edge,
+        ALL,
+        [(i, (N_ROW - i // N_COL) % N_ROW * N_COL + N_COL - 1 - i % N_COL) for i in range(DEV)],
+    )
+    gain = call(
+        gain_kernel,
+        [(N, 2 * LANES)],
+        "shvv",
+        (dev, influence, mirror, edge),
+        [pltpu.VMEM((16, 8, N), f32), pltpu.SemaphoreType.DMA(())],
+    )
     messages, neutral = call(
         spread_kernel,
         [(N_COL, 40, LANES), (1, ATOMS)],
-        2,
-        dev, live_count, sid, charges, cells, fraction,
-        mean, after_row, packed, after_col, before_col, far,
-        z_table(),
-    )
-    gain = call(gain_kernel, [(N, 2 * LANES)], 1, dev, influence, mirror, packed)
-    twiddle, mix = x_tables()
+        "ssvvvvvvvv",
+        (dev, live_count, sums, sid, charges, cells, fraction, zh, zl, z_tab),
+    )
     columns = swap(messages, COL)
-    rows = call(y_forward_kernel, [(N_ROW, 8, 2 * LANES)], 0, columns, y_forward())
+    rows = call(y_forward_kernel, [(N_ROW, 8, 2 * LANES)], "vv", (columns, y_tab))
     rows = swap(rows, ROW)
-    rows = call(x_kernel, [(N_ROW, 8, 2 * LANES)], 0, rows, gain, twiddle, mix)
+    rows = call(x_kernel, [(N_ROW, 8, 2 * LANES)], "vvvv", (rows, gain, twiddle, mix))
     rows = swap(rows, ROW)
-    columns = call(y_back_kernel, [(N_COL, 40, LANES)], 0, rows, y_back())
+    columns = call(y_back_kernel, [(N_COL, 40, LANES)], "vv", (rows, y_tab))
     columns = swap(columns, COL)
     forces, energy = call(
         atom_kernel,
         [(3, ATOMS), (1, ATOMS)],
-        1,
-        dev, columns, neutral, cells, fraction, z_table(),
+        "svvvvvvvvv",
+        (dev, columns, neutral, cells, fraction, zh, zl, vh, vl, z_tab),
     )
     return forces, energy.reshape(ATOMS)
 

time: 137 us -> 134 us (0.978)
  starting transfers between devices: 48.4 us -> 41 us
  blocking collectives: 53.4 us -> 60.1 us
  waiting for transfers between devices: 15.8 us -> 9.55 us
  local copies, waits for them, and re-layouts: 7.36 us -> 9.66 us
  Pallas kernels: 10.2 us -> 11.8 us
    ppermute x11 -> x2, starting transfers between devices: 43.9 us -> 11.1 us  [the longest x1 5.85 us: body(): mirror = lax.ppermute(mirror, ALL, [(i, DEV - 1 - i) for i in range(DEV)])]
    all_to_all x1 -> x2, starting transfers between devices: 4.43 us -> 29.8 us  [swap(): return lax.all_to_all(x, axis, split_axis=0, concat_axis=0, tiled=True)]
    all_to_all x3, blocking collectives: 53.4 us -> 60.1 us  [swap(): return lax.all_to_all(x, axis, split_axis=0, concat_axis=0, tiled=True)]
    ppermute x11 -> x2, waiting for transfers between devices: 5.23 us -> 1.76 us  [the longest x1 1.59 us: body(): lax.ppermute(edge, ALL, [(i, (N_ROW - i // N_COL) % N_ROW * N_COL + N_COL...]
    unnamed x30 -> x34, local copies, waits for them, and re-layouts: 6.51 us -> 9.66 us
    all_to_all x1 -> x2, waiting for transfers between devices: 10.5 us -> 7.79 us  [swap(): return lax.all_to_all(x, axis, split_axis=0, concat_axis=0, tiled=True)]
    pallas_call x8, Pallas kernels: 10.2 us -> 11.8 us  [call(): pl.pallas_call(kernel, out_shape=shapes if many else shapes[0], in_specs=...]
  transfers between devices with their start and end apart: 12 -> 4, of which waited for: 4 -> 3; matrix products, arithmetic and copies ran while one was open for 0% -> 0% of each run, Pallas kernels for 1% -> 2%
where the time goes in v1:
time: 134 us
  blocking collectives  60.1 us (45%)
  starting transfers between devices  41 us (31%)
  Pallas kernels  11.8 us (9%)
  local copies, waits for them, and re-layouts  9.66 us (7%)
  waiting for transfers between devices  9.55 us (7%)
  between operations  1.43 us (1%)
    all_to_all x3, blocking collectives, swap(): return lax.all_to_all(x, axis, split_axis=0, concat_axis=0, tiled=True)  60.1 us
    all_to_all x2, starting transfers between devices, swap(): return lax.all_to_all(x, axis, split_axis=0, concat_axis=0, tiled=True)  29.8 us
    pallas_call x8, Pallas kernels, call(): pl.pallas_call(kernel, out_shape=shapes if many else shapes[0], in_specs=...  11.8 us
    unnamed x34, local copies, waits for them, and re-layouts  9.66 us
    all_to_all x2, waiting for transfers between devices, swap(): return lax.all_to_all(x, axis, split_axis=0, concat_axis=0, tiled=True)  7.79 us
    ppermute x1, starting transfers between devices, body(): mirror = lax.ppermute(mirror, ALL, [(i, DEV - 1 - i) for i in range(DEV)])  5.85 us
    ppermute x1, starting transfers between devices, body(): lax.ppermute(edge, ALL, [(i, (N_ROW - i // N_COL) % N_ROW * N_COL + N_COL...  5.28 us
  transfers between devices with their start and end apart: 4, of which 3 were waited for; matrix products, arithmetic and copies ran while one was open for 0% of the time, Pallas kernels for 2%

profile of v1, /device:TPU:1, one launch (start us, length us, event | category | flops | bytes accessed | tf_op | source)
XLA Modules:
  0.0 133.5 jit_solution(17771074686725942688)
XLA Ops:
  1.3 0.0 copy-start.13
  1.3 0.7 copy-done.13
  2.0 0.0 copy-start.15
  2.0 0.7 copy-done.15
  2.7 0.9 shard_map.113
  3.5 0.0 copy-start.14
  3.5 0.0 copy-start.16
  3.6 22.2 %all-to-all-start = ((f32[512,1,128]{2,1,0:T(1,128)}), f32[512,1,128]{2,1,0:T(1,128)S(1)}, u32[]{:S(2)}, u32[]{:S(2)}) async-start(f32[512,1,128]{2,1,0:T(1,128)} %bitcast.4), calls=%async_computation | async-start | bytes 524288 | tf_op jit(solution)/shard_map/all_to_all | solution.py:590
  25.7 0.0 copy-start
  25.7 0.9 copy-done
  26.6 0.0 copy-start.6
  26.6 1.0 copy-done.6
  27.6 0.0 copy-start.7
  27.6 0.9 copy-done.7
  28.6 0.0 copy-start.10
  28.6 0.8 copy-done.10
  29.3 0.0 copy-start.11
  29.3 0.7 copy-done.11
  30.1 0.0 copy-start.12
  30.1 0.7 copy-done.12
  30.8 1.7 %shard_map.114 = (s32[3,1024]{1,0:T(4,128)S(1)}, f32[3,1024]{1,0:T(4,128)S(1)}, f32[8,8,256]{2,1,0:T(8,128)S(1)}, f32[8,256]{1,0:T(8,128)S(1)}, bf16[2,256,384]{...) custom-call(s32[3,1024]{1,0:T(4,128)S(1)} %copy-done.11, ...), custom_call_target="tpu_custom_call" | custom-call | tf_op jit(solution)/shard_map/pallas_call | solution.py:579
  32.5 0.0 copy-start.2
  32.5 0.8 copy-done.2
  33.3 0.0 copy-start.4
  33.3 0.8 copy-done.4
  34.1 0.0 copy-start.8
  34.1 0.7 copy-done.8
  34.8 7.8 %all-to-all-done = f32[512,1,128]{2,1,0:T(1,128)S(1)} async-done(((f32[512,1,128]{2,1,0:T(1,128)}), f32[512,1,128]{2,1,0:T(1,128)S(1)}, u32[]{:S(2)}, u32[]{:S(2)}) %all-to-all-start) | async-done | bytes 262176 | tf_op jit(solution)/shard_map/all_to_all | solution.py:590
  42.6 0.0 copy-done.14
  42.6 0.0 copy-done.16
  42.6 2.7 %shard_map.115 = (f32[16,40,128]{2,1,0:T(8,128)S(1)}, f32[1,1024]{1,0:T(1,128)S(1)}) custom-call(s32[1]{0:T(128)} %bitcast.dev, s32[1]{0:T(128)S(6)} %copy.13.live, f32[512,128]{1,0:T(8,128)S(1)} %bitcast.8, s32[1,1024]{1,0:T(1,128)S(1)} %bitcast.10, f32[1,1024]{1,0:T(1,128)S(1)} %bitcast.12, s32[3,1024]{1,0:T(4,128)S(1)} %get-tuple-element.18.cells, ...), custom_call_target="tpu_custom_call" | custom-call | tf_op jit(solution)/shard_map/pallas_call | solution.py:579
  45.3 16.1 %all_to_all.25.x = f32[16,40,128]{2,1,0:T(8,128)S(1)} all-to-all(f32[16,40,128]{2,1,0:T(8,128)S(1)} %get-tuple-element.23), channel_id=1, replica_groups=mesh['row_0'=4,'row_1'=8,'col_0'=8,'col_1'=2] {'col_0','col_1'}, dimensions={0} | all-to-all | bytes 655360 | tf_op jit(solution)/shard_map/all_to_all | solution.py:590
  61.4 0.0 copy-start.1
  61.4 1.3 shard_map.116
  62.7 7.7 %all-to-all-start.2 = ((f32[32,8,256]{2,1,0:T(8,128)}), f32[32,8,256]{2,1,0:T(8,128)S(1)}, u32[]{:S(2)}, u32[]{:S(2)}) async-start(f32[32,8,256]{2,1,0:T(8,128)} %shard_map.116), calls=%async_computation.2 | async-start | bytes 524288 | tf_op jit(solution)/shard_map/all_to_all | solution.py:590
  70.4 5.9 %collective-permute-start = (f32[8,8,256]{2,1,0:T(8,128)S(1)}, f32[8,8,256]{2,1,0:T(8,128)S(1)}, u32[]{:S(2)}, u32[]{:S(2)}) collective-permute-start(f32[8,8,256]{2,1,0:T(8,128)S(1)} %get-tuple-element.25), channel_id=1, source_target_pairs={{0,511},{1,510},{2,509},{3,508},{4,507},{5,506},{6,505},{7,504},{8... | collective-permute-start | bytes 196616 | tf_op jit(solution)/shard_map/ppermute | solution.py:631
  76.2 5.3 %collective-permute-start.1 = (f32[8,256]{1,0:T(8,128)S(1)}, f32[8,256]{1,0:T(8,128)S(1)}, u32[]{:S(2)}, u32[]{:S(2)}) collective-permute-start(f32[8,256]{1,0:T(8,128)S(1)} %get-tuple-element.26), channel_id=1, source_target_pairs={{0,15},{1,14},{2,13},{3,12},{4,11},{5,10},{6,9},{7,8},{8,7},{9,6},... | collective-permute-start | bytes 24584 | tf_op jit(solution)/shard_map/ppermute | solution.py:632
  81.5 1.6 %collective-permute-done.1.edge = f32[8,256]{1,0:T(8,128)S(1)} collective-permute-done((f32[8,256]{1,0:T(8,128)S(1)}, f32[8,256]{1,0:T(8,128)S(1)}, u32[]{:S(2)}, u32[]{:S(2)}) %collective-permute-start.1) | collective-permute-done | bytes 8224 | tf_op jit(solution)/shard_map/ppermute | solution.py:632
  83.1 0.2 collective-permute-done.mirror
  83.3 0.0 copy-done.1
  83.3 1.1 shard_map.117.gain
  84.3 0.0 all-to-all-done.2.x
  84.4 0.0 copy-start.9
  84.4 0.9 copy-done.9
  85.3 0.7 shard_map.118
  86.0 21.0 %all_to_all.26.x = f32[32,8,256]{2,1,0:T(8,128)S(1)} all-to-all(f32[32,8,256]{2,1,0:T(8,128)S(1)} %shard_map.118), channel_id=1, replica_groups=mesh['row_0'=4,'row_1'=8,'col_0'=8,'col_1'=2] {'row_0','row_1'}, dimensions={0} | all-to-all | bytes 524288 | tf_op jit(solution)/shard_map/all_to_all | solution.py:590
  107.0 0.0 copy-start.3
  107.0 0.0 copy-start.5
  107.0 0.6 shard_map.119
  107.6 23.0 %all_to_all.27.message = f32[16,40,128]{2,1,0:T(8,128)S(1)} all-to-all(f32[16,40,128]{2,1,0:T(8,128)S(1)} %shard_map.119), channel_id=1, replica_groups=mesh['row_0'=4,'row_1'=8,'col_0'=8,'col_1'=2] {'col_0','col_1'}, dimensions={0} | all-to-all | bytes 655360 | tf_op jit(solution)/shard_map/all_to_all | solution.py:590
  130.6 0.0 copy-done.3
  130.6 0.0 copy-done.5
  130.6 2.9 %shard_map.120 = (f32[3,1024]{1,0:T(4,128)}, f32[1,1024]{1,0:T(1,128)}) custom-call(s32[1]{0:T(128)} %bitcast.dev, f32[16,40,128]{2,1,0:T(8,128)S(1)} %all_to_all.27.message, f32[1,1024]{1,0:T(1,128)S(1)} %get-tuple-element.29.neutral, s32[3,1024]{1,0:T(4,128)S(1)} %get-tuple-element.18.cells, f32[3,1024]{1,0:T(4,128)S(1)} %get-tuple-element.19.fraction, ...), custom_call_target="tpu_custom_call" | custom-call | tf_op jit(solution)/shard_map/pallas_call | solution.py:579
Async XLA Ops:
  1.3 0.7 copy-start.13
  2.0 0.7 copy-start.15
  3.5 39.0 %copy-start.14 = (s32[1024]{0:T(1024)S(1)}, s32[1024]{0:T(1024)}, u32[]{:S(2)}) copy-start(s32[1024]{0:T(1024)} %param.11) | copy-start | bytes 12292
  3.5 39.0 %copy-start.16 = (f32[1024]{0:T(1024)S(1)}, f32[1024]{0:T(1024)}, u32[]{:S(2)}) copy-start(f32[1024]{0:T(1024)} %param.10) | copy-start | bytes 12292
  3.6 39.0 %all-to-all-start = ((f32[512,1,128]{2,1,0:T(1,128)}), f32[512,1,128]{2,1,0:T(1,128)S(1)}, u32[]{:S(2)}, u32[]{:S(2)}) async-start(f32[512,1,128]{2,1,0:T(1,128)} %bitcast.4), calls=%async_computation | async-start | bytes 524288 | tf_op jit(solution)/shard_map/all_to_all | solution.py:590
  25.7 0.9 copy-start
  26.6 1.0 copy-start.6
  27.6 0.9 copy-start.7
  28.6 0.8 copy-start.10
  29.3 0.7 copy-start.11
  30.1 0.7 copy-start.12
  32.5 0.8 copy-start.2
  33.3 0.8 copy-start.4
  34.1 0.7 copy-start.8
  61.4 21.9 %copy-start.1 = (f32[16,8,256]{2,1,0:T(8,128)S(1)}, f32[16,8,256]{2,1,0:T(8,128)}, u32[]{:S(2)}) copy-start(f32[16,8,256]{2,1,0:T(8,128)} %influence.3) | copy-start | bytes 393220
  62.7 21.6 %all-to-all-start.2 = ((f32[32,8,256]{2,1,0:T(8,128)}), f32[32,8,256]{2,1,0:T(8,128)S(1)}, u32[]{:S(2)}, u32[]{:S(2)}) async-start(f32[32,8,256]{2,1,0:T(8,128)} %shard_map.116), calls=%async_computation.2 | async-start | bytes 524288 | tf_op jit(solution)/shard_map/all_to_all | solution.py:590
  70.4 12.9 %collective-permute-start = (f32[8,8,256]{2,1,0:T(8,128)S(1)}, f32[8,8,256]{2,1,0:T(8,128)S(1)}, u32[]{:S(2)}, u32[]{:S(2)}) collective-permute-start(f32[8,8,256]{2,1,0:T(8,128)S(1)} %get-tuple-element.25), channel_id=1, source_target_pairs={{0,511},{1,510},{2,509},{3,508},{4,507},{5,506},{6,505},{7,504},{8... | collective-permute-start | bytes 196616 | tf_op jit(solution)/shard_map/ppermute | solution.py:631
  76.2 6.9 %collective-permute-start.1 = (f32[8,256]{1,0:T(8,128)S(1)}, f32[8,256]{1,0:T(8,128)S(1)}, u32[]{:S(2)}, u32[]{:S(2)}) collective-permute-start(f32[8,256]{1,0:T(8,128)S(1)} %get-tuple-element.26), channel_id=1, source_target_pairs={{0,15},{1,14},{2,13},{3,12},{4,11},{5,10},{6,9},{7,8},{8,7},{9,6},... | collective-permute-start | bytes 24584 | tf_op jit(solution)/shard_map/ppermute | solution.py:632
  84.4 1.0 copy-start.9
  107.0 23.6 %copy-start.3 = (bf16[256,1024]{1,0:T(8,128)(2,1)S(1)}, bf16[256,1024]{1,0:T(8,128)(2,1)}, u32[]{:S(2)}) copy-start(bf16[256,1024]{1,0:T(8,128)(2,1)} %copy-done.2) | copy-start | bytes 1572868
  107.0 23.6 %copy-start.5 = (bf16[256,1024]{1,0:T(8,128)(2,1)S(1)}, bf16[256,1024]{1,0:T(8,128)(2,1)}, u32[]{:S(2)}) copy-start(bf16[256,1024]{1,0:T(8,128)(2,1)} %copy-done.4) | copy-start | bytes 1572868

commit v2 on v1

--- a/solution.py
+++ b/solution.py
@@ -25,7 +25,9 @@
 COL = ("col_0", "col_1")
 ALL = ROW + COL
 MAIN = XI * CY
-PLANE = MAIN + XI * 8
+PLANE = MAIN + 3 * CY
+GROUPS = XI + 3
+ROWS = 2 * CY
 f32 = jnp.float32
 bf16 = jnp.bfloat16
 
@@ -65,31 +67,16 @@
 
 @functools.cache
 def y_table():
-    table = np.zeros((2, N, N_COL, 40))
-    ky = np.arange(N)
-    for c in range(N_COL):
-        for row in range(40):
-            if row < 16:
-                part, j = 0, row
-            elif row < 24:
-                part, j = (row - 16) // 4, 16 + row % 4
-                if j == 19:
-                    continue
-            else:
-                part, j = 1, row - 24
-            angle = 2.0 * np.pi * (ky * (CY * c + j) % N) / N
-            if part == 0:
-                table[0, :, c, row] = np.cos(angle)
-                table[1, :, c, row] = -np.sin(angle)
-            else:
-                table[0, :, c, row] = np.sin(angle)
-                table[1, :, c, row] = np.cos(angle)
-    return table.reshape(2 * N, N_COL * 40)
-
-
-@functools.cache
-def y_forward():
-    return np.concatenate(halves(y_table()), axis=0)
+    k = np.arange(N)
+    angle = (2.0 * np.pi / N) * (k[:, None] * k[None, :] % N)
+    cos = np.cos(angle).reshape(N, N_COL, CY)
+    sin = np.sin(angle).reshape(N, N_COL, CY)
+    table = np.zeros((2, N, N_COL, 2, CY))
+    table[0, :, :, 0] = cos
+    table[0, :, :, 1] = sin
+    table[1, :, :, 0] = -sin
+    table[1, :, :, 1] = cos
+    return np.concatenate(halves(table.reshape(2 * N, 2 * N)), axis=0)
 
 
 @functools.cache
@@ -164,8 +151,7 @@
 
 
 def y_halo_rows(cell, weights):
-    row = lax.broadcasted_iota(jnp.int32, (8, ATOMS), 0)
-    return place(cell, weights, CY + row % 4)
+    return place(cell, weights, CY + lax.broadcasted_iota(jnp.int32, (8, ATOMS), 0))
 
 
 def owners(device):
@@ -235,55 +221,84 @@
 
 
 def to_messages(wave, roll):
-    lanes = lane_iota(16)
-    sub = lax.broadcasted_iota(jnp.int32, (8, LANES), 0)
+    lanes = lane_iota(CY)
     out = []
     for c in range(N_COL):
-        main = [jnp.zeros((16, LANES), f32), jnp.zeros((16, LANES), f32)]
-        halo = [jnp.zeros((8, LANES), f32), jnp.zeros((8, LANES), f32)]
+        parts = []
         for part in range(2):
             tile, lane = group_tile(c, part)
-            cols = slice(tile * LANES, (tile + 1) * LANES)
-            for x in range(XI):
-                shift = (NK * x - lane) % LANES
-                here = (lanes >= NK * x) & (lanes < NK * x + NK)
-                piece = wave[x * CY : (x + 1) * CY, cols]
-                edge = wave[MAIN + x * 8 : MAIN + (x + 1) * 8, cols]
+            acc = jnp.zeros((CY, LANES), f32)
+            for g in range(GROUPS):
+                piece = wave[g * CY : (g + 1) * CY, tile * LANES : (tile + 1) * LANES]
+                shift = (NK * g - lane) % LANES
                 if shift:
                     piece = roll(piece, shift, 1)
-                    edge = roll(edge, shift, 1)
-                main[part] = jnp.where(here, piece, main[part])
-                halo[part] = jnp.where(here[:8], edge, halo[part])
-        both = jnp.where(sub < 4, halo[0], halo[1])
-        out.append(jnp.concatenate([main[0], both, main[1]], axis=0))
+                acc = jnp.where((lanes >= NK * g) & (lanes < NK * g + NK), piece, acc)
+            parts.append(acc)
+        out.append(jnp.concatenate(parts, axis=0))
     return out
 
 
 def from_messages(message, roll):
-    lanes = lane_iota(16)
-    sub = lax.broadcasted_iota(jnp.int32, (8, LANES), 0)
-    main = []
-    halo = []
-    for x in range(XI):
-        wide = [jnp.zeros((16, LANES), f32) for _ in range(3)]
-        edges = [jnp.zeros((8, LANES), f32) for _ in range(3)]
+    lanes = lane_iota(CY)
+    out = []
+    for g in range(GROUPS):
+        wide = [jnp.zeros((CY, LANES), f32) for _ in range(3)]
         for c in range(N_COL):
             block = message(c)
             for part in range(2):
                 tile, lane = group_tile(c, part)
-                shift = (lane - NK * x) % LANES
-                here = (lanes >= lane) & (lanes < lane + NK)
-                piece = block[0:16] if part == 0 else block[24:40]
-                edge = block[16:24]
+                piece = block[part * CY : (part + 1) * CY]
+                shift = (lane - NK * g) % LANES
                 if shift:
                     piece = roll(piece, shift, 1)
-                    edge = roll(edge, shift, 1)
-                wide[tile] = jnp.where(here, piece, wide[tile])
-                own = sub < 4 if part == 0 else sub >= 4
-                edges[tile] = jnp.where(here[:8] & own, edge, edges[tile])
-        main.append(jnp.concatenate(wide, axis=1))
-        halo.append(jnp.concatenate(edges, axis=1))
-    return jnp.concatenate(main + halo, axis=0)
+                wide[tile] = jnp.where((lanes >= lane) & (lanes < lane + NK), piece, wide[tile])
+        out.append(jnp.concatenate(wide, axis=1))
+    return jnp.concatenate(out, axis=0)
+
+
+def add_halo(blocks, roll, slant):
+    lane = lane_iota(8)
+    row = lax.broadcasted_iota(jnp.int32, (8, LANES), 0)
+    out = [None] * N_COL
+    for c in range(N_COL):
+        after = (c + 1) % N_COL
+        pair = []
+        for part in range(2):
+            low = slant(blocks[c][part][:8], 0)
+            high = slant(roll(blocks[c][part][8:], 8 * NK, 1), 0)
+            lines = jnp.zeros((8, LANES), f32)
+            for h in range(3):
+                first = NK * (XI + 2 - h) + NK * row
+                take_low = (lane - first + 2 * LANES) % LANES < NK
+                take_high = ((lane - first - 8 * NK + 3 * LANES) % LANES < NK) & (row < XI - 8)
+                line = jnp.where(take_low, low, 0.0) + jnp.where(take_high, high, 0.0)
+                lines = jnp.where(row == h, jnp.sum(line, axis=0, keepdims=True), lines)
+            lines = slant(lines, LANES - NK * (XI + 2))
+            main = blocks[after][part]
+            pair.append(jnp.concatenate([main[:8] + lines, main[8:]], axis=0))
+        out[after] = pair
+    return out
+
+
+def copy_halo(blocks, roll, slant):
+    lane = lane_iota(8)
+    out = []
+    for c in range(N_COL):
+        after = (c + 1) % N_COL
+        pair = []
+        for part in range(2):
+            low, high = blocks[c][part][:8], blocks[c][part][8:]
+            for h in range(3):
+                line = jnp.broadcast_to(blocks[after][part][h : h + 1], (8, LANES))
+                group = NK * (XI + 2 - h)
+                here = (lane >= group) & (lane < group + NK)
+                base = group - 15 * NK
+                low = jnp.where(here, slant(roll(line, base % LANES, 1), 0), low)
+                high = jnp.where(here, slant(line, base + 8 * NK), high)
+            pair.append(jnp.concatenate([low, high], axis=0))
+        out.append(pair)
+    return out
 
 
 def spread_to_z(neutral, cell_x, cell_y, fraction, z_high, z_low, table, roll):
@@ -295,7 +310,7 @@
     y_edge = y_halo_rows(cell_y, wy)
     plane = jnp.concatenate(
         [y_rows * x_rows[x : x + 1] for x in range(XI)]
-        + [y_edge * x_rows[x : x + 1] for x in range(XI)],
+        + [x_rows * y_edge[h : h + 1] for h in (2, 1, 0)],
         axis=0,
     )
     plane_high, plane_low = split(plane)
@@ -317,14 +332,6 @@
     half = table.shape[0] // 2
     both = dot(table, jnp.concatenate([high, low], axis=1))
     return both[:half, :LANES] + (both[:half, LANES:] + both[half:, :LANES])
-
-
-def y_adjoint(re, im, table):
-    x = jnp.concatenate([re.T, im.T], axis=1)
-    high, low = split(x)
-    both = dot(jnp.concatenate([high, low], axis=0), table[: 2 * N])
-    y = both[:LANES] + (both[LANES:] + dot(high, table[2 * N :]))
-    return y.T
 
 
 def fft(values, sign):
@@ -428,6 +435,8 @@
     wy = [w[1:2] for w in weights]
     vy = [w[1:2] for w in slopes]
     y_rows, y_slopes = place(cell_y, wy, number), place(cell_y, vy, number)
+    x_back = place(cell_x, [w[0:1] for w in weights], 15 - number)
+    x_back_slopes = place(cell_x, [w[0:1] for w in slopes], 15 - number)
     y_edge, y_edge_slopes = y_halo_rows(cell_y, wy), y_halo_rows(cell_y, vy)
     high, low = split(wave)
     grid = dot(high, table[0], NT) + (dot(low, table[0], NT) + dot(high, table[1], NT))
@@ -446,16 +455,21 @@
 
     for x in range(XI):
         main = at[x * CY : (x + 1) * CY]
-        edge = at[MAIN + x * 8 : MAIN + (x + 1) * 8]
-        main_slope = at_slope[x * CY : (x + 1) * CY]
-        edge_slope = at_slope[MAIN + x * 8 : MAIN + (x + 1) * 8]
-        plain = eight(main * y_rows) + edge * y_edge
-        turned = eight(main * y_slopes) + edge * y_edge_slopes
-        risen = eight(main_slope * y_rows) + edge_slope * y_edge
+        plain = eight(main * y_rows)
+        turned = eight(main * y_slopes)
+        risen = eight(at_slope[x * CY : (x + 1) * CY] * y_rows)
         value = value + plain * x_rows[x : x + 1]
         grad_x = grad_x + plain * x_slopes[x : x + 1]
         grad_y = grad_y + turned * x_rows[x : x + 1]
         grad_z = grad_z + risen * x_rows[x : x + 1]
+    for h in range(3):
+        rows = slice(MAIN + (2 - h) * CY, MAIN + (3 - h) * CY)
+        plain = eight(at[rows] * x_back)
+        weight = y_edge[h : h + 1]
+        value = value + plain * weight
+        grad_x = grad_x + eight(at[rows] * x_back_slopes) * weight
+        grad_y = grad_y + plain * y_edge_slopes[h : h + 1]
+        grad_z = grad_z + eight(at_slope[rows] * x_back) * weight
 
     def total(x):
         return jnp.sum(x, axis=0, keepdims=True)
@@ -465,35 +479,55 @@
     return energy, force
 
 
-def partial_kernel(dev, live, sid_hbm, charges_hbm, out, sid, charges, sems):
-    copies = [
-        pltpu.make_async_copy(sid_hbm, sid, sems.at[0]),
-        pltpu.make_async_copy(charges_hbm, charges, sems.at[1]),
-    ]
-    for copy in copies:
-        copy.start()
-    for copy in copies:
-        copy.wait()
-    row = partial_sums(dev[0], live[0], sid[...], charges[...])
-    out[...] = jnp.broadcast_to(row, (DEV, LANES))
-
-
-def prefetch_kernel(cells_hbm, fraction_hbm, influence, z_tab, y_tab, mix_tab, turn_tab, *refs):
-    cells, fraction, mirror, edge, z, y, mix, turn = refs[:8]
-    parts, sems = refs[8:12], refs[12]
-    pairs = [
-        (cells_hbm, cells),
-        (fraction_hbm, fraction),
-        (influence.at[8:16], mirror),
-        (influence.at[8:16, 0], edge),
-        (z_tab, z),
-        (y_tab, y),
-        (mix_tab, mix),
-        (turn_tab, turn),
-    ]
+def run_copies(pairs, sems):
     copies = [pltpu.make_async_copy(a, b, sems.at[i]) for i, (a, b) in enumerate(pairs)]
     for copy in copies:
         copy.start()
+    return copies
+
+
+def partial_kernel(dev, live, sid_hbm, charges_hbm, influence, out, sid, charges, mirror, edge, sems):
+    copies = run_copies(
+        [
+            (sid_hbm, sid),
+            (charges_hbm, charges),
+            (influence.at[8:16], mirror),
+            (influence.at[8:16, 0], edge),
+        ],
+        sems,
+    )
+    copies[0].wait()
+    copies[1].wait()
+    row = partial_sums(dev[0], live[0], sid[...], charges[...])
+    out[...] = jnp.broadcast_to(row, (N_COL, 8, LANES))
+    copies[2].wait()
+    copies[3].wait()
+
+
+def relay_kernel(dev, sums, out):
+    col = dev[0] % N_COL
+    row = lax.broadcasted_iota(jnp.int32, (8, LANES), 0)
+    acc = jnp.zeros((8, LANES), f32)
+    for k in range(5):
+        acc = jnp.where(row == k, sums[(col + N_COL + k - 2) % N_COL, 0:1, :], acc)
+    out[...] = jnp.broadcast_to(acc, (N_ROW, 8, LANES))
+
+
+def prefetch_kernel(cells_hbm, fraction_hbm, influence, z_tab, y_tab, mix_tab, turn_tab, *refs):
+    cells, fraction, own, z, y, mix, turn = refs[:7]
+    parts, sems = refs[7:11], refs[11]
+    copies = run_copies(
+        [
+            (cells_hbm, cells),
+            (fraction_hbm, fraction),
+            (influence, own),
+            (z_tab, z),
+            (y_tab, y),
+            (mix_tab, mix),
+            (turn_tab, turn),
+        ],
+        sems,
+    )
     copies[0].wait()
     copies[1].wait()
     for ref, x in zip(parts, z_parts(cells[2:3], fraction[...])):
@@ -512,7 +546,12 @@
 
 def spread_kernel(dev, live, sums, sid, charges, cells, fraction, z_high, z_low, table, out, neutral_out):
     d = dev[0]
-    means = fragment_means(d, lambda s: sums[pl.ds(s, 1), :], pltpu.roll)
+    col = d % N_COL
+
+    def row_of(s):
+        return sums[s // N_COL, pl.ds((s % N_COL - col + N_COL + 2) % N_COL, 1), :]
+
+    means = fragment_means(d, row_of, pltpu.roll)
     neutral = neutral_charges(d, live[0], sid[...], charges[...], means)
     neutral_out[...] = neutral
     x, y, _ = local_cells(d, cells[...])
@@ -523,22 +562,35 @@
         out[c] = message
 
 
+def slant(x, shift):
+    return pltpu.roll(x, shift, 1, stride=NK, stride_axis=0)
+
+
+def pairs_of(x):
+    return [[x[c, :CY], x[c, CY:]] for c in range(N_COL)]
+
+
 def y_forward_kernel(x, table, out):
-    y = y_stage(x[...].reshape(N_COL * 40, LANES), table[...])
+    blocks = add_halo(pairs_of(x), pltpu.roll, slant)
+    y = y_stage(jnp.concatenate([b for pair in blocks for b in pair], axis=0), table[...])
     out[:, :, :LANES] = y[:N].reshape(N_ROW, 8, LANES)
     out[:, :, LANES:] = y[N:].reshape(N_ROW, 8, LANES)
 
 
 def y_back_kernel(x, table, out):
-    re = x[:, :, :LANES].reshape(N, LANES)
-    im = x[:, :, LANES:].reshape(N, LANES)
-    out[...] = y_adjoint(re, im, table).reshape(N_COL, 40, LANES)
-
-
-def gain_kernel(dev, influence, mirror, edge, out, own, sem):
-    copy = pltpu.make_async_copy(influence, own, sem)
-    copy.start()
-    copy.wait()
+    pieces = []
+    for r in range(0, N_ROW, 2):
+        pieces += [x[r, :, :LANES], x[r + 1, :, :LANES], -x[r, :, LANES:], -x[r + 1, :, LANES:]]
+    y = y_stage(jnp.concatenate(pieces, axis=0), table[...])
+    blocks = [
+        [y[c * CY : (c + 1) * CY], -y[N + c * CY : N + (c + 1) * CY]] for c in range(N_COL)
+    ]
+    for c, (re, im) in enumerate(copy_halo(blocks, pltpu.roll, slant)):
+        out[c, :CY] = re
+        out[c, CY:] = im
+
+
+def gain_kernel(dev, own, mirror, edge, out):
     flat = own[...].reshape(128, N)
     pieces = gain_table(dev[0], flat, mirror[...].reshape(64, N), edge[...], pltpu.roll)
     for k1, piece in enumerate(pieces):
@@ -572,17 +624,21 @@
     kinds = {
         "s": pl.BlockSpec(memory_space=pltpu.SMEM),
         "v": pl.BlockSpec(memory_space=pltpu.VMEM),
-        "h": pl.BlockSpec(memory_space=pl.ANY),
+        "h": pl.BlockSpec(memory_space=pltpu.HBM),
     }
     shapes = [jax.ShapeDtypeStruct(o[0], o[1]) if isinstance(o[0], tuple) else jax.ShapeDtypeStruct(o, f32) for o in outs]
     many = len(shapes) > 1
+    args = [
+        pltpu.with_memory_space_constraint(x, pltpu.HBM) if k == "h" else x
+        for k, x in zip(spaces, args)
+    ]
     return pl.pallas_call(
         kernel,
         out_shape=shapes if many else shapes[0],
         in_specs=[kinds[k] for k in spaces],
         out_specs=[kinds["v"]] * len(shapes) if many else kinds["v"],
         scratch_shapes=list(scratch),
-        compiler_params=pltpu.CompilerParams(vmem_limit_bytes=48 << 20),
+        compiler_params=pltpu.CompilerParams(vmem_limit_bytes=16 << 20),
     )(*args)
 
 
@@ -594,29 +650,33 @@
     dev = lax.axis_index(ALL).astype(jnp.int32).reshape(1)
     charges = charges.reshape(1, ATOMS)
     sid = structure_id.reshape(1, ATOMS)
-    sums = call(
+    sums, sid, charges, mirror, edge = call(
         partial_kernel,
-        [(DEV, LANES)],
-        "sshh",
-        (dev, live_count, sid, charges),
-        [
-            pltpu.VMEM((1, ATOMS), jnp.int32),
-            pltpu.VMEM((1, ATOMS), f32),
-            pltpu.SemaphoreType.DMA((2,)),
-        ],
-    )
-    sums = swap(sums.reshape(DEV, 1, LANES), ALL).reshape(DEV, LANES)
+        [(N_COL, 8, LANES), ((1, ATOMS), jnp.int32), (1, ATOMS), (8, 8, N), (8, N)],
+        "sshhh",
+        (dev, live_count, sid, charges, influence),
+        [pltpu.SemaphoreType.DMA((4,))],
+    )
+    mirror = lax.ppermute(mirror, ALL, [(i, DEV - 1 - i) for i in range(DEV)])
+    edge = lax.ppermute(
+        edge,
+        ALL,
+        [(i, (N_ROW - i // N_COL) % N_ROW * N_COL + N_COL - 1 - i % N_COL) for i in range(DEV)],
+    )
+    sums = swap(sums, COL)
+    sums, mirror, edge = lax.optimization_barrier((sums, mirror, edge))
+    sums = call(relay_kernel, [(N_ROW, 8, LANES)], "sv", (dev, sums))
+    sums = swap(sums, ROW)
     twiddle, mix = x_tables()
     half = ((N, ATOMS), bf16)
-    cells, fraction, mirror, edge, z_tab, y_tab, mix, twiddle, zh, zl, vh, vl = call(
+    cells, fraction, own, z_tab, y_tab, mix, twiddle, zh, zl, vh, vl = call(
         prefetch_kernel,
         [
             ((3, ATOMS), jnp.int32),
             (3, ATOMS),
-            (8, 8, N),
-            (8, N),
+            (16, 8, N),
             ((2, N, 3 * LANES), bf16),
-            ((4 * N, 40 * N_COL), bf16),
+            ((4 * N, 2 * N), bf16),
             ((2, 2 * LANES, 2 * LANES), bf16),
             (N_ROW, 2, LANES),
             half,
@@ -625,25 +685,14 @@
             half,
         ],
         "hhhhhhh",
-        (cells, fraction, influence, z_table(), y_forward(), mix, twiddle),
-        [pltpu.SemaphoreType.DMA((8,))],
-    )
-    mirror = lax.ppermute(mirror, ALL, [(i, DEV - 1 - i) for i in range(DEV)])
-    edge = lax.ppermute(
-        edge,
-        ALL,
-        [(i, (N_ROW - i // N_COL) % N_ROW * N_COL + N_COL - 1 - i % N_COL) for i in range(DEV)],
-    )
-    gain = call(
-        gain_kernel,
-        [(N, 2 * LANES)],
-        "shvv",
-        (dev, influence, mirror, edge),
-        [pltpu.VMEM((16, 8, N), f32), pltpu.SemaphoreType.DMA(())],
-    )
+        (cells, fraction, influence, z_table(), y_table(), mix, twiddle),
+        [pltpu.SemaphoreType.DMA((7,))],
+    )
+    gain = call(gain_kernel, [(N, 2 * LANES)], "svvv", (dev, own, mirror, edge))
+    zh, gain = lax.optimization_barrier((zh, gain))
     messages, neutral = call(
         spread_kernel,
-        [(N_COL, 40, LANES), (1, ATOMS)],
+        [(N_COL, ROWS, LANES), (1, ATOMS)],
         "ssvvvvvvvv",
         (dev, live_count, sums, sid, charges, cells, fraction, zh, zl, z_tab),
     )
@@ -652,7 +701,7 @@
     rows = swap(rows, ROW)
     rows = call(x_kernel, [(N_ROW, 8, 2 * LANES)], "vvvv", (rows, gain, twiddle, mix))
     rows = swap(rows, ROW)
-    columns = call(y_back_kernel, [(N_COL, 40, LANES)], "vv", (rows, y_tab))
+    columns = call(y_back_kernel, [(N_COL, ROWS, LANES)], "vv", (rows, y_tab))
     columns = swap(columns, COL)
     forces, energy = call(
         atom_kernel,

time: 134 us -> 129 us (0.963)
  local copies, waits for them, and re-layouts: 9.66 us -> 1.5 us
  blocking collectives: 60.1 us -> 67.8 us
  starting transfers between devices: 41 us -> 35.8 us
    all_to_all x2, starting transfers between devices: 29.8 us -> 19.9 us  [swap(): return lax.all_to_all(x, axis, split_axis=0, concat_axis=0, tiled=True)]
    unnamed x34 -> x8, local copies, waits for them, and re-layouts: 9.66 us -> 1.5 us
    ppermute x1, starting transfers between devices: 5.85 us -> 13.9 us  [body(): mirror = lax.ppermute(mirror, ALL, [(i, DEV - 1 - i) for i in range(DEV)])]
    all_to_all x3 -> x4, blocking collectives: 60.1 us -> 67.8 us  [swap(): return lax.all_to_all(x, axis, split_axis=0, concat_axis=0, tiled=True)]
    ppermute x1, starting transfers between devices: 5.28 us -> 2.05 us  [body(): lax.ppermute(edge, ALL, [(i, (N_ROW - i // N_COL) % N_ROW * N_COL + N_COL...]
    all_to_all x2, waiting for transfers between devices: 7.79 us -> 4.72 us  [swap(): return lax.all_to_all(x, axis, split_axis=0, concat_axis=0, tiled=True)]
    ppermute x1, waiting for transfers between devices: 1.59 us -> 4.12 us  [body(): lax.ppermute(edge, ALL, [(i, (N_ROW - i // N_COL) % N_ROW * N_COL + N_COL...]
    pallas_call x8 -> x9, Pallas kernels: 11.8 us -> 12.7 us  [call(): pl.pallas_call(kernel, out_shape=shapes if many else shapes[0], in_specs=...]
  transfers between devices with their start and end apart: 4 -> 4, of which waited for: 3 -> 2; matrix products, arithmetic and copies ran while one was open for 0% -> 0% of each run, Pallas kernels for 2% -> 2%
where the time goes in v2:
time: 129 us; the launch traced here: 128 us
  blocking collectives  67.8 us (53%)
  starting transfers between devices  35.8 us (28%)
  Pallas kernels  12.7 us (10%)
  waiting for transfers between devices  8.84 us (7%)
  local copies, waits for them, and re-layouts  1.5 us (1%)
  between operations  1.38 us (1%)
    all_to_all x4, blocking collectives, swap(): return lax.all_to_all(x, axis, split_axis=0, concat_axis=0, tiled=True)  67.8 us
    all_to_all x2, starting transfers between devices, swap(): return lax.all_to_all(x, axis, split_axis=0, concat_axis=0, tiled=True)  19.9 us
    ppermute x1, starting transfers between devices, body(): mirror = lax.ppermute(mirror, ALL, [(i, DEV - 1 - i) for i in range(DEV)])  13.9 us
    pallas_call x9, Pallas kernels, call(): pl.pallas_call(kernel, out_shape=shapes if many else shapes[0], in_specs=...  12.7 us
    all_to_all x2, waiting for transfers between devices, swap(): return lax.all_to_all(x, axis, split_axis=0, concat_axis=0, tiled=True)  4.72 us
    ppermute x1, waiting for transfers between devices, body(): lax.ppermute(edge, ALL, [(i, (N_ROW - i // N_COL) % N_ROW * N_COL + N_COL...  4.12 us
  transfers between devices with their start and end apart: 4, of which 2 were waited for; matrix products, arithmetic and copies ran while one was open for 0% of the time, Pallas kernels for 2%

profile of v2, /device:TPU:1, one launch (start us, length us, event | category | flops | bytes accessed | tf_op | source)
XLA Modules:
  0.0 128.1 jit_solution(4925515501206729674)
XLA Ops:
  1.3 1.5 %shard_map.113 = (f32[16,8,128]{2,1,0:T(8,128)}, s32[1,1024]{1,0:T(1,128)S(1)}, f32[1,1024]{1,0:T(1,128)S(1)}, f32[8,8,256]{2,1,0:T(8,128)S(1)}, f32[8,256]{1,0:T(8,128)S(1)}) custom-call(s32[1]{0:T(128)} %bitcast.dev, s32[1]{0:T(128)S(6)} %copy.12.live, s32[1,1024]{1,0:T(1,128)} %bitcast.4, f32[1,1024]{1,0:T(1,128)} %bitcast.5, f32[16,8,256]{2,1,0:T(8,128)} %influence.3), custom_call_target="tpu_custom_call" | custom-call | tf_op jit(solution)/shard_map/pallas_call | solution.py:635
  2.8 10.2 %all-to-all-start = ((f32[16,8,128]{2,1,0:T(8,128)}), f32[16,8,128]{2,1,0:T(8,128)S(1)}, u32[]{:S(2)}, u32[]{:S(2)}) async-start(f32[16,8,128]{2,1,0:T(8,128)} %get-tuple-element.27), calls=%async_computation | async-start | bytes 131072 | tf_op jit(solution)/shard_map/all_to_all | solution.py:646
  13.0 13.9 %collective-permute-start = (f32[8,8,256]{2,1,0:T(8,128)S(1)}, f32[8,8,256]{2,1,0:T(8,128)S(1)}, u32[]{:S(2)}, u32[]{:S(2)}) collective-permute-start(f32[8,8,256]{2,1,0:T(8,128)S(1)} %get-tuple-element.28), channel_id=1, source_target_pairs={{0,511},{1,510},{2,509},{3,508},{4,507},{5,506},{6,505},{7,504},{8... | collective-permute-start | bytes 196616 | tf_op jit(solution)/shard_map/ppermute | solution.py:660
  26.9 2.0 %collective-permute-start.1 = (f32[8,256]{1,0:T(8,128)S(1)}, f32[8,256]{1,0:T(8,128)S(1)}, u32[]{:S(2)}, u32[]{:S(2)}) collective-permute-start(f32[8,256]{1,0:T(8,128)S(1)} %get-tuple-element.29), channel_id=1, source_target_pairs={{0,15},{1,14},{2,13},{3,12},{4,11},{5,10},{6,9},{7,8},{8,7},{9,6},... | collective-permute-start | bytes 24584 | tf_op jit(solution)/shard_map/ppermute | solution.py:661
  28.9 4.1 %collective-permute-done.1.edge = f32[8,256]{1,0:T(8,128)S(1)} collective-permute-done((f32[8,256]{1,0:T(8,128)S(1)}, f32[8,256]{1,0:T(8,128)S(1)}, u32[]{:S(2)}, u32[]{:S(2)}) %collective-permute-start.1) | collective-permute-done | bytes 8224 | tf_op jit(solution)/shard_map/ppermute | solution.py:661
  33.1 0.0 collective-permute-done.mirror
  33.1 0.0 all-to-all-done.sums
  33.1 0.7 shard_map.114
  33.7 9.7 %all-to-all-start.1 = ((f32[32,8,128]{2,1,0:T(8,128)}), f32[32,8,128]{2,1,0:T(8,128)S(1)}, u32[]{:S(2)}, u32[]{:S(2)}) async-start(f32[32,8,128]{2,1,0:T(8,128)} %shard_map.114), calls=%async_computation.1 | async-start | bytes 262144 | tf_op jit(solution)/shard_map/all_to_all | solution.py:646
  43.5 2.0 %shard_map.115 = (s32[3,1024]{1,0:T(4,128)S(1)}, f32[3,1024]{1,0:T(4,128)S(1)}, f32[16,8,256]{2,1,0:T(8,128)S(1)}, bf16[2,256,384]{2,1,0:T(8,128)(2,1)S(1)}, bf1...) custom-call(s32[3,1024]{1,0:T(4,128)} %cells_hbm.1, ...), custom_call_target="tpu_custom_call" | custom-call | tf_op jit(solution)/shard_map/pallas_call | solution.py:635
  45.5 0.0 copy-start
  45.5 0.8 copy-done
  46.3 0.0 copy-start.2
  46.3 0.7 copy-done.2
  47.0 0.9 shard_map.116.gain
  47.9 4.7 %all-to-all-done.1.sums = f32[32,8,128]{2,1,0:T(8,128)S(1)} async-done(((f32[32,8,128]{2,1,0:T(8,128)}), f32[32,8,128]{2,1,0:T(8,128)S(1)}, u32[]{:S(2)}, u32[]{:S(2)}) %all-to-all-start.1) | async-done | bytes 131104 | tf_op jit(solution)/shard_map/all_to_all | solution.py:646
  52.6 2.7 %shard_map.117 = (f32[16,32,128]{2,1,0:T(8,128)S(1)}, f32[1,1024]{1,0:T(1,128)S(1)}) custom-call(s32[1]{0:T(128)} %bitcast.dev, s32[1]{0:T(128)S(6)} %copy.12.live, f32[32,8,128]{2,1,0:T(8,128)S(1)} %all-to-all-done.1.sums, s32[1,1024]{1,0:T(1,128)S(1)} %get-tuple-element.31.sid, f32[1,1024]{1,0:T(1,128)S(1)} %get-tuple-element.32.charges, ...), custom_call_target="tpu_custom_call" | custom-call | tf_op jit(solution)/shard_map/pallas_call | solution.py:635
  55.3 19.9 %all_to_all.30.x = f32[16,32,128]{2,1,0:T(8,128)S(1)} all-to-all(f32[16,32,128]{2,1,0:T(8,128)S(1)} %get-tuple-element.42), channel_id=1, replica_groups=mesh['row_0'=4,'row_1'=8,'col_0'=8,'col_1'=2] {'col_0','col_1'}, dimensions={0} | all-to-all | bytes 524288 | tf_op jit(solution)/shard_map/all_to_all | solution.py:646
  75.3 0.7 shard_map.118
  76.0 0.0 copy-start.3
  76.0 14.2 %all_to_all.31.x = f32[32,8,256]{2,1,0:T(8,128)S(1)} all-to-all(f32[32,8,256]{2,1,0:T(8,128)S(1)} %shard_map.118), channel_id=1, replica_groups=mesh['row_0'=4,'row_1'=8,'col_0'=8,'col_1'=2] {'row_0','row_1'}, dimensions={0} | all-to-all | bytes 524288 | tf_op jit(solution)/shard_map/all_to_all | solution.py:646
  90.2 0.0 copy-done.3
  90.2 0.7 shard_map.119
  90.9 15.6 %all_to_all.32.x = f32[32,8,256]{2,1,0:T(8,128)S(1)} all-to-all(f32[32,8,256]{2,1,0:T(8,128)S(1)} %shard_map.119), channel_id=1, replica_groups=mesh['row_0'=4,'row_1'=8,'col_0'=8,'col_1'=2] {'row_0','row_1'}, dimensions={0} | all-to-all | bytes 524288 | tf_op jit(solution)/shard_map/all_to_all | solution.py:646
  106.5 0.7 shard_map.120
  107.2 0.0 copy-start.1
  107.2 18.1 %all_to_all.33.message = f32[16,32,128]{2,1,0:T(8,128)S(1)} all-to-all(f32[16,32,128]{2,1,0:T(8,128)S(1)} %shard_map.120), channel_id=1, replica_groups=mesh['row_0'=4,'row_1'=8,'col_0'=8,'col_1'=2] {'col_0','col_1'}, dimensions={0} | all-to-all | bytes 524288 | tf_op jit(solution)/shard_map/all_to_all | solution.py:646
  125.3 0.0 copy-done.1
  125.4 2.8 %shard_map.121 = (f32[3,1024]{1,0:T(4,128)}, f32[1,1024]{1,0:T(1,128)}) custom-call(s32[1]{0:T(128)} %bitcast.dev, f32[16,32,128]{2,1,0:T(8,128)S(1)} %all_to_all.33.message, f32[1,1024]{1,0:T(1,128)S(1)} %get-tuple-element.47.neutral, s32[3,1024]{1,0:T(4,128)S(1)} %get-tuple-element.33.cells, f32[3,1024]{1,0:T(4,128)S(1)} %get-tuple-element.34.fraction, ...), custom_call_target="tpu_custom_call" | custom-call | tf_op jit(solution)/shard_map/pallas_call | solution.py:635
Async XLA Ops:
  2.8 30.2 %all-to-all-start = ((f32[16,8,128]{2,1,0:T(8,128)}), f32[16,8,128]{2,1,0:T(8,128)S(1)}, u32[]{:S(2)}, u32[]{:S(2)}) async-start(f32[16,8,128]{2,1,0:T(8,128)} %get-tuple-element.27), calls=%async_computation | async-start | bytes 131072 | tf_op jit(solution)/shard_map/all_to_all | solution.py:646
  13.0 20.1 %collective-permute-start = (f32[8,8,256]{2,1,0:T(8,128)S(1)}, f32[8,8,256]{2,1,0:T(8,128)S(1)}, u32[]{:S(2)}, u32[]{:S(2)}) collective-permute-start(f32[8,8,256]{2,1,0:T(8,128)S(1)} %get-tuple-element.28), channel_id=1, source_target_pairs={{0,511},{1,510},{2,509},{3,508},{4,507},{5,506},{6,505},{7,504},{8... | collective-permute-start | bytes 196616 | tf_op jit(solution)/shard_map/ppermute | solution.py:660
  26.9 6.2 %collective-permute-start.1 = (f32[8,256]{1,0:T(8,128)S(1)}, f32[8,256]{1,0:T(8,128)S(1)}, u32[]{:S(2)}, u32[]{:S(2)}) collective-permute-start(f32[8,256]{1,0:T(8,128)S(1)} %get-tuple-element.29), channel_id=1, source_target_pairs={{0,15},{1,14},{2,13},{3,12},{4,11},{5,10},{6,9},{7,8},{8,7},{9,6},... | collective-permute-start | bytes 24584 | tf_op jit(solution)/shard_map/ppermute | solution.py:661
  33.7 18.9 %all-to-all-start.1 = ((f32[32,8,128]{2,1,0:T(8,128)}), f32[32,8,128]{2,1,0:T(8,128)S(1)}, u32[]{:S(2)}, u32[]{:S(2)}) async-start(f32[32,8,128]{2,1,0:T(8,128)} %shard_map.114), calls=%async_computation.1 | async-start | bytes 262144 | tf_op jit(solution)/shard_map/all_to_all | solution.py:646
  45.5 0.8 copy-start
  46.3 0.7 copy-start.2
  76.0 14.2 %copy-start.3 = (bf16[2,256,256]{2,1,0:T(8,128)(2,1)S(1)}, bf16[2,256,256]{2,1,0:T(8,128)(2,1)}, u32[]{:S(2)}) copy-start(bf16[2,256,256]{2,1,0:T(8,128)(2,1)} %copy-done.2) | copy-start | bytes 786436
  107.2 18.1 %copy-start.1 = (bf16[256,1024]{1,0:T(8,128)(2,1)S(1)}, bf16[256,1024]{1,0:T(8,128)(2,1)}, u32[]{:S(2)}) copy-start(bf16[256,1024]{1,0:T(8,128)(2,1)} %copy-done) | copy-start | bytes 1572868

commit v3 on v2

--- a/solution.py
+++ b/solution.py
@@ -154,17 +154,15 @@
     return place(cell, weights, CY + lax.broadcasted_iota(jnp.int32, (8, ATOMS), 0))
 
 
+STEPS = ((0, 0), (1, 0), (-1, 0), (0, 1), (0, -1), (N_ROW // 2, 0))
+
+
 def owners(device):
     row = device // N_COL
     col = device % N_COL
-    return (
-        device,
-        (row + 1) % N_ROW * N_COL + col,
-        (row + N_ROW - 1) % N_ROW * N_COL + col,
-        row * N_COL + (col + 1) % N_COL,
-        row * N_COL + (col + N_COL - 1) % N_COL,
-        (device + DEV // 2) % DEV,
-    )
+    return [
+        (row + N_ROW + dr) % N_ROW * N_COL + (col + N_COL + dc) % N_COL for dr, dc in STEPS
+    ]
 
 
 def member_masks(device, live, sid):
@@ -186,20 +184,34 @@
     return jnp.sum(acc, axis=0, keepdims=True)
 
 
-def fragment_means(device, sums, roll):
+def fragment_means(row_of, roll):
     row = lax.broadcasted_iota(jnp.int32, (8, LANES), 0)
     lane = lax.broadcasted_iota(jnp.int32, (8, LANES), 1)
     means = []
-    for owner in owners(device):
-        around = owners(owner)
+    for owner_row, owner_col in STEPS:
         total = jnp.zeros((1, LANES), f32)
-        for slot, source in enumerate((0, 2, 1, 4, 3, 5)):
-            part = sums(around[source])
-            total = total + (roll(part, LANES - 16 * slot, 1) if slot else part)
+        for slot, (dr, dc) in enumerate(STEPS):
+            step = owner_col - dc
+            if abs(step) == 2:
+                k, start = 1 + step // 2, 96
+            else:
+                k, start = 1 + step, 16 * slot
+            part = row_of(owner_row - dr, k)
+            total = total + (roll(part, LANES - start, 1) if start else part)
         mean = total / roll(total, LANES - 8, 1)
         mean = jnp.where(lane == row, jnp.broadcast_to(mean, (8, LANES)), 0.0)
         means.append(jnp.sum(mean, axis=1, keepdims=True))
     return means
+
+
+def relay_rows(col, sums, roll):
+    row = lax.broadcasted_iota(jnp.int32, (8, LANES), 0)
+    lane = lax.broadcasted_iota(jnp.int32, (8, LANES), 1)
+    near = [sums((col + N_COL + k) % N_COL) for k in (-2, -1, 0, 1, 2)]
+    first = jnp.where(lane < 96, near[1], roll(near[0], 48, 1))
+    last = jnp.where(lane < 96, near[3], roll(near[4], 32, 1))
+    out = jnp.where(row % 4 == 0, first, last)
+    return jnp.where(row % 4 == 1, near[2], out)
 
 
 def neutral_charges(device, live, sid, charges, means):
@@ -222,6 +234,7 @@
 
 def to_messages(wave, roll):
     lanes = lane_iota(CY)
+    here = [(lanes >= NK * g) & (lanes < NK * g + NK) for g in range(GROUPS)]
     out = []
     for c in range(N_COL):
         parts = []
@@ -233,7 +246,7 @@
                 shift = (NK * g - lane) % LANES
                 if shift:
                     piece = roll(piece, shift, 1)
-                acc = jnp.where((lanes >= NK * g) & (lanes < NK * g + NK), piece, acc)
+                acc = jnp.where(here[g], piece, acc)
             parts.append(acc)
         out.append(jnp.concatenate(parts, axis=0))
     return out
@@ -241,6 +254,7 @@
 
 def from_messages(message, roll):
     lanes = lane_iota(CY)
+    here = [(lanes >= NK * g) & (lanes < NK * g + NK) for g in range(GROUPS)]
     out = []
     for g in range(GROUPS):
         wide = [jnp.zeros((CY, LANES), f32) for _ in range(3)]
@@ -252,7 +266,7 @@
                 shift = (lane - NK * g) % LANES
                 if shift:
                     piece = roll(piece, shift, 1)
-                wide[tile] = jnp.where((lanes >= lane) & (lanes < lane + NK), piece, wide[tile])
+                wide[tile] = jnp.where(here[lane // NK], piece, wide[tile])
         out.append(jnp.concatenate(wide, axis=1))
     return jnp.concatenate(out, axis=0)
 
@@ -357,9 +371,9 @@
     return out
 
 
-def x_forward(values, twiddle):
+def x_turn(values, twiddle):
     out = []
-    for k1, (re, im) in enumerate(fft(values, -1.0)):
+    for k1, (re, im) in enumerate(values):
         cos, sin = twiddle(k1)
         out.append(jnp.concatenate([re * cos - im * sin, re * sin + im * cos], axis=1))
     return jnp.concatenate(out, axis=0)
@@ -486,48 +500,27 @@
     return copies
 
 
-def partial_kernel(dev, live, sid_hbm, charges_hbm, influence, out, sid, charges, mirror, edge, sems):
+def partial_kernel(dev, live, sid_hbm, charges_hbm, influence, out, mirror, sid, charges, sems):
     copies = run_copies(
-        [
-            (sid_hbm, sid),
-            (charges_hbm, charges),
-            (influence.at[8:16], mirror),
-            (influence.at[8:16, 0], edge),
-        ],
-        sems,
+        [(sid_hbm, sid), (charges_hbm, charges), (influence.at[8:16], mirror)], sems
     )
     copies[0].wait()
     copies[1].wait()
     row = partial_sums(dev[0], live[0], sid[...], charges[...])
-    out[...] = jnp.broadcast_to(row, (N_COL, 8, LANES))
+    out[...] = jnp.broadcast_to(row, (N_COL, LANES))
     copies[2].wait()
-    copies[3].wait()
 
 
 def relay_kernel(dev, sums, out):
-    col = dev[0] % N_COL
-    row = lax.broadcasted_iota(jnp.int32, (8, LANES), 0)
-    acc = jnp.zeros((8, LANES), f32)
-    for k in range(5):
-        acc = jnp.where(row == k, sums[(col + N_COL + k - 2) % N_COL, 0:1, :], acc)
-    out[...] = jnp.broadcast_to(acc, (N_ROW, 8, LANES))
-
-
-def prefetch_kernel(cells_hbm, fraction_hbm, influence, z_tab, y_tab, mix_tab, turn_tab, *refs):
-    cells, fraction, own, z, y, mix, turn = refs[:7]
-    parts, sems = refs[7:11], refs[11]
-    copies = run_copies(
-        [
-            (cells_hbm, cells),
-            (fraction_hbm, fraction),
-            (influence, own),
-            (z_tab, z),
-            (y_tab, y),
-            (mix_tab, mix),
-            (turn_tab, turn),
-        ],
-        sems,
-    )
+    rows = relay_rows(dev[0] % N_COL, lambda c: sums[pl.ds(c, 1), :], pltpu.roll)
+    for k in range(N_ROW // 2):
+        out[k * 8 : (k + 1) * 8, :] = rows
+
+
+def prefetch_kernel(cells_hbm, fraction_hbm, z_tab, y_tab, *refs):
+    z, y = refs[:2]
+    parts, cells, fraction, sems = refs[2:6], refs[6], refs[7], refs[8]
+    copies = run_copies([(cells_hbm, cells), (fraction_hbm, fraction), (z_tab, z), (y_tab, y)], sems)
     copies[0].wait()
     copies[1].wait()
     for ref, x in zip(parts, z_parts(cells[2:3], fraction[...])):
@@ -544,22 +537,45 @@
     )
 
 
-def spread_kernel(dev, live, sums, sid, charges, cells, fraction, z_high, z_low, table, out, neutral_out):
+def spread_kernel(
+    dev, live, sums, sid_hbm, charges_hbm, cells_hbm, fraction_hbm, influence, z_high, z_low, table,
+    out, neutral_out, edge,
+    sid, charges, cells, fraction, neutral_buf, buf, sems, out_sems,
+):
+    copies = run_copies(
+        [
+            (sid_hbm, sid),
+            (charges_hbm, charges),
+            (cells_hbm, cells),
+            (fraction_hbm, fraction),
+            (influence.at[8:16, 0], edge),
+        ],
+        sems,
+    )
     d = dev[0]
-    col = d % N_COL
-
-    def row_of(s):
-        return sums[s // N_COL, pl.ds((s % N_COL - col + N_COL + 2) % N_COL, 1), :]
-
-    means = fragment_means(d, row_of, pltpu.roll)
+    row = d // N_COL
+
+    def row_of(dr, k):
+        return sums[pl.ds((row + 2 * N_ROW + dr) % N_ROW * 4 + k, 1), :]
+
+    means = fragment_means(row_of, pltpu.roll)
+    for copy in copies[:4]:
+        copy.wait()
     neutral = neutral_charges(d, live[0], sid[...], charges[...], means)
-    neutral_out[...] = neutral
+    neutral_buf[...] = neutral
+    leaving = [pltpu.make_async_copy(neutral_buf, neutral_out, sems.at[5])]
+    leaving[0].start()
     x, y, _ = local_cells(d, cells[...])
     messages = spread_to_z(
         neutral, x, y, fraction[...], z_high[...], z_low[...], table, pltpu.roll
     )
     for c, message in enumerate(messages):
-        out[c] = message
+        buf[c] = message
+        leaving.append(pltpu.make_async_copy(buf.at[c], out.at[c], out_sems.at[c]))
+        leaving[-1].start()
+    copies[4].wait()
+    for copy in leaving:
+        copy.wait()
 
 
 def slant(x, shift):
@@ -590,7 +606,9 @@
         out[c, CY:] = im
 
 
-def gain_kernel(dev, own, mirror, edge, out):
+def gain_kernel(dev, own_hbm, mirror_hbm, edge_hbm, out, own, mirror, edge, sems):
+    for copy in run_copies([(own_hbm, own), (mirror_hbm, mirror), (edge_hbm, edge)], sems):
+        copy.wait()
     flat = own[...].reshape(128, N)
     pieces = gain_table(dev[0], flat, mirror[...].reshape(64, N), edge[...], pltpu.roll)
     for k1, piece in enumerate(pieces):
@@ -598,19 +616,32 @@
         out[k1 * 8 : (k1 + 1) * 8, LANES:] = piece
 
 
-def x_kernel(x, gain, twiddle, mix, out):
+def x_kernel(x, gain, twiddle_hbm, mix_hbm, out, twiddle, mix, sems):
+    copies = run_copies([(twiddle_hbm, twiddle), (mix_hbm, mix)], sems)
+
     def factor(k1):
         return twiddle[k1, 0:1, :], twiddle[k1, 1:2, :]
 
-    values = [(x[r, :, :LANES], x[r, :, LANES:]) for r in range(N_ROW)]
-    wave = x_mix(x_forward(values, factor), gain[...], mix)
+    values = fft([(x[r, :, :LANES], x[r, :, LANES:]) for r in range(N_ROW)], -1.0)
+    for copy in copies:
+        copy.wait()
+    wave = x_mix(x_turn(values, factor), gain[...], mix)
     for r, (re, im) in enumerate(x_back(wave, factor)):
         out[r, :, :LANES] = re
         out[r, :, LANES:] = im
 
 
-def atom_kernel(dev, message, neutral, cells, fraction, zh, zl, vh, vl, table, force, energy):
+def atom_kernel(
+    dev, message, neutral_hbm, cells_hbm, fraction_hbm, zh, zl, vh, vl, table,
+    force, energy,
+    neutral, cells, fraction, sems,
+):
+    copies = run_copies(
+        [(neutral_hbm, neutral), (cells_hbm, cells), (fraction_hbm, fraction)], sems
+    )
     wave = from_messages(lambda c: message[c], pltpu.roll)
+    for copy in copies:
+        copy.wait()
     x, y, _ = local_cells(dev[0], cells[...])
     e, g = interpolate(
         wave, neutral[...], x, y, fraction[...], (zh[...], zl[...]), (vh[...], vl[...]), table
@@ -620,26 +651,30 @@
         force[d : d + 1, :] = g[d]
 
 
+KINDS = {"s": pltpu.SMEM, "v": pltpu.VMEM, "h": pltpu.HBM}
+
+
 def call(kernel, outs, spaces, args, scratch=()):
-    kinds = {
-        "s": pl.BlockSpec(memory_space=pltpu.SMEM),
-        "v": pl.BlockSpec(memory_space=pltpu.VMEM),
-        "h": pl.BlockSpec(memory_space=pltpu.HBM),
-    }
-    shapes = [jax.ShapeDtypeStruct(o[0], o[1]) if isinstance(o[0], tuple) else jax.ShapeDtypeStruct(o, f32) for o in outs]
-    many = len(shapes) > 1
     args = [
         pltpu.with_memory_space_constraint(x, pltpu.HBM) if k == "h" else x
         for k, x in zip(spaces, args)
     ]
-    return pl.pallas_call(
+    result = pl.pallas_call(
         kernel,
-        out_shape=shapes if many else shapes[0],
-        in_specs=[kinds[k] for k in spaces],
-        out_specs=[kinds["v"]] * len(shapes) if many else kinds["v"],
+        out_shape=[
+            pltpu.HBM(shape, dtype) if k == "h" else jax.ShapeDtypeStruct(shape, dtype)
+            for k, shape, dtype in outs
+        ],
+        in_specs=[pl.BlockSpec(memory_space=KINDS[k]) for k in spaces],
+        out_specs=[pl.BlockSpec(memory_space=KINDS[k]) for k, _, _ in outs],
         scratch_shapes=list(scratch),
         compiler_params=pltpu.CompilerParams(vmem_limit_bytes=16 << 20),
     )(*args)
+    return result if len(outs) > 1 else result[0]
+
+
+def sems(count):
+    return pltpu.SemaphoreType.DMA((count,))
 
 
 def swap(x, axis):
@@ -650,64 +685,85 @@
     dev = lax.axis_index(ALL).astype(jnp.int32).reshape(1)
     charges = charges.reshape(1, ATOMS)
     sid = structure_id.reshape(1, ATOMS)
-    sums, sid, charges, mirror, edge = call(
+    sid_buf = pltpu.VMEM((1, ATOMS), jnp.int32)
+    row_buf = pltpu.VMEM((1, ATOMS), f32)
+    cell_buf = pltpu.VMEM((3, ATOMS), jnp.int32)
+    fraction_buf = pltpu.VMEM((3, ATOMS), f32)
+    sums, mirror = call(
         partial_kernel,
-        [(N_COL, 8, LANES), ((1, ATOMS), jnp.int32), (1, ATOMS), (8, 8, N), (8, N)],
+        [("v", (N_COL, LANES), f32), ("h", (8, 8, N), f32)],
         "sshhh",
         (dev, live_count, sid, charges, influence),
-        [pltpu.SemaphoreType.DMA((4,))],
-    )
+        [sid_buf, row_buf, sems(3)],
+    )
+    sums = swap(sums.reshape(N_COL, 1, LANES), COL).reshape(N_COL, LANES)
+    sums = call(relay_kernel, [("v", (4 * N_ROW, LANES), f32)], "sv", (dev, sums))
+    sums, mirror = lax.optimization_barrier((sums, mirror))
     mirror = lax.ppermute(mirror, ALL, [(i, DEV - 1 - i) for i in range(DEV)])
+    sums = swap(sums.reshape(N_ROW, 4, LANES), ROW).reshape(4 * N_ROW, LANES)
+    twiddle, mix = x_tables()
+    z_tab, y_tab, zh, zl, vh, vl = call(
+        prefetch_kernel,
+        [("v", (2, N, 3 * LANES), bf16), ("v", (4 * N, 2 * N), bf16)]
+        + [("v", (N, ATOMS), bf16)] * 4,
+        "hhhh",
+        (cells, fraction, z_table(), y_table()),
+        [cell_buf, fraction_buf, sems(4)],
+    )
+    sums, mirror, zh = lax.optimization_barrier((sums, mirror, zh))
+    messages, neutral, edge = call(
+        spread_kernel,
+        [("h", (N_COL, ROWS, LANES), f32), ("h", (1, ATOMS), f32), ("h", (8, N), f32)],
+        "ssvhhhhhvvv",
+        (
+            dev, live_count, sums, sid, charges, cells, fraction, influence,
+            zh, zl, z_tab,
+        ),
+        [
+            sid_buf, row_buf, cell_buf, fraction_buf, row_buf,
+            pltpu.VMEM((N_COL, ROWS, LANES), f32), sems(6), sems(N_COL),
+        ],
+    )
     edge = lax.ppermute(
         edge,
         ALL,
         [(i, (N_ROW - i // N_COL) % N_ROW * N_COL + N_COL - 1 - i % N_COL) for i in range(DEV)],
     )
-    sums = swap(sums, COL)
-    sums, mirror, edge = lax.optimization_barrier((sums, mirror, edge))
-    sums = call(relay_kernel, [(N_ROW, 8, LANES)], "sv", (dev, sums))
-    sums = swap(sums, ROW)
-    twiddle, mix = x_tables()
-    half = ((N, ATOMS), bf16)
-    cells, fraction, own, z_tab, y_tab, mix, twiddle, zh, zl, vh, vl = call(
-        prefetch_kernel,
+    columns = swap(messages, COL)
+    gain = call(
+        gain_kernel,
+        [("v", (N, 2 * LANES), f32)],
+        "shhh",
+        (dev, influence, mirror, edge),
         [
-            ((3, ATOMS), jnp.int32),
-            (3, ATOMS),
-            (16, 8, N),
-            ((2, N, 3 * LANES), bf16),
-            ((4 * N, 2 * N), bf16),
-            ((2, 2 * LANES, 2 * LANES), bf16),
-            (N_ROW, 2, LANES),
-            half,
-            half,
-            half,
-            half,
+            pltpu.VMEM((16, 8, N), f32), pltpu.VMEM((8, 8, N), f32), pltpu.VMEM((8, N), f32),
+            sems(3),
         ],
-        "hhhhhhh",
-        (cells, fraction, influence, z_table(), y_table(), mix, twiddle),
-        [pltpu.SemaphoreType.DMA((7,))],
-    )
-    gain = call(gain_kernel, [(N, 2 * LANES)], "svvv", (dev, own, mirror, edge))
-    zh, gain = lax.optimization_barrier((zh, gain))
-    messages, neutral = call(
-        spread_kernel,
-        [(N_COL, ROWS, LANES), (1, ATOMS)],
-        "ssvvvvvvvv",
-        (dev, live_count, sums, sid, charges, cells, fraction, zh, zl, z_tab),
-    )
-    columns = swap(messages, COL)
-    rows = call(y_forward_kernel, [(N_ROW, 8, 2 * LANES)], "vv", (columns, y_tab))
+    )
+    columns, gain = lax.optimization_barrier((columns, gain))
+    strip = [("v", (N_ROW, 8, 2 * LANES), f32)]
+    rows = call(y_forward_kernel, strip, "vv", (columns, y_tab))
     rows = swap(rows, ROW)
-    rows = call(x_kernel, [(N_ROW, 8, 2 * LANES)], "vvvv", (rows, gain, twiddle, mix))
+    rows = call(
+        x_kernel,
+        strip,
+        "vvhh",
+        (rows, gain, twiddle, mix),
+        [
+            pltpu.VMEM((N_ROW, 2, LANES), f32),
+            pltpu.VMEM((2, 2 * LANES, 2 * LANES), bf16),
+            sems(2),
+        ],
+    )
     rows = swap(rows, ROW)
-    columns = call(y_back_kernel, [(N_COL, ROWS, LANES)], "vv", (rows, y_tab))
+    columns = call(y_back_kernel, [("v", (N_COL, ROWS, LANES), f32)], "vv", (rows, y_tab))
     columns = swap(columns, COL)
     forces, energy = call(
         atom_kernel,
-        [(3, ATOMS), (1, ATOMS)],
-        "svvvvvvvvv",
+        [("v", (3, ATOMS), f32), ("v", (1, ATOMS), f32)],
+        "svhhhvvvvv",
         (dev, columns, neutral, cells, fraction, zh, zl, vh, vl, z_tab),
+        [row_buf, cell_buf, fraction_buf, sems(3)],
     )
     return forces, energy.reshape(ATOMS)
 

time: 129 us -> 136 us (1.054)
  blocking collectives: 67.8 us -> 77.3 us
  starting transfers between devices: 35.8 us -> 28.9 us
  Pallas kernels: 12.7 us -> 18.9 us
    all_to_all x4, blocking collectives: 67.8 us -> 77.3 us  [swap(): return lax.all_to_all(x, axis, split_axis=0, concat_axis=0, tiled=True)]
    ppermute x1, starting transfers between devices: 13.9 us -> 7.57 us  [body(): mirror = lax.ppermute(mirror, ALL, [(i, DEV - 1 - i) for i in range(DEV)])]
    pallas_call x9, Pallas kernels: 12.7 us -> 18.9 us  [call(): pl.pallas_call(kernel, out_shape=[pltpu.HBM(shape, dtype) if k == 'h' els...]
    all_to_all x2, waiting for transfers between devices: 4.72 us -> 0.51 us  [swap(): return lax.all_to_all(x, axis, split_axis=0, concat_axis=0, tiled=True)]
    ppermute x1, waiting for transfers between devices: 0.01 us -> 3.9 us  [body(): mirror = lax.ppermute(mirror, ALL, [(i, DEV - 1 - i) for i in range(DEV)])]
    all_to_all x2, starting transfers between devices: 19.9 us -> 16.5 us  [swap(): return lax.all_to_all(x, axis, split_axis=0, concat_axis=0, tiled=True)]
    ppermute x1, starting transfers between devices: 2.05 us -> 4.84 us  [body(): lax.ppermute(edge, ALL, [(i, (N_ROW - i // N_COL) % N_ROW * N_COL + N_COL...]
  transfers between devices with their start and end apart: 4 -> 4, of which waited for: 2 -> 3; matrix products, arithmetic and copies ran while one was open for 0% -> 0% of each run, Pallas kernels for 2% -> 3%
where the time goes in v3:
time: 136 us
  blocking collectives  77.3 us (57%)
  starting transfers between devices  28.9 us (21%)
  Pallas kernels  18.9 us (14%)
  waiting for transfers between devices  8.47 us (6%)
  between operations  1.39 us (1%)
    all_to_all x4, blocking collectives, swap(): return lax.all_to_all(x, axis, split_axis=0, concat_axis=0, tiled=True)  77.3 us
    pallas_call x9, Pallas kernels, call(): pl.pallas_call(kernel, out_shape=[pltpu.HBM(shape, dtype) if k == 'h' els...  18.9 us
    all_to_all x2, starting transfers between devices, swap(): return lax.all_to_all(x, axis, split_axis=0, concat_axis=0, tiled=True)  16.5 us
    ppermute x1, starting transfers between devices, body(): mirror = lax.ppermute(mirror, ALL, [(i, DEV - 1 - i) for i in range(DEV)])  7.57 us
    ppermute x1, starting transfers between devices, body(): lax.ppermute(edge, ALL, [(i, (N_ROW - i // N_COL) % N_ROW * N_COL + N_COL...  4.84 us
    ppermute x1, waiting for transfers between devices, body(): lax.ppermute(edge, ALL, [(i, (N_ROW - i // N_COL) % N_ROW * N_COL + N_COL...  4.06 us
    ppermute x1, waiting for transfers between devices, body(): mirror = lax.ppermute(mirror, ALL, [(i, DEV - 1 - i) for i in range(DEV)])  3.9 us
  transfers between devices with their start and end apart: 4, of which 3 were waited for; matrix products, arithmetic and copies ran while one was open for 0% of the time, Pallas kernels for 3%

profile of v3, /device:TPU:1, one launch (start us, length us, event | category | flops | bytes accessed | tf_op | source)
XLA Modules:
  0.0 135.6 jit_solution(5648275512246588173)
XLA Ops:
  1.3 3.1 %shard_map.113 = (f32[16,128]{1,0:T(8,128)S(1)}, f32[8,8,256]{2,1,0:T(8,128)}) custom-call(s32[1]{0:T(128)} %bitcast.dev, s32[1]{0:T(128)S(6)} %copy.13.live, s32[1,1024]{1,0:T(1,128)} %bitcast.12, f32[1,1024]{1,0:T(1,128)} %bitcast.14, f32[16,8,256]{2,1,0:T(8,128)} %own_hbm.1), custom_call_target="tpu_custom_call" | custom-call | tf_op jit(solution)/shard_map/pallas_call | solution.py:662
  4.4 16.3 %all_to_all.30 = f32[16,1,128]{2,1,0:T(1,128)S(1)} all-to-all(f32[16,1,128]{2,1,0:T(1,128)S(1)} %bitcast.11), channel_id=1, replica_groups=mesh['row_0'=4,'row_1'=8,'col_0'=8,'col_1'=2] {'col_0','col_1'}, dimensions={0} | all-to-all | bytes 16384 | tf_op jit(solution)/shard_map/all_to_all | solution.py:681
  20.7 0.7 shard_map.114
  21.4 12.1 %all-to-all-start.1 = ((f32[32,4,128]{2,1,0:T(4,128)}), f32[32,4,128]{2,1,0:T(4,128)}, u32[]{:S(2)}, u32[]{:S(2)}) async-start(f32[32,4,128]{2,1,0:T(4,128)} %bitcast.6), calls=%async_computation.1 | async-start | bytes 131072 | tf_op jit(solution)/shard_map/all_to_all | solution.py:681
  33.6 7.6 %collective-permute-start = (f32[8,8,256]{2,1,0:T(8,128)}, f32[8,8,256]{2,1,0:T(8,128)}, u32[]{:S(2)}, u32[]{:S(2)}) collective-permute-start(f32[8,8,256]{2,1,0:T(8,128)} %get-tuple-element.25), channel_id=1, source_target_pairs={{0,511},{1,510},{2,509},{3,508},{4,507},{5,506},{6,505},{7,504},{8... | collective-permute-start | bytes 196616 | tf_op jit(solution)/shard_map/ppermute | solution.py:702
  41.1 2.0 %shard_map.115 = (bf16[2,256,384]{2,1,0:T(8,128)(2,1)S(1)}, bf16[1024,512]{1,0:T(8,128)(2,1)S(1)}, bf16[256,1024]{1,0:T(8,128)(2,1)S(1)}, bf16[256,1024]{1,0:T(8...) custom-call(s32[3,1024]{1,0:T(4,128)} %cells_hbm.5, f32[3,1024]{1,0:T(4,128)} %fraction_hbm.5, ...), custom_call_target="tpu_custom_call" | custom-call | tf_op jit(solution)/shard_map/pallas_call | solution.py:662
  43.1 0.0 copy-start
  43.1 3.9 %collective-permute-done.mirror_hbm = f32[8,8,256]{2,1,0:T(8,128)} collective-permute-done((f32[8,8,256]{2,1,0:T(8,128)}, f32[8,8,256]{2,1,0:T(8,128)}, u32[]{:S(2)}, u32[]{:S(2)}) %collective-permute-start) | collective-permute-done | bytes 65568 | tf_op jit(solution)/shard_map/ppermute | solution.py:702
  47.0 0.0 all-to-all-done.1
  47.0 4.6 %shard_map.116 = (f32[16,32,128]{2,1,0:T(8,128)}, f32[1,1024]{1,0:T(1,128)}, f32[8,256]{1,0:T(8,128)}) custom-call(s32[1]{0:T(128)} %bitcast.dev, s32[1]{0:T(128)S(6)} %copy.13.live, f32[128,128]{1,0:T(8,128)} %bitcast.7.sums, s32[1,1024]{1,0:T(1,128)} %bitcast.13, f32[1,1024]{1,0:T(1,128)} %bitcast.15, s32[3,1024]{1,0:T(4,128)} %cells_hbm.5, ...), custom_call_target="tpu_custom_call" | custom-call | tf_op jit(solution)/shard_map/pallas_call | solution.py:662
  51.6 0.0 copy-done
  51.6 0.0 copy-start.3
  51.6 4.3 %all-to-all-start.2 = ((f32[16,32,128]{2,1,0:T(8,128)}), f32[16,32,128]{2,1,0:T(8,128)S(1)}, u32[]{:S(2)}, u32[]{:S(2)}) async-start(f32[16,32,128]{2,1,0:T(8,128)} %get-tuple-element.31), calls=%async_computation.2 | async-start | bytes 524288 | tf_op jit(solution)/shard_map/all_to_all | solution.py:681
  56.0 0.0 copy-done.3
  56.0 4.8 %collective-permute-start.1 = (f32[8,256]{1,0:T(8,128)S(1)}, f32[8,256]{1,0:T(8,128)S(1)}, u32[]{:S(2)}, u32[]{:S(2)}) collective-permute-start(f32[8,256]{1,0:T(8,128)S(1)} %copy-done.3), channel_id=1, source_target_pairs={{0,15},{1,14},{2,13},{3,12},{4,11},{5,10},{6,9},{7,8},{8,7},{9,6},... | collective-permute-start | bytes 24584 | tf_op jit(solution)/shard_map/ppermute | solution.py:727
  60.8 4.1 %collective-permute-done.1.edge_hbm = f32[8,256]{1,0:T(8,128)S(1)} collective-permute-done((f32[8,256]{1,0:T(8,128)S(1)}, f32[8,256]{1,0:T(8,128)S(1)}, u32[]{:S(2)}, u32[]{:S(2)}) %collective-permute-start.1) | collective-permute-done | bytes 8224 | tf_op jit(solution)/shard_map/ppermute | solution.py:727
  64.9 0.0 copy-start.2
  64.9 0.6 copy-done.2
  65.5 1.8 %shard_map.117.gain = f32[256,256]{1,0:T(8,128)S(1)} custom-call(s32[1]{0:T(128)} %bitcast.dev, f32[16,8,256]{2,1,0:T(8,128)} %own_hbm.1, f32[8,8,256]{2,1,0:T(8,128)} %collective-permute-done.mirror_hbm, f32[8,256]{1,0:T(8,128)} %copy-done.2), custom_call_target="tpu_custom_call" | custom-call | tf_op jit(solution)/shard_map/pallas_call | solution.py:662
  67.3 0.5 all-to-all-done.2.x
  67.8 0.7 shard_map.118
  68.6 22.1 %all_to_all.31.x = f32[32,8,256]{2,1,0:T(8,128)S(1)} all-to-all(f32[32,8,256]{2,1,0:T(8,128)S(1)} %shard_map.118), channel_id=1, replica_groups=mesh['row_0'=4,'row_1'=8,'col_0'=8,'col_1'=2] {'row_0','row_1'}, dimensions={0} | all-to-all | bytes 524288 | tf_op jit(solution)/shard_map/all_to_all | solution.py:681
  90.7 1.6 %shard_map.119 = f32[32,8,256]{2,1,0:T(8,128)S(1)} custom-call(f32[32,8,256]{2,1,0:T(8,128)S(1)} %all_to_all.31.x, f32[256,256]{1,0:T(8,128)S(1)} %shard_map.117.gain, f32[32,2,128]{2,1,0:T(2,128)} %constant.33.clone.twiddle_hbm, bf16[2,256,256]{2,1,0:T(8,128)(2,1)} %constant.34.clone.mix_hbm), custom_call_target="tpu_custom_call" | custom-call | tf_op jit(solution)/shard_map/pallas_call | solution.py:662
  92.4 16.0 %all_to_all.32.x = f32[32,8,256]{2,1,0:T(8,128)S(1)} all-to-all(f32[32,8,256]{2,1,0:T(8,128)S(1)} %shard_map.119), channel_id=1, replica_groups=mesh['row_0'=4,'row_1'=8,'col_0'=8,'col_1'=2] {'row_0','row_1'}, dimensions={0} | all-to-all | bytes 524288 | tf_op jit(solution)/shard_map/all_to_all | solution.py:681
  108.3 0.7 shard_map.120
  109.0 0.0 copy-start.1
  109.0 22.9 %all_to_all.33.message = f32[16,32,128]{2,1,0:T(8,128)S(1)} all-to-all(f32[16,32,128]{2,1,0:T(8,128)S(1)} %shard_map.120), channel_id=1, replica_groups=mesh['row_0'=4,'row_1'=8,'col_0'=8,'col_1'=2] {'col_0','col_1'}, dimensions={0} | all-to-all | bytes 524288 | tf_op jit(solution)/shard_map/all_to_all | solution.py:681
  131.9 0.0 copy-done.1
  131.9 3.7 %shard_map.121 = (f32[3,1024]{1,0:T(4,128)}, f32[1,1024]{1,0:T(1,128)}) custom-call(s32[1]{0:T(128)} %bitcast.dev, f32[16,32,128]{2,1,0:T(8,128)S(1)} %all_to_all.33.message, f32[1,1024]{1,0:T(1,128)} %get-tuple-element.37.neutral_hbm, s32[3,1024]{1,0:T(4,128)} %cells_hbm.5, f32[3,1024]{1,0:T(4,128)} %fraction_hbm.5, ...), custom_call_target="tpu_custom_call" | custom-call | tf_op jit(solution)/shard_map/pallas_call | solution.py:662
Async XLA Ops:
  21.4 25.6 %all-to-all-start.1 = ((f32[32,4,128]{2,1,0:T(4,128)}), f32[32,4,128]{2,1,0:T(4,128)}, u32[]{:S(2)}, u32[]{:S(2)}) async-start(f32[32,4,128]{2,1,0:T(4,128)} %bitcast.6), calls=%async_computation.1 | async-start | bytes 131072 | tf_op jit(solution)/shard_map/all_to_all | solution.py:681
  33.6 13.5 %collective-permute-start = (f32[8,8,256]{2,1,0:T(8,128)}, f32[8,8,256]{2,1,0:T(8,128)}, u32[]{:S(2)}, u32[]{:S(2)}) collective-permute-start(f32[8,8,256]{2,1,0:T(8,128)} %get-tuple-element.25), channel_id=1, source_target_pairs={{0,511},{1,510},{2,509},{3,508},{4,507},{5,506},{6,505},{7,504},{8... | collective-permute-start | bytes 196616 | tf_op jit(solution)/shard_map/ppermute | solution.py:702
  43.1 8.5 %copy-start = (bf16[256,1024]{1,0:T(8,128)(2,1)}, bf16[256,1024]{1,0:T(8,128)(2,1)S(1)}, u32[]{:S(2)}) copy-start(bf16[256,1024]{1,0:T(8,128)(2,1)S(1)} %get-tuple-element.39.vl) | copy-start | bytes 1572868
  51.6 4.4 %copy-start.3 = (f32[8,256]{1,0:T(8,128)S(1)}, f32[8,256]{1,0:T(8,128)}, u32[]{:S(2)}) copy-start(f32[8,256]{1,0:T(8,128)} %get-tuple-element.33) | copy-start | bytes 24580
  51.6 16.2 %all-to-all-start.2 = ((f32[16,32,128]{2,1,0:T(8,128)}), f32[16,32,128]{2,1,0:T(8,128)S(1)}, u32[]{:S(2)}, u32[]{:S(2)}) async-start(f32[16,32,128]{2,1,0:T(8,128)} %get-tuple-element.31), calls=%async_computation.2 | async-start | bytes 524288 | tf_op jit(solution)/shard_map/all_to_all | solution.py:681
  56.0 8.9 %collective-permute-start.1 = (f32[8,256]{1,0:T(8,128)S(1)}, f32[8,256]{1,0:T(8,128)S(1)}, u32[]{:S(2)}, u32[]{:S(2)}) collective-permute-start(f32[8,256]{1,0:T(8,128)S(1)} %copy-done.3), channel_id=1, source_target_pairs={{0,15},{1,14},{2,13},{3,12},{4,11},{5,10},{6,9},{7,8},{8,7},{9,6},... | collective-permute-start | bytes 24584 | tf_op jit(solution)/shard_map/ppermute | solution.py:727
  64.9 0.6 copy-start.2
  109.0 22.9 %copy-start.1 = (bf16[256,1024]{1,0:T(8,128)(2,1)S(1)}, bf16[256,1024]{1,0:T(8,128)(2,1)}, u32[]{:S(2)}) copy-start(bf16[256,1024]{1,0:T(8,128)(2,1)} %copy-done) | copy-start | bytes 1572868

commit v4 on v3

--- a/solution.py
+++ b/solution.py
@@ -214,13 +214,41 @@
     return jnp.where(row % 4 == 1, near[2], out)
 
 
-def neutral_charges(device, live, sid, charges, means):
+SPREAD_ROWS = 16 + 16 + 8 + 8 + 48
+ATOM_ROWS = 16 * 6 + 8 * 2
+
+
+def atom_weights(cell_x, cell_y, fraction):
+    number = lax.broadcasted_iota(jnp.int32, (16, ATOMS), 0)
+    weights = spline_values(fraction)
+    slopes = spline_slopes(fraction)
+    wx, vx = [w[0:1] for w in weights], [w[0:1] for w in slopes]
+    wy, vy = [w[1:2] for w in weights], [w[1:2] for w in slopes]
+    return [
+        place(cell_x, wx, number),
+        place(cell_x, vx, number),
+        place(cell_x, wx, 15 - number),
+        place(cell_x, vx, 15 - number),
+        place(cell_y, wy, number),
+        place(cell_y, vy, number),
+        y_halo_rows(cell_y, wy),
+        y_halo_rows(cell_y, vy),
+    ]
+
+
+def spread_rows(device, live, sid, charges, weights):
+    alive = lax.broadcasted_iota(jnp.int32, (8, ATOMS), 1) < live
+    row = lax.broadcasted_iota(jnp.int32, (8, ATOMS), 0)
+    basis = jnp.where(alive, jnp.where(row == 0, charges, 1.0), 0.0)
+    masks = [jnp.where(m, 1.0, 0.0) for m in member_masks(device, live, sid)]
+    return [weights[0], weights[4], weights[6], basis] + masks
+
+
+def neutral_charges(pack, means):
     acc = jnp.zeros((8, ATOMS), f32)
-    for mask, mean in zip(member_masks(device, live, sid), means):
-        acc = acc + jnp.where(mask, mean, 0.0)
-    mean = jnp.sum(acc, axis=0, keepdims=True)
-    lane = lax.broadcasted_iota(jnp.int32, (1, ATOMS), 1)
-    return jnp.where(lane < live, charges - mean, 0.0)
+    for slot, mean in enumerate(means):
+        acc = acc + pack[48 + 8 * slot : 56 + 8 * slot] * mean
+    return pack[40:41] - jnp.sum(acc, axis=0, keepdims=True)
 
 
 def lane_iota(rows):
@@ -315,13 +343,10 @@
     return out
 
 
-def spread_to_z(neutral, cell_x, cell_y, fraction, z_high, z_low, table, roll):
-    weights = spline_values(fraction)
-    wx = [w[0:1] * neutral for w in weights]
-    wy = [w[1:2] for w in weights]
-    x_rows = place(cell_x, wx, lax.broadcasted_iota(jnp.int32, (16, ATOMS), 0))
-    y_rows = place(cell_y, wy, lax.broadcasted_iota(jnp.int32, (16, ATOMS), 0))
-    y_edge = y_halo_rows(cell_y, wy)
+def spread_to_z(neutral, pack, z_high, z_low, table, roll):
+    x_rows = pack[0:16] * neutral
+    y_rows = pack[16:32]
+    y_edge = pack[32:40]
     plane = jnp.concatenate(
         [y_rows * x_rows[x : x + 1] for x in range(XI)]
         + [x_rows * y_edge[h : h + 1] for h in (2, 1, 0)],
@@ -332,13 +357,6 @@
     grid_high, grid_low = split(grid)
     wave = dot(grid_high, table[0]) + (dot(grid_low, table[0]) + dot(grid_high, table[1]))
     return to_messages(wave, roll)
-
-
-def z_parts(cell_z, fraction):
-    z = fraction[2:3]
-    return split(place_periodic(cell_z, spline_values(z))) + split(
-        place_periodic(cell_z, spline_slopes(z))
-    )
 
 
 def y_stage(x, table):
@@ -401,14 +419,13 @@
     col = device % N_COL
     r = lax.broadcasted_iota(jnp.int32, (72, 128), 0)
     k = lax.broadcasted_iota(jnp.int32, (72, 128), 1)
-    take_own = (k == r).astype(bf16)
+    take_own = ((r % 8 < 7) & (k == r + 1)).astype(bf16)
     r = lax.broadcasted_iota(jnp.int32, (72, 64), 0)
     k = lax.broadcasted_iota(jnp.int32, (72, 64), 1)
-    slot, i = r // 8, r % 8
-    take_mirror = ((slot > 0) & (i > 0) & (k == (8 - slot) * 8 + 8 - i)).astype(bf16)
-    r = lax.broadcasted_iota(jnp.int32, (72, 8), 0)
-    k = lax.broadcasted_iota(jnp.int32, (72, 8), 1)
-    take_edge = ((r // 8 > 0) & (r % 8 == 0) & (k == 8 - r // 8)).astype(bf16)
+    take_mirror = ((r >= 8) & (k == (8 - r // 8) * 8 + 7 - r % 8)).astype(bf16)
+    r = lax.broadcasted_iota(jnp.int32, (72, NK), 0)
+    k = lax.broadcasted_iota(jnp.int32, (72, NK), 1)
+    take_edge = ((r % 8 == 7) & (k == r // 8)).astype(bf16)
     kx = lax.broadcasted_iota(jnp.int32, (N, N), 0)
     lane = lax.broadcasted_iota(jnp.int32, (N, N), 1)
     wave = lane // 8 + 32 * (lane % 8)
@@ -422,7 +439,7 @@
         return dot(high, permutation) + dot(low, permutation)
 
     gain = ordered(own, take_own, order)
-    gain = gain + ordered(mirror, take_mirror, reverse) + ordered(edge, take_edge, reverse)
+    gain = gain + ordered(mirror, take_mirror, reverse) + ordered(edge, take_edge, order)
     row = lax.broadcasted_iota(jnp.int32, (72, N), 0)
     gain = jnp.where((row >= 64) & (col >= 8), 0.0, gain) * (1.0 / (N * N * N))
     lanes = lane_iota(8)
@@ -440,18 +457,11 @@
     return out
 
 
-def interpolate(wave, neutral, cell_x, cell_y, fraction, z_rows, z_slopes, table):
-    weights = spline_values(fraction)
-    slopes = spline_slopes(fraction)
-    number = lax.broadcasted_iota(jnp.int32, (16, ATOMS), 0)
-    x_rows = place(cell_x, [w[0:1] for w in weights], number)
-    x_slopes = place(cell_x, [w[0:1] for w in slopes], number)
-    wy = [w[1:2] for w in weights]
-    vy = [w[1:2] for w in slopes]
-    y_rows, y_slopes = place(cell_y, wy, number), place(cell_y, vy, number)
-    x_back = place(cell_x, [w[0:1] for w in weights], 15 - number)
-    x_back_slopes = place(cell_x, [w[0:1] for w in slopes], 15 - number)
-    y_edge, y_edge_slopes = y_halo_rows(cell_y, wy), y_halo_rows(cell_y, vy)
+def interpolate(wave, neutral, pack, z_rows, z_slopes, table):
+    x_rows, x_slopes, x_back, x_back_slopes, y_rows, y_slopes = [
+        pack[16 * k : 16 * (k + 1)] for k in range(6)
+    ]
+    y_edge, y_edge_slopes = pack[96:104], pack[104:112]
     high, low = split(wave)
     grid = dot(high, table[0], NT) + (dot(low, table[0], NT) + dot(high, table[1], NT))
     grid_high, grid_low = split(grid)
@@ -500,15 +510,24 @@
     return copies
 
 
-def partial_kernel(dev, live, sid_hbm, charges_hbm, influence, out, mirror, sid, charges, sems):
+def partial_kernel(
+    dev, live, sid_hbm, charges_hbm, influence, out, mirror, edge, sid, charges, sems
+):
     copies = run_copies(
-        [(sid_hbm, sid), (charges_hbm, charges), (influence.at[8:16], mirror)], sems
+        [
+            (sid_hbm, sid),
+            (charges_hbm, charges),
+            (influence.at[8:16], mirror),
+            (influence.at[0:NK, 0], edge),
+        ],
+        sems,
     )
     copies[0].wait()
     copies[1].wait()
     row = partial_sums(dev[0], live[0], sid[...], charges[...])
     out[...] = jnp.broadcast_to(row, (N_COL, LANES))
     copies[2].wait()
+    copies[3].wait()
 
 
 def relay_kernel(dev, sums, out):
@@ -517,15 +536,44 @@
         out[k * 8 : (k + 1) * 8, :] = rows
 
 
-def prefetch_kernel(cells_hbm, fraction_hbm, z_tab, y_tab, *refs):
-    z, y = refs[:2]
-    parts, cells, fraction, sems = refs[2:6], refs[6], refs[7], refs[8]
-    copies = run_copies([(cells_hbm, cells), (fraction_hbm, fraction), (z_tab, z), (y_tab, y)], sems)
-    copies[0].wait()
-    copies[1].wait()
-    for ref, x in zip(parts, z_parts(cells[2:3], fraction[...])):
-        ref[...] = x
-    for copy in copies[2:]:
+def prefetch_kernel(
+    dev, live, cells_hbm, fraction_hbm, sid_hbm, charges_hbm, own_hbm, z_tab, y_tab, turn_tab,
+    own, z, y, turn, spread_pack, zh, zl, atom_pack_hbm, vh_hbm, vl_hbm,
+    cells, fraction, sid, charges, atom_pack, vh, vl, sems,
+):
+    copies = run_copies(
+        [
+            (cells_hbm, cells),
+            (fraction_hbm, fraction),
+            (sid_hbm, sid),
+            (charges_hbm, charges),
+            (own_hbm, own),
+            (z_tab, z),
+            (y_tab, y),
+            (turn_tab, turn),
+        ],
+        sems,
+    )
+    for copy in copies[:4]:
+        copy.wait()
+    z_cell = cells[2:3]
+    vh[...], vl[...] = split(place_periodic(z_cell, spline_slopes(fraction[2:3])))
+    x, y_cell, _ = local_cells(dev[0], cells[...])
+    weights = atom_weights(x, y_cell, fraction[...])
+    start = 0
+    for rows in weights:
+        atom_pack[start : start + rows.shape[0], :] = rows
+        start += rows.shape[0]
+    pairs = [(atom_pack, atom_pack_hbm), (vh, vh_hbm), (vl, vl_hbm)]
+    leaving = [pltpu.make_async_copy(a, b, sems.at[8 + i]) for i, (a, b) in enumerate(pairs)]
+    for copy in leaving:
+        copy.start()
+    start = 0
+    for rows in spread_rows(dev[0], live[0], sid[...], charges[...], weights):
+        spread_pack[start : start + rows.shape[0], :] = rows
+        start += rows.shape[0]
+    zh[...], zl[...] = split(place_periodic(z_cell, spline_values(fraction[2:3])))
+    for copy in copies[4:] + leaving:
         copy.wait()
 
 
@@ -537,45 +585,17 @@
     )
 
 
-def spread_kernel(
-    dev, live, sums, sid_hbm, charges_hbm, cells_hbm, fraction_hbm, influence, z_high, z_low, table,
-    out, neutral_out, edge,
-    sid, charges, cells, fraction, neutral_buf, buf, sems, out_sems,
-):
-    copies = run_copies(
-        [
-            (sid_hbm, sid),
-            (charges_hbm, charges),
-            (cells_hbm, cells),
-            (fraction_hbm, fraction),
-            (influence.at[8:16, 0], edge),
-        ],
-        sems,
-    )
-    d = dev[0]
-    row = d // N_COL
+def spread_kernel(dev, sums, pack, z_high, z_low, table, out, neutral_out):
+    row = dev[0] // N_COL
 
     def row_of(dr, k):
         return sums[pl.ds((row + 2 * N_ROW + dr) % N_ROW * 4 + k, 1), :]
 
-    means = fragment_means(row_of, pltpu.roll)
-    for copy in copies[:4]:
-        copy.wait()
-    neutral = neutral_charges(d, live[0], sid[...], charges[...], means)
-    neutral_buf[...] = neutral
-    leaving = [pltpu.make_async_copy(neutral_buf, neutral_out, sems.at[5])]
-    leaving[0].start()
-    x, y, _ = local_cells(d, cells[...])
-    messages = spread_to_z(
-        neutral, x, y, fraction[...], z_high[...], z_low[...], table, pltpu.roll
-    )
+    neutral = neutral_charges(pack, fragment_means(row_of, pltpu.roll))
+    neutral_out[...] = neutral
+    messages = spread_to_z(neutral, pack, z_high[...], z_low[...], table, pltpu.roll)
     for c, message in enumerate(messages):
-        buf[c] = message
-        leaving.append(pltpu.make_async_copy(buf.at[c], out.at[c], out_sems.at[c]))
-        leaving[-1].start()
-    copies[4].wait()
-    for copy in leaving:
-        copy.wait()
+        out[c] = message
 
 
 def slant(x, shift):
@@ -589,14 +609,16 @@
 def y_forward_kernel(x, table, out):
     blocks = add_halo(pairs_of(x), pltpu.roll, slant)
     y = y_stage(jnp.concatenate([b for pair in blocks for b in pair], axis=0), table[...])
-    out[:, :, :LANES] = y[:N].reshape(N_ROW, 8, LANES)
-    out[:, :, LANES:] = y[N:].reshape(N_ROW, 8, LANES)
+    out[:, :, :LANES] = pltpu.roll(y[:N], N - 1, 0).reshape(N_ROW, 8, LANES)
+    out[:, :, LANES:] = pltpu.roll(y[N:], N - 1, 0).reshape(N_ROW, 8, LANES)
 
 
 def y_back_kernel(x, table, out):
+    re = pltpu.roll(x[:, :, :LANES].reshape(N, LANES), 1, 0)
+    im = -pltpu.roll(x[:, :, LANES:].reshape(N, LANES), 1, 0)
     pieces = []
-    for r in range(0, N_ROW, 2):
-        pieces += [x[r, :, :LANES], x[r + 1, :, :LANES], -x[r, :, LANES:], -x[r + 1, :, LANES:]]
+    for c in range(N_COL):
+        pieces += [re[c * CY : (c + 1) * CY], im[c * CY : (c + 1) * CY]]
     y = y_stage(jnp.concatenate(pieces, axis=0), table[...])
     blocks = [
         [y[c * CY : (c + 1) * CY], -y[N + c * CY : N + (c + 1) * CY]] for c in range(N_COL)
@@ -606,9 +628,7 @@
         out[c, CY:] = im
 
 
-def gain_kernel(dev, own_hbm, mirror_hbm, edge_hbm, out, own, mirror, edge, sems):
-    for copy in run_copies([(own_hbm, own), (mirror_hbm, mirror), (edge_hbm, edge)], sems):
-        copy.wait()
+def gain_kernel(dev, own, mirror, edge, out):
     flat = own[...].reshape(128, N)
     pieces = gain_table(dev[0], flat, mirror[...].reshape(64, N), edge[...], pltpu.roll)
     for k1, piece in enumerate(pieces):
@@ -616,35 +636,21 @@
         out[k1 * 8 : (k1 + 1) * 8, LANES:] = piece
 
 
-def x_kernel(x, gain, twiddle_hbm, mix_hbm, out, twiddle, mix, sems):
-    copies = run_copies([(twiddle_hbm, twiddle), (mix_hbm, mix)], sems)
-
+def x_kernel(x, gain, twiddle, mix, out):
     def factor(k1):
         return twiddle[k1, 0:1, :], twiddle[k1, 1:2, :]
 
     values = fft([(x[r, :, :LANES], x[r, :, LANES:]) for r in range(N_ROW)], -1.0)
-    for copy in copies:
-        copy.wait()
     wave = x_mix(x_turn(values, factor), gain[...], mix)
     for r, (re, im) in enumerate(x_back(wave, factor)):
         out[r, :, :LANES] = re
         out[r, :, LANES:] = im
 
 
-def atom_kernel(
-    dev, message, neutral_hbm, cells_hbm, fraction_hbm, zh, zl, vh, vl, table,
-    force, energy,
-    neutral, cells, fraction, sems,
-):
-    copies = run_copies(
-        [(neutral_hbm, neutral), (cells_hbm, cells), (fraction_hbm, fraction)], sems
-    )
+def atom_kernel(message, neutral, pack, zh, zl, vh, vl, table, force, energy):
     wave = from_messages(lambda c: message[c], pltpu.roll)
-    for copy in copies:
-        copy.wait()
-    x, y, _ = local_cells(dev[0], cells[...])
     e, g = interpolate(
-        wave, neutral[...], x, y, fraction[...], (zh[...], zl[...]), (vh[...], vl[...]), table
+        wave, neutral[...], pack, (zh[...], zl[...]), (vh[...], vl[...]), table
     )
     energy[...] = e
     for d in range(3):
@@ -685,85 +691,56 @@
     dev = lax.axis_index(ALL).astype(jnp.int32).reshape(1)
     charges = charges.reshape(1, ATOMS)
     sid = structure_id.reshape(1, ATOMS)
-    sid_buf = pltpu.VMEM((1, ATOMS), jnp.int32)
-    row_buf = pltpu.VMEM((1, ATOMS), f32)
-    cell_buf = pltpu.VMEM((3, ATOMS), jnp.int32)
-    fraction_buf = pltpu.VMEM((3, ATOMS), f32)
-    sums, mirror = call(
+    sums, mirror, edge = call(
         partial_kernel,
-        [("v", (N_COL, LANES), f32), ("h", (8, 8, N), f32)],
+        [("v", (N_COL, LANES), f32), ("v", (8, 8, N), f32), ("v", (NK, N), f32)],
         "sshhh",
         (dev, live_count, sid, charges, influence),
-        [sid_buf, row_buf, sems(3)],
-    )
+        [pltpu.VMEM((1, ATOMS), jnp.int32), pltpu.VMEM((1, ATOMS), f32), sems(4)],
+    )
+    edge = lax.ppermute(edge, ROW, [((i + 1) % N_ROW, i) for i in range(N_ROW)])
     sums = swap(sums.reshape(N_COL, 1, LANES), COL).reshape(N_COL, LANES)
     sums = call(relay_kernel, [("v", (4 * N_ROW, LANES), f32)], "sv", (dev, sums))
     sums, mirror = lax.optimization_barrier((sums, mirror))
     mirror = lax.ppermute(mirror, ALL, [(i, DEV - 1 - i) for i in range(DEV)])
     sums = swap(sums.reshape(N_ROW, 4, LANES), ROW).reshape(4 * N_ROW, LANES)
     twiddle, mix = x_tables()
-    z_tab, y_tab, zh, zl, vh, vl = call(
+    sources = (cells, fraction, sid, charges, influence, z_table(), y_table(), twiddle)
+    half = ((N, ATOMS), bf16)
+    own, z_tab, y_tab, twiddle, spread_pack, zh, zl, atom_pack, vh, vl = call(
         prefetch_kernel,
-        [("v", (2, N, 3 * LANES), bf16), ("v", (4 * N, 2 * N), bf16)]
-        + [("v", (N, ATOMS), bf16)] * 4,
-        "hhhh",
-        (cells, fraction, z_table(), y_table()),
-        [cell_buf, fraction_buf, sems(4)],
-    )
-    sums, mirror, zh = lax.optimization_barrier((sums, mirror, zh))
-    messages, neutral, edge = call(
+        [("v", x.shape, x.dtype) for x in sources[4:]]
+        + [("v", (SPREAD_ROWS, ATOMS), f32), ("v",) + half, ("v",) + half]
+        + [("h", (ATOM_ROWS, ATOMS), f32), ("h",) + half, ("h",) + half],
+        "ss" + "h" * len(sources),
+        (dev, live_count) + sources,
+        [
+            pltpu.VMEM((3, ATOMS), jnp.int32), pltpu.VMEM((3, ATOMS), f32),
+            pltpu.VMEM((1, ATOMS), jnp.int32), pltpu.VMEM((1, ATOMS), f32),
+            pltpu.VMEM((ATOM_ROWS, ATOMS), f32), pltpu.VMEM(*half), pltpu.VMEM(*half), sems(11),
+        ],
+    )
+    gain = call(gain_kernel, [("v", (N, 2 * LANES), f32)], "svvv", (dev, own, mirror, edge))
+    zh, gain = lax.optimization_barrier((zh, gain))
+    messages, neutral = call(
         spread_kernel,
-        [("h", (N_COL, ROWS, LANES), f32), ("h", (1, ATOMS), f32), ("h", (8, N), f32)],
-        "ssvhhhhhvvv",
-        (
-            dev, live_count, sums, sid, charges, cells, fraction, influence,
-            zh, zl, z_tab,
-        ),
-        [
-            sid_buf, row_buf, cell_buf, fraction_buf, row_buf,
-            pltpu.VMEM((N_COL, ROWS, LANES), f32), sems(6), sems(N_COL),
-        ],
-    )
-    edge = lax.ppermute(
-        edge,
-        ALL,
-        [(i, (N_ROW - i // N_COL) % N_ROW * N_COL + N_COL - 1 - i % N_COL) for i in range(DEV)],
+        [("v", (N_COL, ROWS, LANES), f32), ("v", (1, ATOMS), f32)],
+        "svvvvv",
+        (dev, sums, spread_pack, zh, zl, z_tab),
     )
     columns = swap(messages, COL)
-    gain = call(
-        gain_kernel,
-        [("v", (N, 2 * LANES), f32)],
-        "shhh",
-        (dev, influence, mirror, edge),
-        [
-            pltpu.VMEM((16, 8, N), f32), pltpu.VMEM((8, 8, N), f32), pltpu.VMEM((8, N), f32),
-            sems(3),
-        ],
-    )
-    columns, gain = lax.optimization_barrier((columns, gain))
     strip = [("v", (N_ROW, 8, 2 * LANES), f32)]
     rows = call(y_forward_kernel, strip, "vv", (columns, y_tab))
     rows = swap(rows, ROW)
-    rows = call(
-        x_kernel,
-        strip,
-        "vvhh",
-        (rows, gain, twiddle, mix),
-        [
-            pltpu.VMEM((N_ROW, 2, LANES), f32),
-            pltpu.VMEM((2, 2 * LANES, 2 * LANES), bf16),
-            sems(2),
-        ],
-    )
+    rows = call(x_kernel, strip, "vvvv", (rows, gain, twiddle, mix))
     rows = swap(rows, ROW)
     columns = call(y_back_kernel, [("v", (N_COL, ROWS, LANES), f32)], "vv", (rows, y_tab))
     columns = swap(columns, COL)
     forces, energy = call(
         atom_kernel,
         [("v", (3, ATOMS), f32), ("v", (1, ATOMS), f32)],
-        "svhhhvvvvv",
-        (dev, columns, neutral, cells, fraction, zh, zl, vh, vl, z_tab),
-        [row_buf, cell_buf, fraction_buf, sems(3)],
+        "vvvvvvvv",
+        (columns, neutral, atom_pack, zh, zl, vh, vl, z_tab),
     )
     return forces, energy.reshape(ATOMS)
 

time: 136 us -> 122 us (0.90)
  blocking collectives: 77.3 us -> 85.4 us
  starting transfers between devices: 28.9 us -> 21.5 us
  waiting for transfers between devices: 8.47 us -> 1.11 us
  Pallas kernels: 18.9 us -> 12.4 us
    all_to_all x4 -> x5, blocking collectives: 77.3 us -> 85.4 us  [swap(): return lax.all_to_all(x, axis, split_axis=0, concat_axis=0, tiled=True)]
    pallas_call x9, Pallas kernels: 18.9 us -> 12.4 us  [call(): pl.pallas_call(kernel, out_shape=[pltpu.HBM(shape, dtype) if k == 'h' els...]
    all_to_all x2 -> x1, starting transfers between devices: 16.5 us -> 12 us  [swap(): return lax.all_to_all(x, axis, split_axis=0, concat_axis=0, tiled=True)]
    ppermute x1, waiting for transfers between devices: 3.9 us -> 0.01 us  [body(): mirror = lax.ppermute(mirror, ALL, [(i, DEV - 1 - i) for i in range(DEV)])]
    ppermute x1, waiting for transfers between devices: 4.06 us -> 1.11 us  [body(): edge = lax.ppermute(edge, ROW, [((i + 1) % N_ROW, i) for i in range(N_ROW)])]
    ppermute x1, starting transfers between devices: 4.84 us -> 1.92 us  [body(): edge = lax.ppermute(edge, ROW, [((i + 1) % N_ROW, i) for i in range(N_ROW)])]
  transfers between devices with their start and end apart: 4 -> 3, of which waited for: 3 -> 1; matrix products, arithmetic and copies ran while one was open for 0% -> 0% of each run, Pallas kernels for 3% -> 3%
where the time goes in v4:
time: 122 us
  blocking collectives  85.4 us (70%)
  starting transfers between devices  21.5 us (18%)
  Pallas kernels  12.4 us (10%)
  between operations  1.38 us (1%)
    all_to_all x5, blocking collectives, swap(): return lax.all_to_all(x, axis, split_axis=0, concat_axis=0, tiled=True)  85.4 us
    pallas_call x9, Pallas kernels, call(): pl.pallas_call(kernel, out_shape=[pltpu.HBM(shape, dtype) if k == 'h' els...  12.4 us
    all_to_all x1, starting transfers between devices, swap(): return lax.all_to_all(x, axis, split_axis=0, concat_axis=0, tiled=True)  12 us
    ppermute x1, starting transfers between devices, body(): mirror = lax.ppermute(mirror, ALL, [(i, DEV - 1 - i) for i in range(DEV)])  7.64 us
  transfers between devices with their start and end apart: 3, of which 1 were waited for; matrix products, arithmetic and copies ran while one was open for 0% of the time, Pallas kernels for 3%

profile of v4, /device:TPU:1, one launch (start us, length us, event | category | flops | bytes accessed | tf_op | source)
XLA Modules:
  0.0 121.8 jit_solution(1068133354199362123)
XLA Ops:
  1.3 0.9 shard_map.113
  2.2 16.3 %all_to_all.30 = f32[16,1,128]{2,1,0:T(1,128)S(1)} all-to-all(f32[16,1,128]{2,1,0:T(1,128)S(1)} %bitcast.12), channel_id=1, replica_groups=mesh['row_0'=4,'row_1'=8,'col_0'=8,'col_1'=2] {'col_0','col_1'}, dimensions={0} | all-to-all | bytes 16384 | tf_op jit(solution)/shard_map/all_to_all | solution.py:687
  18.5 0.7 shard_map.114
  19.2 12.0 %all-to-all-start.1 = ((f32[32,4,128]{2,1,0:T(4,128)}), f32[32,4,128]{2,1,0:T(4,128)S(1)}, u32[]{:S(2)}, u32[]{:S(2)}) async-start(f32[32,4,128]{2,1,0:T(4,128)} %bitcast.6), calls=%async_computation.1 | async-start | bytes 131072 | tf_op jit(solution)/shard_map/all_to_all | solution.py:687
  31.2 7.6 %collective-permute-start = (f32[8,8,256]{2,1,0:T(8,128)S(1)}, f32[8,8,256]{2,1,0:T(8,128)S(1)}, u32[]{:S(2)}, u32[]{:S(2)}) collective-permute-start(f32[8,8,256]{2,1,0:T(8,128)S(1)} %get-tuple-element.29), channel_id=1, source_target_pairs={{0,511},{1,510},{2,509},{3,508},{4,507},{5,506},{6,505},{7,504},{8... | collective-permute-start | bytes 196616 | tf_op jit(solution)/shard_map/ppermute | solution.py:705
  38.9 1.9 %collective-permute-start.1 = (f32[9,256]{1,0:T(8,128)S(1)}, f32[9,256]{1,0:T(8,128)S(1)}, u32[]{:S(2)}, u32[]{:S(2)}) collective-permute-start(f32[9,256]{1,0:T(8,128)S(1)} %get-tuple-element.30), channel_id=1, source_target_pairs={{16,0},{32,16},{48,32},{64,48},{80,64},{96,80},{112,96},{128,112},... | collective-permute-start | bytes 27656 | tf_op jit(solution)/shard_map/ppermute | solution.py:701
  40.8 2.7 %shard_map.115 = (f32[16,8,256]{2,1,0:T(8,128)S(1)}, bf16[2,256,384]{2,1,0:T(8,128)(2,1)S(1)}, bf16[1024,512]{1,0:T(8,128)(2,1)S(1)}, f32[32,2,128]{2,1,0:T(2,12...) custom-call(s32[1]{0:T(128)} %bitcast.dev, ...), custom_call_target="tpu_custom_call" | custom-call | tf_op jit(solution)/shard_map/pallas_call | solution.py:668
  43.5 1.1 collective-permute-done.1.edge
  44.7 0.0 collective-permute-done.mirror
  44.7 0.9 shard_map.116.gain
  45.6 0.0 all-to-all-done.1
  45.6 2.4 %shard_map.117 = (f32[16,32,128]{2,1,0:T(8,128)S(1)}, f32[1,1024]{1,0:T(1,128)S(1)}) custom-call(s32[1]{0:T(128)} %bitcast.dev, f32[128,128]{1,0:T(8,128)S(1)} %bitcast.10, f32[96,1024]{1,0:T(8,128)S(1)} %get-tuple-element.26.pack, bf16[256,1024]{1,0:T(8,128)(2,1)S(1)} %get-tuple-element.31.z_high.zh, bf16[256,1024]{1,0:T(8,128)(2,1)S(1)} %get-tuple-element.32.z_low.zl, ...), custom_call_target="tpu_custom_call" | custom-call | tf_op jit(solution)/shard_map/pallas_call | solution.py:668
  47.9 16.5 %all_to_all.31.x = f32[16,32,128]{2,1,0:T(8,128)S(1)} all-to-all(f32[16,32,128]{2,1,0:T(8,128)S(1)} %get-tuple-element.34), channel_id=1, replica_groups=mesh['row_0'=4,'row_1'=8,'col_0'=8,'col_1'=2] {'col_0','col_1'}, dimensions={0} | all-to-all | bytes 524288 | tf_op jit(solution)/shard_map/all_to_all | solution.py:687
  64.4 0.7 shard_map.118
  65.2 0.0 copy-start.3
  65.2 18.9 %all_to_all.32.x = f32[32,8,256]{2,1,0:T(8,128)S(1)} all-to-all(f32[32,8,256]{2,1,0:T(8,128)S(1)} %shard_map.118), channel_id=1, replica_groups=mesh['row_0'=4,'row_1'=8,'col_0'=8,'col_1'=2] {'row_0','row_1'}, dimensions={0} | all-to-all | bytes 524288 | tf_op jit(solution)/shard_map/all_to_all | solution.py:687
  84.1 0.0 copy-done.3
  84.1 0.7 shard_map.119
  84.8 15.6 %all_to_all.33.x = f32[32,8,256]{2,1,0:T(8,128)S(1)} all-to-all(f32[32,8,256]{2,1,0:T(8,128)S(1)} %shard_map.119), channel_id=1, replica_groups=mesh['row_0'=4,'row_1'=8,'col_0'=8,'col_1'=2] {'row_0','row_1'}, dimensions={0} | all-to-all | bytes 524288 | tf_op jit(solution)/shard_map/all_to_all | solution.py:687
  100.3 0.0 copy-start.1
  100.3 0.0 copy-start.2
  100.3 0.7 shard_map.120
  101.1 0.0 copy-start
  101.1 18.1 %all_to_all.34.message = f32[16,32,128]{2,1,0:T(8,128)S(1)} all-to-all(f32[16,32,128]{2,1,0:T(8,128)S(1)} %shard_map.120), channel_id=1, replica_groups=mesh['row_0'=4,'row_1'=8,'col_0'=8,'col_1'=2] {'col_0','col_1'}, dimensions={0} | all-to-all | bytes 524288 | tf_op jit(solution)/shard_map/all_to_all | solution.py:687
  119.2 0.0 copy-done.1
  119.2 0.0 copy-done.2
  119.2 0.0 copy-done
  119.2 2.6 %shard_map.121 = (f32[3,1024]{1,0:T(4,128)}, f32[1,1024]{1,0:T(1,128)}) custom-call(f32[16,32,128]{2,1,0:T(8,128)S(1)} %all_to_all.34.message, f32[1,1024]{1,0:T(1,128)S(1)} %get-tuple-element.38.neutral, f32[112,1024]{1,0:T(8,128)S(1)} %copy-done.2, bf16[256,1024]{1,0:T(8,128)(2,1)S(1)} %get-tuple-element.31.z_high.zh, ...), custom_call_target="tpu_custom_call" | custom-call | tf_op jit(solution)/shard_map/pallas_call | solution.py:668
Async XLA Ops:
  19.2 26.3 %all-to-all-start.1 = ((f32[32,4,128]{2,1,0:T(4,128)}), f32[32,4,128]{2,1,0:T(4,128)S(1)}, u32[]{:S(2)}, u32[]{:S(2)}) async-start(f32[32,4,128]{2,1,0:T(4,128)} %bitcast.6), calls=%async_computation.1 | async-start | bytes 131072 | tf_op jit(solution)/shard_map/all_to_all | solution.py:687
  31.2 13.4 %collective-permute-start = (f32[8,8,256]{2,1,0:T(8,128)S(1)}, f32[8,8,256]{2,1,0:T(8,128)S(1)}, u32[]{:S(2)}, u32[]{:S(2)}) collective-permute-start(f32[8,8,256]{2,1,0:T(8,128)S(1)} %get-tuple-element.29), channel_id=1, source_target_pairs={{0,511},{1,510},{2,509},{3,508},{4,507},{5,506},{6,505},{7,504},{8... | collective-permute-start | bytes 196616 | tf_op jit(solution)/shard_map/ppermute | solution.py:705
  38.9 5.8 %collective-permute-start.1 = (f32[9,256]{1,0:T(8,128)S(1)}, f32[9,256]{1,0:T(8,128)S(1)}, u32[]{:S(2)}, u32[]{:S(2)}) collective-permute-start(f32[9,256]{1,0:T(8,128)S(1)} %get-tuple-element.30), channel_id=1, source_target_pairs={{16,0},{32,16},{48,32},{64,48},{80,64},{96,80},{112,96},{128,112},... | collective-permute-start | bytes 27656 | tf_op jit(solution)/shard_map/ppermute | solution.py:701
  65.2 18.9 %copy-start.3 = (bf16[2,256,256]{2,1,0:T(8,128)(2,1)S(1)}, bf16[2,256,256]{2,1,0:T(8,128)(2,1)}, u32[]{:S(2)}) copy-start(bf16[2,256,256]{2,1,0:T(8,128)(2,1)} %constant.34.clone.mix) | copy-start | bytes 786436
  100.3 18.9 %copy-start.1 = (bf16[256,1024]{1,0:T(8,128)(2,1)S(1)}, bf16[256,1024]{1,0:T(8,128)(2,1)}, u32[]{:S(2)}) copy-start(bf16[256,1024]{1,0:T(8,128)(2,1)} %get-tuple-element.41.vl) | copy-start | bytes 1572868
  100.3 18.9 %copy-start.2 = (f32[112,1024]{1,0:T(8,128)S(1)}, f32[112,1024]{1,0:T(8,128)}, u32[]{:S(2)}) copy-start(f32[112,1024]{1,0:T(8,128)} %get-tuple-element.39.pack) | copy-start | bytes 1376260
  101.1 18.1 %copy-start = (bf16[256,1024]{1,0:T(8,128)(2,1)S(1)}, bf16[256,1024]{1,0:T(8,128)(2,1)}, u32[]{:S(2)}) copy-start(bf16[256,1024]{1,0:T(8,128)(2,1)} %get-tuple-element.40.vh) | copy-start | bytes 1572868

commit v5 on v4

--- a/solution.py
+++ b/solution.py
@@ -419,13 +419,14 @@
     col = device % N_COL
     r = lax.broadcasted_iota(jnp.int32, (72, 128), 0)
     k = lax.broadcasted_iota(jnp.int32, (72, 128), 1)
-    take_own = ((r % 8 < 7) & (k == r + 1)).astype(bf16)
+    take_own = (k == r).astype(bf16)
     r = lax.broadcasted_iota(jnp.int32, (72, 64), 0)
     k = lax.broadcasted_iota(jnp.int32, (72, 64), 1)
-    take_mirror = ((r >= 8) & (k == (8 - r // 8) * 8 + 7 - r % 8)).astype(bf16)
-    r = lax.broadcasted_iota(jnp.int32, (72, NK), 0)
-    k = lax.broadcasted_iota(jnp.int32, (72, NK), 1)
-    take_edge = ((r % 8 == 7) & (k == r // 8)).astype(bf16)
+    slot, i = r // 8, r % 8
+    take_mirror = ((slot > 0) & (i > 0) & (k == (8 - slot) * 8 + 8 - i)).astype(bf16)
+    r = lax.broadcasted_iota(jnp.int32, (72, 8), 0)
+    k = lax.broadcasted_iota(jnp.int32, (72, 8), 1)
+    take_edge = ((r // 8 > 0) & (r % 8 == 0) & (k == 8 - r // 8)).astype(bf16)
     kx = lax.broadcasted_iota(jnp.int32, (N, N), 0)
     lane = lax.broadcasted_iota(jnp.int32, (N, N), 1)
     wave = lane // 8 + 32 * (lane % 8)
@@ -439,7 +440,7 @@
         return dot(high, permutation) + dot(low, permutation)
 
     gain = ordered(own, take_own, order)
-    gain = gain + ordered(mirror, take_mirror, reverse) + ordered(edge, take_edge, order)
+    gain = gain + ordered(mirror, take_mirror, reverse) + ordered(edge, take_edge, reverse)
     row = lax.broadcasted_iota(jnp.int32, (72, N), 0)
     gain = jnp.where((row >= 64) & (col >= 8), 0.0, gain) * (1.0 / (N * N * N))
     lanes = lane_iota(8)
@@ -510,24 +511,11 @@
     return copies
 
 
-def partial_kernel(
-    dev, live, sid_hbm, charges_hbm, influence, out, mirror, edge, sid, charges, sems
-):
-    copies = run_copies(
-        [
-            (sid_hbm, sid),
-            (charges_hbm, charges),
-            (influence.at[8:16], mirror),
-            (influence.at[0:NK, 0], edge),
-        ],
-        sems,
-    )
-    copies[0].wait()
-    copies[1].wait()
+def partial_kernel(dev, live, sid_hbm, charges_hbm, out, sid, charges, sems):
+    for copy in run_copies([(sid_hbm, sid), (charges_hbm, charges)], sems):
+        copy.wait()
     row = partial_sums(dev[0], live[0], sid[...], charges[...])
     out[...] = jnp.broadcast_to(row, (N_COL, LANES))
-    copies[2].wait()
-    copies[3].wait()
 
 
 def relay_kernel(dev, sums, out):
@@ -536,18 +524,37 @@
         out[k * 8 : (k + 1) * 8, :] = rows
 
 
+def mirror_of(device):
+    return DEV - 1 - device
+
+
+def edge_mirror_of(device):
+    return (N_ROW - device // N_COL) % N_ROW * N_COL + N_COL - 1 - device % N_COL
+
+
+def pairs_by(partner):
+    return [[d, partner(d)] for d in range(DEV) if d < partner(d)]
+
+
 def prefetch_kernel(
-    dev, live, cells_hbm, fraction_hbm, sid_hbm, charges_hbm, own_hbm, z_tab, y_tab, turn_tab,
-    own, z, y, turn, spread_pack, zh, zl, atom_pack_hbm, vh_hbm, vl_hbm,
-    cells, fraction, sid, charges, atom_pack, vh, vl, sems,
+    dev, live, cells_hbm, fraction_hbm, sid_hbm, charges_hbm, influence, z_tab, y_tab, turn_tab,
+    own, z, y, turn, spread_pack, zh, zl, atom_pack_hbm, vh_hbm, vl_hbm, mirror_hbm, edge_hbm,
+    cells, fraction, sid, charges, atom_pack, vh, vl, mirror, edge, sems,
 ):
+    d = dev[0]
+    slot = jnp.where(d < mirror_of(d), 8, 0)
+    edge_slot = jnp.where(d < edge_mirror_of(d), 8, 0)
+    mirror[pl.ds(8 - slot, 8)] = jnp.zeros((8, 8, N), f32)
+    edge[pl.ds(pl.multiple_of(8 - edge_slot, 8), 8), :] = jnp.zeros((8, N), f32)
     copies = run_copies(
         [
             (cells_hbm, cells),
             (fraction_hbm, fraction),
             (sid_hbm, sid),
             (charges_hbm, charges),
-            (own_hbm, own),
+            (influence.at[8:16], mirror.at[pl.ds(slot, 8)]),
+            (influence.at[8:16, 0], edge.at[pl.ds(pl.multiple_of(edge_slot, 8), 8), :]),
+            (influence, own),
             (z_tab, z),
             (y_tab, y),
             (turn_tab, turn),
@@ -558,22 +565,30 @@
         copy.wait()
     z_cell = cells[2:3]
     vh[...], vl[...] = split(place_periodic(z_cell, spline_slopes(fraction[2:3])))
-    x, y_cell, _ = local_cells(dev[0], cells[...])
+    x, y_cell, _ = local_cells(d, cells[...])
     weights = atom_weights(x, y_cell, fraction[...])
     start = 0
     for rows in weights:
         atom_pack[start : start + rows.shape[0], :] = rows
         start += rows.shape[0]
-    pairs = [(atom_pack, atom_pack_hbm), (vh, vh_hbm), (vl, vl_hbm)]
-    leaving = [pltpu.make_async_copy(a, b, sems.at[8 + i]) for i, (a, b) in enumerate(pairs)]
+    copies[4].wait()
+    copies[5].wait()
+    pairs = [
+        (mirror, mirror_hbm),
+        (edge, edge_hbm),
+        (atom_pack, atom_pack_hbm),
+        (vh, vh_hbm),
+        (vl, vl_hbm),
+    ]
+    leaving = [pltpu.make_async_copy(a, b, sems.at[10 + i]) for i, (a, b) in enumerate(pairs)]
     for copy in leaving:
         copy.start()
     start = 0
-    for rows in spread_rows(dev[0], live[0], sid[...], charges[...], weights):
+    for rows in spread_rows(d, live[0], sid[...], charges[...], weights):
         spread_pack[start : start + rows.shape[0], :] = rows
         start += rows.shape[0]
     zh[...], zl[...] = split(place_periodic(z_cell, spline_values(fraction[2:3])))
-    for copy in copies[4:] + leaving:
+    for copy in copies[6:] + leaving:
         copy.wait()
 
 
@@ -609,13 +624,13 @@
 def y_forward_kernel(x, table, out):
     blocks = add_halo(pairs_of(x), pltpu.roll, slant)
     y = y_stage(jnp.concatenate([b for pair in blocks for b in pair], axis=0), table[...])
-    out[:, :, :LANES] = pltpu.roll(y[:N], N - 1, 0).reshape(N_ROW, 8, LANES)
-    out[:, :, LANES:] = pltpu.roll(y[N:], N - 1, 0).reshape(N_ROW, 8, LANES)
+    out[:, :, :LANES] = y[:N].reshape(N_ROW, 8, LANES)
+    out[:, :, LANES:] = y[N:].reshape(N_ROW, 8, LANES)
 
 
 def y_back_kernel(x, table, out):
-    re = pltpu.roll(x[:, :, :LANES].reshape(N, LANES), 1, 0)
-    im = -pltpu.roll(x[:, :, LANES:].reshape(N, LANES), 1, 0)
+    re = x[:, :, :LANES].reshape(N, LANES)
+    im = -x[:, :, LANES:].reshape(N, LANES)
     pieces = []
     for c in range(N_COL):
         pieces += [re[c * CY : (c + 1) * CY], im[c * CY : (c + 1) * CY]]
@@ -630,7 +645,7 @@
 
 def gain_kernel(dev, own, mirror, edge, out):
     flat = own[...].reshape(128, N)
-    pieces = gain_table(dev[0], flat, mirror[...].reshape(64, N), edge[...], pltpu.roll)
+    pieces = gain_table(dev[0], flat, mirror[...], edge[...], pltpu.roll)
     for k1, piece in enumerate(pieces):
         out[k1 * 8 : (k1 + 1) * 8, :LANES] = piece
         out[k1 * 8 : (k1 + 1) * 8, LANES:] = piece
@@ -691,37 +706,38 @@
     dev = lax.axis_index(ALL).astype(jnp.int32).reshape(1)
     charges = charges.reshape(1, ATOMS)
     sid = structure_id.reshape(1, ATOMS)
-    sums, mirror, edge = call(
+    sums = call(
         partial_kernel,
-        [("v", (N_COL, LANES), f32), ("v", (8, 8, N), f32), ("v", (NK, N), f32)],
-        "sshhh",
-        (dev, live_count, sid, charges, influence),
-        [pltpu.VMEM((1, ATOMS), jnp.int32), pltpu.VMEM((1, ATOMS), f32), sems(4)],
-    )
-    edge = lax.ppermute(edge, ROW, [((i + 1) % N_ROW, i) for i in range(N_ROW)])
+        [("v", (N_COL, LANES), f32)],
+        "sshh",
+        (dev, live_count, sid, charges),
+        [pltpu.VMEM((1, ATOMS), jnp.int32), pltpu.VMEM((1, ATOMS), f32), sems(2)],
+    )
     sums = swap(sums.reshape(N_COL, 1, LANES), COL).reshape(N_COL, LANES)
     sums = call(relay_kernel, [("v", (4 * N_ROW, LANES), f32)], "sv", (dev, sums))
-    sums, mirror = lax.optimization_barrier((sums, mirror))
-    mirror = lax.ppermute(mirror, ALL, [(i, DEV - 1 - i) for i in range(DEV)])
     sums = swap(sums.reshape(N_ROW, 4, LANES), ROW).reshape(4 * N_ROW, LANES)
     twiddle, mix = x_tables()
     sources = (cells, fraction, sid, charges, influence, z_table(), y_table(), twiddle)
     half = ((N, ATOMS), bf16)
-    own, z_tab, y_tab, twiddle, spread_pack, zh, zl, atom_pack, vh, vl = call(
+    own, z_tab, y_tab, twiddle, spread_pack, zh, zl, atom_pack, vh, vl, mirror, edge = call(
         prefetch_kernel,
         [("v", x.shape, x.dtype) for x in sources[4:]]
         + [("v", (SPREAD_ROWS, ATOMS), f32), ("v",) + half, ("v",) + half]
-        + [("h", (ATOM_ROWS, ATOMS), f32), ("h",) + half, ("h",) + half],
+        + [("h", (ATOM_ROWS, ATOMS), f32), ("h",) + half, ("h",) + half]
+        + [("h", (16, 8, N), f32), ("h", (16, N), f32)],
         "ss" + "h" * len(sources),
         (dev, live_count) + sources,
         [
             pltpu.VMEM((3, ATOMS), jnp.int32), pltpu.VMEM((3, ATOMS), f32),
             pltpu.VMEM((1, ATOMS), jnp.int32), pltpu.VMEM((1, ATOMS), f32),
-            pltpu.VMEM((ATOM_ROWS, ATOMS), f32), pltpu.VMEM(*half), pltpu.VMEM(*half), sems(11),
+            pltpu.VMEM((ATOM_ROWS, ATOMS), f32), pltpu.VMEM(*half), pltpu.VMEM(*half),
+            pltpu.VMEM((16, 8, N), f32), pltpu.VMEM((16, N), f32), sems(15),
         ],
     )
-    gain = call(gain_kernel, [("v", (N, 2 * LANES), f32)], "svvv", (dev, own, mirror, edge))
-    zh, gain = lax.optimization_barrier((zh, gain))
+    mirror = lax.psum_scatter(
+        mirror.reshape(128, N), ALL, axis_index_groups=pairs_by(mirror_of), tiled=True
+    )
+    edge = lax.psum_scatter(edge, ALL, axis_index_groups=pairs_by(edge_mirror_of), tiled=True)
     messages, neutral = call(
         spread_kernel,
         [("v", (N_COL, ROWS, LANES), f32), ("v", (1, ATOMS), f32)],
@@ -729,6 +745,8 @@
         (dev, sums, spread_pack, zh, zl, z_tab),
     )
     columns = swap(messages, COL)
+    gain = call(gain_kernel, [("v", (N, 2 * LANES), f32)], "svvv", (dev, own, mirror, edge))
+    columns, gain = lax.optimization_barrier((columns, gain))
     strip = [("v", (N_ROW, 8, 2 * LANES), f32)]
     rows = call(y_forward_kernel, strip, "vv", (columns, y_tab))
     rows = swap(rows, ROW)

time: 122 us -> 166 us (1.36)
  waiting for transfers between devices: 1.11 us -> 51.5 us
  blocking collectives: 85.4 us -> 66.8 us
  between operations: 1.38 us -> 14.8 us
  starting transfers between devices: 21.5 us -> 17.5 us
    reduce_scatter x0 -> x2, waiting for transfers between devices: none -> 44.3 us  [the longest x1 28.3 us: body(): lax.psum_scatter(mirror.reshape(128, N), ALL, axis_index_groups=pairs_by(...]
    all_to_all x5 -> x4, blocking collectives: 85.4 us -> 66.8 us  [swap(): return lax.all_to_all(x, axis, split_axis=0, concat_axis=0, tiled=True)]
    ppermute x2 -> x0, starting transfers between devices: 9.56 us -> none  [the longest x1 7.64 us: body(): mirror = lax.ppermute(mirror, ALL, [(i, DEV - 1 - i) for i in range(DEV)])]
    all_to_all x1 -> x2, waiting for transfers between devices: 0.01 us -> 5.8 us  [swap(): return lax.all_to_all(x, axis, split_axis=0, concat_axis=0, tiled=True)]
    all_to_all x1 -> x2, starting transfers between devices: 12 us -> 17.4 us  [swap(): return lax.all_to_all(x, axis, split_axis=0, concat_axis=0, tiled=True)]
  transfers between devices with their start and end apart: 3 -> 4, of which waited for: 1 -> 3; matrix products, arithmetic and copies ran while one was open for 0% -> 0% of each run, Pallas kernels for 3% -> 2%
where the time goes in v5:
time: 166 us; the launch traced here: 165 us
  blocking collectives  66.8 us (40%)
  waiting for transfers between devices  51.5 us (31%)
  starting transfers between devices  17.5 us (11%)
  between operations  14.8 us (9%)
  Pallas kernels  13.3 us (8%)
    all_to_all x4, blocking collectives, swap(): return lax.all_to_all(x, axis, split_axis=0, concat_axis=0, tiled=True)  66.8 us
    reduce_scatter x1, waiting for transfers between devices, body(): lax.psum_scatter(mirror.reshape(128, N), ALL, axis_index_groups=pairs_by(...  28.3 us
    all_to_all x2, starting transfers between devices, swap(): return lax.all_to_all(x, axis, split_axis=0, concat_axis=0, tiled=True)  17.4 us
    reduce_scatter x1, waiting for transfers between devices, body(): lax.psum_scatter(edge, ALL, axis_index_groups=pairs_by(edge_mirror_of), t...  16 us
    pallas_call x9, Pallas kernels, call(): pl.pallas_call(kernel, out_shape=[pltpu.HBM(shape, dtype) if k == 'h' els...  13.3 us
    all_to_all x2, waiting for transfers between devices, swap(): return lax.all_to_all(x, axis, split_axis=0, concat_axis=0, tiled=True)  5.8 us
  transfers between devices with their start and end apart: 4, of which 3 were waited for; matrix products, arithmetic and copies ran while one was open for 0% of the time, Pallas kernels for 2%

profile of v5, /device:TPU:1, one launch (start us, length us, event | category | flops | bytes accessed | tf_op | source)
XLA Modules:
  0.0 165.4 jit_solution(18383609473735289392)
XLA Ops:
  7.8 0.8 shard_map.113
  8.7 16.3 %all_to_all.30 = f32[16,1,128]{2,1,0:T(1,128)S(1)} all-to-all(f32[16,1,128]{2,1,0:T(1,128)S(1)} %bitcast.13), channel_id=1, replica_groups=mesh['row_0'=4,'row_1'=8,'col_0'=8,'col_1'=2] {'col_0','col_1'}, dimensions={0} | all-to-all | bytes 16384 | tf_op jit(solution)/shard_map/all_to_all | solution.py:702
  25.0 0.7 shard_map.114
  25.7 12.0 %all-to-all-start.1 = ((f32[32,4,128]{2,1,0:T(4,128)}), f32[32,4,128]{2,1,0:T(4,128)S(1)}, u32[]{:S(2)}, u32[]{:S(2)}) async-start(f32[32,4,128]{2,1,0:T(4,128)} %bitcast.6), calls=%async_computation.1 | async-start | bytes 131072 | tf_op jit(solution)/shard_map/all_to_all | solution.py:702
  37.7 3.1 %shard_map.115 = (f32[16,8,256]{2,1,0:T(8,128)S(1)}, bf16[2,256,384]{2,1,0:T(8,128)(2,1)S(1)}, bf16[1024,512]{1,0:T(8,128)(2,1)S(1)}, f32[32,2,128]{2,1,0:T(2,12...) custom-call(s32[1]{0:T(128)} %bitcast.dev, ...), custom_call_target="tpu_custom_call" | custom-call | tf_op jit(solution)/shard_map/pallas_call | solution.py:683
  40.8 5.8 %all-to-all-done.1 = f32[32,4,128]{2,1,0:T(4,128)S(1)} async-done(((f32[32,4,128]{2,1,0:T(4,128)}), f32[32,4,128]{2,1,0:T(4,128)S(1)}, u32[]{:S(2)}, u32[]{:S(2)}) %all-to-all-start.1) | async-done | bytes 65568 | tf_op jit(solution)/shard_map/all_to_all | solution.py:702
  46.6 3.0 %shard_map.116 = (f32[16,32,128]{2,1,0:T(8,128)}, f32[1,1024]{1,0:T(1,128)S(1)}) custom-call(s32[1]{0:T(128)} %bitcast.dev, f32[128,128]{1,0:T(8,128)S(1)} %bitcast.11, f32[96,1024]{1,0:T(8,128)S(1)} %get-tuple-element.20.pack, bf16[256,1024]{1,0:T(8,128)(2,1)S(1)} %get-tuple-element.21.z_high.zh, bf16[256,1024]{1,0:T(8,128)(2,1)S(1)} %get-tuple-element.22.z_low.zl, ...), custom_call_target="tpu_custom_call" | custom-call | tf_op jit(solution)/shard_map/pallas_call | solution.py:683
  49.6 5.4 %all-to-all-start.2 = ((f32[16,32,128]{2,1,0:T(8,128)}), f32[16,32,128]{2,1,0:T(8,128)S(1)}, u32[]{:S(2)}, u32[]{:S(2)}) async-start(f32[16,32,128]{2,1,0:T(8,128)} %get-tuple-element.24), calls=%async_computation.2 | async-start | bytes 524288 | tf_op jit(solution)/shard_map/all_to_all | solution.py:702
  55.0 0.0 reduce-scatter.5.cloned.1.call-start
  55.1 0.7 reduce-scatter.5.cloned.1.call-update
  55.7 0.0 reduce-scatter.3.cloned.1.call-start
  55.8 0.7 reduce-scatter.3.cloned.1.call-update
  56.5 16.0 %reduce-scatter.5.cloned.1.call-done.edge = f32[8,256]{1,0:T(8,128)} async-done(((f32[16,256]{1,0:T(8,128)}), f32[8,256]{1,0:T(8,128)}) %reduce-scatter.5.cloned.1.call-update) | async-done | bytes 8208 | tf_op jit(solution)/shard_map/reduce_scatter | solution.py:740
  72.5 28.3 %reduce-scatter.3.cloned.1.call-done.mirror = f32[64,256]{1,0:T(8,128)} async-done(((f32[128,256]{1,0:T(8,128)}), f32[64,256]{1,0:T(8,128)}) %reduce-scatter.3.cloned.1.call-update) | async-done | bytes 65552 | tf_op jit(solution)/shard_map/reduce_scatter | solution.py:737
  100.8 0.0 copy-start.4
  100.8 0.8 copy-done.4
  101.6 0.0 copy-start.5
  101.6 0.7 copy-done.5
  102.3 0.9 shard_map.117.gain
  103.2 0.0 all-to-all-done.2.x
  103.3 0.7 shard_map.118
  104.0 0.0 copy-start.3
  104.0 14.3 %all_to_all.31.x = f32[32,8,256]{2,1,0:T(8,128)S(1)} all-to-all(f32[32,8,256]{2,1,0:T(8,128)S(1)} %shard_map.118), channel_id=1, replica_groups=mesh['row_0'=4,'row_1'=8,'col_0'=8,'col_1'=2] {'row_0','row_1'}, dimensions={0} | all-to-all | bytes 524288 | tf_op jit(solution)/shard_map/all_to_all | solution.py:702
  118.3 0.0 copy-done.3
  118.3 0.7 shard_map.119
  119.0 16.4 %all_to_all.32.x = f32[32,8,256]{2,1,0:T(8,128)S(1)} all-to-all(f32[32,8,256]{2,1,0:T(8,128)S(1)} %shard_map.119), channel_id=1, replica_groups=mesh['row_0'=4,'row_1'=8,'col_0'=8,'col_1'=2] {'row_0','row_1'}, dimensions={0} | all-to-all | bytes 524288 | tf_op jit(solution)/shard_map/all_to_all | solution.py:702
  135.3 0.0 copy-start.1
  135.3 0.0 copy-start.2
  135.3 0.7 shard_map.120
  136.1 0.0 copy-start
  136.1 19.9 %all_to_all.33.message = f32[16,32,128]{2,1,0:T(8,128)S(1)} all-to-all(f32[16,32,128]{2,1,0:T(8,128)S(1)} %shard_map.120), channel_id=1, replica_groups=mesh['row_0'=4,'row_1'=8,'col_0'=8,'col_1'=2] {'col_0','col_1'}, dimensions={0} | all-to-all | bytes 524288 | tf_op jit(solution)/shard_map/all_to_all | solution.py:702
  156.0 0.0 copy-done.1
  156.0 0.0 copy-done.2
  156.0 0.0 copy-done
  156.0 2.6 %shard_map.121 = (f32[3,1024]{1,0:T(4,128)}, f32[1,1024]{1,0:T(1,128)}) custom-call(f32[16,32,128]{2,1,0:T(8,128)S(1)} %all_to_all.33.message, f32[1,1024]{1,0:T(1,128)S(1)} %get-tuple-element.32.neutral, f32[112,1024]{1,0:T(8,128)S(1)} %copy-done.2, bf16[256,1024]{1,0:T(8,128)(2,1)S(1)} %get-tuple-element.21.z_high.zh, ...), custom_call_target="tpu_custom_call" | custom-call | tf_op jit(solution)/shard_map/pallas_call | solution.py:683
Async XLA Ops:
  25.7 20.9 %all-to-all-start.1 = ((f32[32,4,128]{2,1,0:T(4,128)}), f32[32,4,128]{2,1,0:T(4,128)S(1)}, u32[]{:S(2)}, u32[]{:S(2)}) async-start(f32[32,4,128]{2,1,0:T(4,128)} %bitcast.6), calls=%async_computation.1 | async-start | bytes 131072 | tf_op jit(solution)/shard_map/all_to_all | solution.py:702
  49.6 53.6 %all-to-all-start.2 = ((f32[16,32,128]{2,1,0:T(8,128)}), f32[16,32,128]{2,1,0:T(8,128)S(1)}, u32[]{:S(2)}, u32[]{:S(2)}) async-start(f32[16,32,128]{2,1,0:T(8,128)} %get-tuple-element.24), calls=%async_computation.2 | async-start | bytes 524288 | tf_op jit(solution)/shard_map/all_to_all | solution.py:702
  55.0 17.5 %reduce-scatter.5.cloned.1.call-start = ((), (), s32[]{:S(2)}) async-start(), calls=%async_computation.9 | async-start | bytes 24576 | tf_op jit(solution)/shard_map/reduce_scatter | solution.py:740
  55.7 45.1 %reduce-scatter.3.cloned.1.call-start = ((), (), s32[]{:S(2)}) async-start(), calls=%async_computation.8 | async-start | bytes 196608 | tf_op jit(solution)/shard_map/reduce_scatter | solution.py:737
  100.8 0.8 copy-start.4
  101.6 0.7 copy-start.5
  104.0 14.3 %copy-start.3 = (bf16[2,256,256]{2,1,0:T(8,128)(2,1)S(1)}, bf16[2,256,256]{2,1,0:T(8,128)(2,1)}, u32[]{:S(2)}) copy-start(bf16[2,256,256]{2,1,0:T(8,128)(2,1)} %constant.34.clone.mix) | copy-start | bytes 786436
  135.3 20.6 %copy-start.1 = (bf16[256,1024]{1,0:T(8,128)(2,1)S(1)}, bf16[256,1024]{1,0:T(8,128)(2,1)}, u32[]{:S(2)}) copy-start(bf16[256,1024]{1,0:T(8,128)(2,1)} %get-tuple-element.35.vl) | copy-start | bytes 1572868
  135.3 20.6 %copy-start.2 = (f32[112,1024]{1,0:T(8,128)S(1)}, f32[112,1024]{1,0:T(8,128)}, u32[]{:S(2)}) copy-start(f32[112,1024]{1,0:T(8,128)} %get-tuple-element.33.pack) | copy-start | bytes 1376260
  136.1 19.9 %copy-start = (bf16[256,1024]{1,0:T(8,128)(2,1)S(1)}, bf16[256,1024]{1,0:T(8,128)(2,1)}, u32[]{:S(2)}) copy-start(bf16[256,1024]{1,0:T(8,128)(2,1)} %get-tuple-element.34.vh) | copy-start | bytes 1572868
Sparse Core Ops, SparseCore 0:
  59.1 13.2 reduce-scatter.4
  75.2 25.5 reduce-scatter.2

commit v6 on v4

--- a/solution.py
+++ b/solution.py
@@ -28,6 +28,7 @@
 PLANE = MAIN + 3 * CY
 GROUPS = XI + 3
 ROWS = 2 * CY
+RELAY = 24
 f32 = jnp.float32
 bf16 = jnp.bfloat16
 
@@ -510,30 +511,27 @@
     return copies
 
 
-def partial_kernel(
-    dev, live, sid_hbm, charges_hbm, influence, out, mirror, edge, sid, charges, sems
-):
+def partial_kernel(dev, live, sid_hbm, charges_hbm, influence, out, edge, sid, charges, sems):
     copies = run_copies(
-        [
-            (sid_hbm, sid),
-            (charges_hbm, charges),
-            (influence.at[8:16], mirror),
-            (influence.at[0:NK, 0], edge),
-        ],
-        sems,
+        [(sid_hbm, sid), (charges_hbm, charges), (influence.at[0:NK, 0], edge)], sems
     )
     copies[0].wait()
     copies[1].wait()
     row = partial_sums(dev[0], live[0], sid[...], charges[...])
     out[...] = jnp.broadcast_to(row, (N_COL, LANES))
     copies[2].wait()
-    copies[3].wait()
-
-
-def relay_kernel(dev, sums, out):
+
+
+def relay_kernel(dev, sums, edge, out):
     rows = relay_rows(dev[0] % N_COL, lambda c: sums[pl.ds(c, 1), :], pltpu.roll)
-    for k in range(N_ROW // 2):
-        out[k * 8 : (k + 1) * 8, :] = rows
+    sub = lax.broadcasted_iota(jnp.int32, (8, LANES), 0)
+    rows = jnp.where(sub == 0, edge[8:9, :LANES], rows)
+    rows = jnp.where(sub == 1, edge[8:9, LANES:], rows)
+    first, second = edge[0:8, :LANES], edge[0:8, LANES:]
+    for k in range(N_ROW):
+        out[k * RELAY : k * RELAY + 8, :] = first
+        out[k * RELAY + 8 : k * RELAY + 16, :] = second
+        out[k * RELAY + 16 : k * RELAY + 24, :] = rows
 
 
 def prefetch_kernel(
@@ -589,7 +587,7 @@
     row = dev[0] // N_COL
 
     def row_of(dr, k):
-        return sums[pl.ds((row + 2 * N_ROW + dr) % N_ROW * 4 + k, 1), :]
+        return sums[pl.ds((row + 2 * N_ROW + dr) % N_ROW * RELAY + 20 + k, 1), :]
 
     neutral = neutral_charges(pack, fragment_means(row_of, pltpu.roll))
     neutral_out[...] = neutral
@@ -628,9 +626,18 @@
         out[c, CY:] = im
 
 
-def gain_kernel(dev, own, mirror, edge, out):
+def gain_kernel(dev, own, mirror, sums, out):
+    after = pl.multiple_of((dev[0] // N_COL + 1) % N_ROW * RELAY, 8)
+    sent = sums[pl.ds(after, RELAY), :]
+    edge = jnp.concatenate(
+        [
+            jnp.concatenate([sent[0:8], sent[16:17]], axis=0),
+            jnp.concatenate([sent[8:16], sent[17:18]], axis=0),
+        ],
+        axis=1,
+    )
     flat = own[...].reshape(128, N)
-    pieces = gain_table(dev[0], flat, mirror[...].reshape(64, N), edge[...], pltpu.roll)
+    pieces = gain_table(dev[0], flat, mirror[8:16].reshape(64, N), edge, pltpu.roll)
     for k1, piece in enumerate(pieces):
         out[k1 * 8 : (k1 + 1) * 8, :LANES] = piece
         out[k1 * 8 : (k1 + 1) * 8, LANES:] = piece
@@ -691,19 +698,18 @@
     dev = lax.axis_index(ALL).astype(jnp.int32).reshape(1)
     charges = charges.reshape(1, ATOMS)
     sid = structure_id.reshape(1, ATOMS)
-    sums, mirror, edge = call(
+    sums, edge = call(
         partial_kernel,
-        [("v", (N_COL, LANES), f32), ("v", (8, 8, N), f32), ("v", (NK, N), f32)],
+        [("v", (N_COL, LANES), f32), ("v", (NK, N), f32)],
         "sshhh",
         (dev, live_count, sid, charges, influence),
-        [pltpu.VMEM((1, ATOMS), jnp.int32), pltpu.VMEM((1, ATOMS), f32), sems(4)],
-    )
-    edge = lax.ppermute(edge, ROW, [((i + 1) % N_ROW, i) for i in range(N_ROW)])
+        [pltpu.VMEM((1, ATOMS), jnp.int32), pltpu.VMEM((1, ATOMS), f32), sems(3)],
+    )
     sums = swap(sums.reshape(N_COL, 1, LANES), COL).reshape(N_COL, LANES)
-    sums = call(relay_kernel, [("v", (4 * N_ROW, LANES), f32)], "sv", (dev, sums))
-    sums, mirror = lax.optimization_barrier((sums, mirror))
+    sums = call(relay_kernel, [("v", (RELAY * N_ROW, LANES), f32)], "svv", (dev, sums, edge))
+    sums, mirror = lax.optimization_barrier((sums, influence))
     mirror = lax.ppermute(mirror, ALL, [(i, DEV - 1 - i) for i in range(DEV)])
-    sums = swap(sums.reshape(N_ROW, 4, LANES), ROW).reshape(4 * N_ROW, LANES)
+    sums = swap(sums.reshape(N_ROW, RELAY, LANES), ROW).reshape(RELAY * N_ROW, LANES)
     twiddle, mix = x_tables()
     sources = (cells, fraction, sid, charges, influence, z_table(), y_table(), twiddle)
     half = ((N, ATOMS), bf16)
@@ -720,8 +726,8 @@
             pltpu.VMEM((ATOM_ROWS, ATOMS), f32), pltpu.VMEM(*half), pltpu.VMEM(*half), sems(11),
         ],
     )
-    gain = call(gain_kernel, [("v", (N, 2 * LANES), f32)], "svvv", (dev, own, mirror, edge))
-    zh, gain = lax.optimization_barrier((zh, gain))
+    gain = call(gain_kernel, [("v", (N, 2 * LANES), f32)], "svvv", (dev, own, mirror, sums))
+    sums, gain = lax.optimization_barrier((sums, gain))
     messages, neutral = call(
         spread_kernel,
         [("v", (N_COL, ROWS, LANES), f32), ("v", (1, ATOMS), f32)],

time: 122 us -> 126 us (1.033)
  waiting for transfers between devices: 1.11 us -> 6.1 us
  starting transfers between devices: 21.5 us -> 19.6 us
    ppermute x1, waiting for transfers between devices: 0.01 us -> 6.1 us  [body(): mirror = lax.ppermute(mirror, ALL, [(i, DEV - 1 - i) for i in range(DEV)])]
    ppermute x1 -> x0, starting transfers between devices: 1.92 us -> none  [body(): edge = lax.ppermute(edge, ROW, [((i + 1) % N_ROW, i) for i in range(N_ROW)])]
  transfers between devices with their start and end apart: 3 -> 2, of which waited for: 1 -> 1; matrix products, arithmetic and copies ran while one was open for 0% -> 0% of each run, Pallas kernels for 3% -> 2%
where the time goes in v6:
time: 126 us
  blocking collectives  85.7 us (68%)
  starting transfers between devices  19.6 us (16%)
  Pallas kernels  12.5 us (10%)
  waiting for transfers between devices  6.1 us (5%)
  between operations  1.38 us (1%)
    all_to_all x5, blocking collectives, swap(): return lax.all_to_all(x, axis, split_axis=0, concat_axis=0, tiled=True)  85.7 us
    pallas_call x9, Pallas kernels, call(): pl.pallas_call(kernel, out_shape=[pltpu.HBM(shape, dtype) if k == 'h' els...  12.5 us
    all_to_all x1, starting transfers between devices, swap(): return lax.all_to_all(x, axis, split_axis=0, concat_axis=0, tiled=True)  12 us
    ppermute x1, starting transfers between devices, body(): mirror = lax.ppermute(mirror, ALL, [(i, DEV - 1 - i) for i in range(DEV)])  7.64 us
    ppermute x1, waiting for transfers between devices, body(): mirror = lax.ppermute(mirror, ALL, [(i, DEV - 1 - i) for i in range(DEV)])  6.1 us
  transfers between devices with their start and end apart: 2, of which 1 were waited for; matrix products, arithmetic and copies ran while one was open for 0% of the time, Pallas kernels for 2%

profile of v6, /device:TPU:1, one launch (start us, length us, event | category | flops | bytes accessed | tf_op | source)
XLA Modules:
  0.0 125.9 jit_solution(16626922782004310727)
XLA Ops:
  1.3 0.9 shard_map.113
  2.2 16.3 %all_to_all.30 = f32[16,1,128]{2,1,0:T(1,128)S(1)} all-to-all(f32[16,1,128]{2,1,0:T(1,128)S(1)} %bitcast.13), channel_id=1, replica_groups=mesh['row_0'=4,'row_1'=8,'col_0'=8,'col_1'=2] {'col_0','col_1'}, dimensions={0} | all-to-all | bytes 16384 | tf_op jit(solution)/shard_map/all_to_all | solution.py:694
  18.5 0.8 shard_map.114
  19.3 12.0 %all-to-all-start.1 = ((f32[32,24,128]{2,1,0:T(8,128)}), f32[32,24,128]{2,1,0:T(8,128)S(1)}, u32[]{:S(2)}, u32[]{:S(2)}) async-start(f32[32,24,128]{2,1,0:T(8,128)} %bitcast.6), calls=%async_computation.1 | async-start | bytes 786432 | tf_op jit(solution)/shard_map/all_to_all | solution.py:694
  31.3 7.6 %collective-permute-start = (f32[16,8,256]{2,1,0:T(8,128)}, f32[16,8,256]{2,1,0:T(8,128)S(1)}, u32[]{:S(2)}, u32[]{:S(2)}) collective-permute-start(f32[16,8,256]{2,1,0:T(8,128)} %own_hbm.1), channel_id=1, source_target_pairs={{0,511},{1,510},{2,509},{3,508},{4,507},{5,506},{6,505},{7,504},{8... | collective-permute-start | bytes 393224 | tf_op jit(solution)/shard_map/ppermute | solution.py:711
  39.0 2.7 %shard_map.115 = (f32[16,8,256]{2,1,0:T(8,128)S(1)}, bf16[2,256,384]{2,1,0:T(8,128)(2,1)S(1)}, bf16[1024,512]{1,0:T(8,128)(2,1)S(1)}, f32[32,2,128]{2,1,0:T(2,12...) custom-call(s32[1]{0:T(128)} %bitcast.dev, ...), custom_call_target="tpu_custom_call" | custom-call | tf_op jit(solution)/shard_map/pallas_call | solution.py:675
  41.7 0.0 copy-start.4
  41.7 0.6 copy-done.4
  42.3 6.1 %collective-permute-done.mirror = f32[16,8,256]{2,1,0:T(8,128)S(1)} collective-permute-done((f32[16,8,256]{2,1,0:T(8,128)}, f32[16,8,256]{2,1,0:T(8,128)S(1)}, u32[]{:S(2)}, u32[]{:S(2)}) %collective-permute-start) | collective-permute-done | bytes 131104 | tf_op jit(solution)/shard_map/ppermute | solution.py:711
  48.4 0.0 all-to-all-done.1
  48.4 0.9 shard_map.116.gain
  49.3 2.4 %shard_map.117 = (f32[16,32,128]{2,1,0:T(8,128)S(1)}, f32[1,1024]{1,0:T(1,128)S(1)}) custom-call(s32[1]{0:T(128)} %bitcast.dev, f32[768,128]{1,0:T(8,128)S(1)} %bitcast.11, f32[96,1024]{1,0:T(8,128)S(1)} %get-tuple-element.28.pack, bf16[256,1024]{1,0:T(8,128)(2,1)S(1)} %get-tuple-element.29.z_high.zh, bf16[256,1024]{1,0:T(8,128)(2,1)S(1)} %get-tuple-element.30.z_low.zl, ...), custom_call_target="tpu_custom_call" | custom-call | tf_op jit(solution)/shard_map/pallas_call | solution.py:675
  51.7 16.0 %all_to_all.31.x = f32[16,32,128]{2,1,0:T(8,128)S(1)} all-to-all(f32[16,32,128]{2,1,0:T(8,128)S(1)} %get-tuple-element.32), channel_id=1, replica_groups=mesh['row_0'=4,'row_1'=8,'col_0'=8,'col_1'=2] {'col_0','col_1'}, dimensions={0} | all-to-all | bytes 524288 | tf_op jit(solution)/shard_map/all_to_all | solution.py:694
  67.7 0.7 shard_map.118
  68.5 0.0 copy-start.3
  68.5 0.0 copy-start.5
  68.5 20.1 %all_to_all.32.x = f32[32,8,256]{2,1,0:T(8,128)S(1)} all-to-all(f32[32,8,256]{2,1,0:T(8,128)S(1)} %shard_map.118), channel_id=1, replica_groups=mesh['row_0'=4,'row_1'=8,'col_0'=8,'col_1'=2] {'row_0','row_1'}, dimensions={0} | all-to-all | bytes 524288 | tf_op jit(solution)/shard_map/all_to_all | solution.py:694
  88.6 0.0 copy-done.3
  88.6 0.0 copy-done.5
  88.6 0.7 shard_map.119
  89.4 15.1 %all_to_all.33.x = f32[32,8,256]{2,1,0:T(8,128)S(1)} all-to-all(f32[32,8,256]{2,1,0:T(8,128)S(1)} %shard_map.119), channel_id=1, replica_groups=mesh['row_0'=4,'row_1'=8,'col_0'=8,'col_1'=2] {'row_0','row_1'}, dimensions={0} | all-to-all | bytes 524288 | tf_op jit(solution)/shard_map/all_to_all | solution.py:694
  104.4 0.0 copy-start.1
  104.4 0.0 copy-start.2
  104.4 0.7 shard_map.120
  105.2 0.0 copy-start
  105.2 18.1 %all_to_all.34.message = f32[16,32,128]{2,1,0:T(8,128)S(1)} all-to-all(f32[16,32,128]{2,1,0:T(8,128)S(1)} %shard_map.120), channel_id=1, replica_groups=mesh['row_0'=4,'row_1'=8,'col_0'=8,'col_1'=2] {'col_0','col_1'}, dimensions={0} | all-to-all | bytes 524288 | tf_op jit(solution)/shard_map/all_to_all | solution.py:694
  123.3 0.0 copy-done.1
  123.3 0.0 copy-done.2
  123.3 0.0 copy-done
  123.3 2.6 %shard_map.121 = (f32[3,1024]{1,0:T(4,128)}, f32[1,1024]{1,0:T(1,128)}) custom-call(f32[16,32,128]{2,1,0:T(8,128)S(1)} %all_to_all.34.message, f32[1,1024]{1,0:T(1,128)S(1)} %get-tuple-element.36.neutral, f32[112,1024]{1,0:T(8,128)S(1)} %copy-done.2, bf16[256,1024]{1,0:T(8,128)(2,1)S(1)} %get-tuple-element.29.z_high.zh, ...), custom_call_target="tpu_custom_call" | custom-call | tf_op jit(solution)/shard_map/pallas_call | solution.py:675
Async XLA Ops:
  19.3 29.1 %all-to-all-start.1 = ((f32[32,24,128]{2,1,0:T(8,128)}), f32[32,24,128]{2,1,0:T(8,128)S(1)}, u32[]{:S(2)}, u32[]{:S(2)}) async-start(f32[32,24,128]{2,1,0:T(8,128)} %bitcast.6), calls=%async_computation.1 | async-start | bytes 786432 | tf_op jit(solution)/shard_map/all_to_all | solution.py:694
  31.3 17.1 %collective-permute-start = (f32[16,8,256]{2,1,0:T(8,128)}, f32[16,8,256]{2,1,0:T(8,128)S(1)}, u32[]{:S(2)}, u32[]{:S(2)}) collective-permute-start(f32[16,8,256]{2,1,0:T(8,128)} %own_hbm.1), channel_id=1, source_target_pairs={{0,511},{1,510},{2,509},{3,508},{4,507},{5,506},{6,505},{7,504},{8... | collective-permute-start | bytes 393224 | tf_op jit(solution)/shard_map/ppermute | solution.py:711
  41.7 0.6 copy-start.4
  68.5 20.2 %copy-start.3 = (bf16[2,256,256]{2,1,0:T(8,128)(2,1)S(1)}, bf16[2,256,256]{2,1,0:T(8,128)(2,1)}, u32[]{:S(2)}) copy-start(bf16[2,256,256]{2,1,0:T(8,128)(2,1)} %constant.34.clone.mix) | copy-start | bytes 786436
  68.5 20.2 %copy-start.5 = (f32[32,2,128]{2,1,0:T(2,128)S(1)}, f32[32,2,128]{2,1,0:T(2,128)}, u32[]{:S(2)}) copy-start(f32[32,2,128]{2,1,0:T(2,128)} %copy-done.4) | copy-start | bytes 98308
  104.4 18.8 %copy-start.1 = (bf16[256,1024]{1,0:T(8,128)(2,1)S(1)}, bf16[256,1024]{1,0:T(8,128)(2,1)}, u32[]{:S(2)}) copy-start(bf16[256,1024]{1,0:T(8,128)(2,1)} %get-tuple-element.39.vl) | copy-start | bytes 1572868
  104.4 18.8 %copy-start.2 = (f32[112,1024]{1,0:T(8,128)S(1)}, f32[112,1024]{1,0:T(8,128)}, u32[]{:S(2)}) copy-start(f32[112,1024]{1,0:T(8,128)} %get-tuple-element.37.pack) | copy-start | bytes 1376260
  105.2 18.1 %copy-start = (bf16[256,1024]{1,0:T(8,128)(2,1)S(1)}, bf16[256,1024]{1,0:T(8,128)(2,1)}, u32[]{:S(2)}) copy-start(bf16[256,1024]{1,0:T(8,128)(2,1)} %get-tuple-element.38.vh) | copy-start | bytes 1572868
